TPU v7x, 32 devices: a whole 2x2x4 slice. The times are simulated.
32 devices in a mesh: spec: 8 (over z, y), wave: 4 (over x, core).
Axes of the slice: x: 2, y: 2, z: 4, core: 2. Of those that a mesh axis runs over, the one named last changes fastest.
Arguments:
- observed_flux: bfloat16 [2048, 2048], P('spec', 'wave'), may hold values from -6 to 6
- continuum_coeffs: bfloat16 [2048, 16], P('spec'), may hold values from -6 to 6
- continuum_basis: bfloat16 [16, 2048], P(None, 'wave'), may hold values from -1.5 to 1.5
- centres: int32 [2048, 16], P('spec', 'wave'), may hold values from 0 to 2047, as said below
- line_index: int32 [2048, 16], P('spec', 'wave'), may hold values from 0 to 31
- column_factor: float32 [2048, 16], P('spec', 'wave'), may hold values from 0.3 to 3
- wing_width: int32 [2048], P('spec'), may hold values from 8 to 32, as said below
- line_strength: float32 [32], replicated, may hold values from 0.2 to 2
- line_widths: float32 [32], replicated, may hold values from 1 to 6
- sketch_matrix: bfloat16 [2048, 512], P('wave'), may hold values from -0.125 to 0.125
Outputs:
- residual: bfloat16 [2048, 2048], P('spec', 'wave')
- rfactor: float32 [512, 512], replicated
Inputs may be any that keep to these rules, and one draw needn't show every extreme that they name: The absorbers in columns k * 4 to (k + 1) * 4 - 1 have centres in pixels k * 512 to (k + 1) * 512 - 1; spectrum 0 has absorbers at pixel 0 and at pixel 2048 - 1. `wing_width`: spectrum 0 has the largest half-width.
All inputs are finite; a program needn't handle non-finite values.
Results may differ from a plain program's by a relative error of at most 0.0026.
Values sent between devices are 32-bit elements; how exact they have to be, the bound alone decides.
No kernel may reach another device: no remote copies, remote signals or barrier semaphores. Data moves between devices by JAX's collectives and lax.ppermute only.
A program may use at most 64 MiB of HBM per device.

v0:
```python
import jax
import jax.numpy as jnp
from jax import lax
from jax.sharding import PartitionSpec as P

WING = 32


voigt_mix = 0.5
log_two = 0.6931471805599453


def extended_2(block, sides, width):
    for axis, dim in sides:
        count = lax.axis_size(axis)
        forward = [(i, i + 1) for i in range(count - 1)]
        backward = [(target, source) for source, target in forward]
        low = lax.ppermute(
            lax.slice_in_dim(block, block.shape[dim] - width, None, axis=dim), axis, forward
        )
        high = lax.ppermute(lax.slice_in_dim(block, 0, width, axis=dim), axis, backward)
        block = jnp.concatenate([low, block, high], axis=dim)
    return block


def profile(offset, amplitude, inverse_width, wing_limit):
    scaled = offset * inverse_width
    values = amplitude * (
        voigt_mix / (1.0 + scaled * scaled)
        + (1.0 - voigt_mix) * jnp.exp(-log_two * scaled * scaled)
    )
    return jnp.where(jnp.abs(offset) <= wing_limit, values, 0.0)


def windowed_depth(centre_int, amplitude, inverse_width, wing_limit, anchor, width):
    pixels = anchor + jnp.arange(width, dtype=jnp.int32)
    offset_int = pixels[None, None, :] - centre_int[:, :, None]
    offset_float = offset_int.astype(jnp.float32)
    values = profile(
        offset_float, amplitude[:, :, None], inverse_width[:, :, None], wing_limit[:, :, None]
    )
    return jnp.sum(values, axis=1)


def shards(
    observed_flux,
    continuum_coeffs,
    continuum_basis,
    centres,
    line_index,
    column_factor,
    wing_width,
    line_strength,
    line_widths,
    sketch_matrix,
):
    spectra, pix_local = observed_flux.shape
    first_pixel = lax.axis_index("wave") * pix_local
    onehot = (
        line_index[:, :, None] == jnp.arange(line_strength.shape[0], dtype=jnp.int32)[None, None, :]
    ).astype(jnp.float32)
    amplitude = column_factor * jnp.sum(onehot * line_strength, axis=2)
    inverse_width = 1.0 / jnp.sum(onehot * line_widths, axis=2)
    wing_limit = wing_width.astype(jnp.float32)[:, None]
    extended = windowed_depth(
        centres, amplitude, inverse_width, wing_limit, first_pixel - WING, pix_local + 2 * WING
    )
    outgoing = jnp.concatenate([extended[:, :WING], extended[:, -WING:]], axis=1)
    padded_rims = extended_2(outgoing, (("wave", 1),), WING)
    optical_depth = extended[:, WING:-WING]
    optical_depth = optical_depth.at[:, :WING].add(padded_rims[:, :WING])
    optical_depth = optical_depth.at[:, -WING:].add(padded_rims[:, 3 * WING :])
    continuum = jnp.dot(continuum_coeffs, continuum_basis, preferred_element_type=jnp.float32)
    residual = (observed_flux.astype(jnp.float32) - continuum * jnp.exp(-optical_depth)).astype(
        jnp.bfloat16
    )
    spectra_total = spectra * lax.axis_size("spec")
    partial_sketch = jnp.dot(residual, sketch_matrix, preferred_element_type=jnp.float32)
    sketch = lax.psum(partial_sketch, "wave")
    local_gram = jnp.dot(
        sketch.T, sketch, precision=lax.Precision.HIGHEST, preferred_element_type=jnp.float32
    )
    gram_matrix = lax.psum(local_gram, "spec")
    gram_matrix = gram_matrix / spectra_total
    rfactor = jnp.linalg.cholesky(gram_matrix).T
    return (residual, rfactor)


def solution(mesh):
    return jax.shard_map(
        shards,
        mesh=mesh,
        in_specs=(
            P("spec", "wave"),
            P("spec", None),
            P(None, "wave"),
            P("spec", "wave"),
            P("spec", "wave"),
            P("spec", "wave"),
            P("spec"),
            P(),
            P(),
            P("wave", None),
        ),
        out_specs=(P("spec", "wave"), P()),
        check_vma=False,
    )
```

profile of v0, /device:TPU:0, one launch (start us, length us, event | category | flops | bytes accessed | tf_op | source)
XLA Modules:
  0.0 237.7 jit_solution(6965424051535711169)
XLA Ops:
  7.2 0.0 all-reduce.4.cloned.1.call-start
  7.2 0.7 convert_element_type.15
  8.0 0.8 select_reduce_fusion.1
  8.8 0.7 mul.59
  9.5 2.2 fusion.5
  11.7 0.1 copy.28
  11.8 2.4 collective-permute-start
  14.2 0.1 copy.29
  14.3 1.3 collective-permute-start.1
  15.7 0.2 copy.26
  15.9 0.1 copy.27
  16.0 0.6 compare_reduce_fusion.4
  16.6 0.7 add_select_fusion
  17.3 1.1 scatter-add.6
  18.4 1.3 collective-permute-done.1
  19.6 0.1 slice_add_fusion
  19.7 0.9 scatter-add.9
  20.7 0.2 subtract_convert_fusion
  20.9 1.1 fusion.19
  22.0 0.0 all-reduce.4.cloned.1.call-update
  22.1 0.2 all-reduce.6.cloned.1.call-start
  22.3 36.6 %all-reduce.4.cloned.1.call-done = f32[256,512]{1,0:T(8,128)} async-done(((f32[256,512]{1,0:T(8,128)}), f32[256,512]{1,0:T(8,128)}) %all-reduce.4.cloned.1.call-update) | async-done | bytes 524304 | tf_op jit(solution)/shard_map/psum | solution.py:79
  58.9 3.2 %fusion.20 = f32[512,512]{0,1:T(8,128)} fusion(f32[256,512]{1,0:T(8,128)} %all-reduce.4.cloned.1.call-done), kind=kOutput, calls=%fused_computation.57 | convolution fusion | flops 805306368 | bytes 1572864 | tf_op jit(solution)/shard_map/dot_general | solution.py:80
  62.2 0.0 all-reduce.6.cloned.1.call-update
  62.2 78.9 %all-reduce.6.cloned.1.call-done = f32[512,512]{0,1:T(8,128)} async-done(((f32[512,512]{0,1:T(8,128)}), f32[512,512]{0,1:T(8,128)}) %all-reduce.6.cloned.1.call-update) | async-done | bytes 1048592 | tf_op jit(solution)/shard_map/psum | solution.py:83
  141.0 2.3 broadcast_multiply_fusion
  143.3 1.6 copy.23
  145.0 0.2 fusion.6
  145.3 1.0 copy-done.2
  146.2 11.7 %cholesky.104 = f32[128,128]{1,0:T(8,128)S(1)} custom-call(f32[128,128]{1,0:T(8,128)S(1)} %cholesky.266), custom_call_target="Cholesky" | custom-call | tf_op jit(solution)/shard_map/jit(cholesky)/cholesky | solution.py:85
  158.0 9.8 %custom-call.27 = f32[1,128,128]{1,2,0:T(8,128)S(1)} custom-call(f32[1,128,128]{2,1,0:T(8,128)S(1)} %get-tuple-element.44), custom_call_target="InvertDiagBlocksLowerTriangular" | custom-call | tf_op jit(solution)/shard_map/jit(cholesky)/cholesky | solution.py:85
  167.8 0.1 cholesky.224
  167.9 0.3 constant_dynamic-update-slice_fusion.2
  168.3 0.3 convolution_subtract_fusion
  168.6 11.8 %cholesky.217 = f32[128,128]{1,0:T(8,128)S(1)} custom-call(f32[128,128]{1,0:T(8,128)S(1)} %cholesky.270), custom_call_target="Cholesky" | custom-call | tf_op jit(solution)/shard_map/jit(cholesky)/cholesky | solution.py:85
  180.5 9.8 %custom-call.28 = f32[1,128,128]{1,2,0:T(8,128)S(1)} custom-call(f32[1,128,128]{2,1,0:T(8,128)S(1)} %get-tuple-element.41), custom_call_target="InvertDiagBlocksLowerTriangular" | custom-call | tf_op jit(solution)/shard_map/jit(cholesky)/cholesky | solution.py:85
  190.3 0.3 convolution_dynamic-update-slice_fusion
  190.6 0.4 convolution_subtract_fusion.1
  191.0 11.7 %cholesky.238 = f32[128,128]{1,0:T(8,128)S(1)} custom-call(f32[128,128]{1,0:T(8,128)S(1)} %cholesky.275), custom_call_target="Cholesky" | custom-call | tf_op jit(solution)/shard_map/jit(cholesky)/cholesky | solution.py:85
  202.7 0.7 compare_reduce_fusion.1
  203.4 9.8 %custom-call.29 = f32[1,128,128]{1,2,0:T(8,128)S(1)} custom-call(f32[1,128,128]{2,1,0:T(8,128)S(1)} %get-tuple-element.38), custom_call_target="InvertDiagBlocksLowerTriangular" | custom-call | tf_op jit(solution)/shard_map/jit(cholesky)/cholesky | solution.py:85
  213.3 0.2 convolution_dynamic-update-slice_fusion.1
  213.5 0.4 convolution_subtract_fusion.2
  213.9 11.7 %cholesky.255 = f32[128,128]{1,0:T(8,128)S(1)} custom-call(f32[128,128]{1,0:T(8,128)S(1)} %convolution_subtract_fusion.2), custom_call_target="Cholesky" | custom-call | tf_op jit(solution)/shard_map/jit(cholesky)/cholesky | solution.py:85
  225.6 0.6 compare_reduce_fusion
  226.2 0.7 compare_reduce_fusion.2
  229.4 0.1 select_bitcast_fusion
  229.6 1.3 copy.24
  (27 shorter events, 0.3 us)
Async XLA Ops:
  7.2 13.8 %copy-start = (bf16[512,512]{1,0:T(8,128)(2,1)S(1)}, bf16[512,512]{1,0:T(8,128)(2,1)}, u32[]{:S(2)}) copy-start(bf16[512,512]{1,0:T(8,128)(2,1)} %param.23) | copy-start | bytes 1572868
  7.2 51.8 %all-reduce.4.cloned.1.call-start = ((), (), s32[]{:S(2)}) async-start(), calls=%async_computation | async-start | bytes 1048576 | tf_op jit(solution)/shard_map/psum | solution.py:79
  11.8 4.8 %collective-permute-start = (f32[256,32]{1,0:T(8,128)S(1)}, f32[256,32]{1,0:T(8,128)S(1)}, u32[]{:S(2)}, u32[]{:S(2)}) collective-permute-start(f32[256,32]{1,0:T(8,128)S(1)} %copy.28), channel_id=1, source_target_pairs={{0,1},{1,2},{2,3},{4,5},{5,6},{6,7},{8,9},{9,10},{10,11},{12,13},{... | collective-permute-start | bytes 98312 | tf_op jit(solution)/shard_map/ppermute | solution.py:18
  14.3 5.3 %collective-permute-start.1 = (f32[256,32]{1,0:T(8,128)S(1)}, f32[256,32]{1,0:T(8,128)S(1)}, u32[]{:S(2)}, u32[]{:S(2)}) collective-permute-start(f32[256,32]{1,0:T(8,128)S(1)} %copy.29), channel_id=1, source_target_pairs={{1,0},{2,1},{3,2},{5,4},{6,5},{7,6},{9,8},{10,9},{11,10},{13,12},{... | collective-permute-start | bytes 98312 | tf_op jit(solution)/shard_map/ppermute | solution.py:21
  15.6 5.0 %copy-start.5 = (bf16[256,512]{1,0:T(8,128)(2,1)S(1)}, bf16[256,512]{1,0:T(8,128)(2,1)}, u32[]{:S(2)}) copy-start(bf16[256,512]{1,0:T(8,128)(2,1)} %param.14) | copy-start | bytes 786436
  15.7 5.0 %copy-start.6 = (bf16[16,512]{1,0:T(8,128)(2,1)S(1)}, bf16[16,512]{1,0:T(8,128)(2,1)}, u32[]{:S(2)}) copy-start(bf16[16,512]{1,0:T(8,128)(2,1)} %param.16) | copy-start | bytes 49156
  15.7 5.0 %copy-start.7 = (bf16[256,16]{0,1:T(8,128)(2,1)S(1)}, bf16[256,16]{0,1:T(8,128)(2,1)}, u32[]{:S(2)}) copy-start(bf16[256,16]{0,1:T(8,128)(2,1)} %param.15) | copy-start | bytes 24580
  20.9 41.2 %copy-start.4 = (bf16[256,512]{1,0:T(8,128)(2,1)}, bf16[256,512]{1,0:T(8,128)(2,1)S(1)}, u32[]{:S(2)}) copy-start(bf16[256,512]{1,0:T(8,128)(2,1)S(1)} %subtract_convert_fusion) | copy-start | bytes 786436
  22.1 119.0 %all-reduce.6.cloned.1.call-start = ((), (), s32[]{:S(2)}) async-start(), calls=%async_computation.1 | async-start | bytes 2097152 | tf_op jit(solution)/shard_map/psum | solution.py:83
  143.3 1.7 copy-start.1
  145.2 1.0 copy-start.2
  146.2 21.7 %copy-start.3 = (f32[512,512]{1,0:T(8,128)S(1)}, f32[512,512]{1,0:T(8,128)}, u32[]{:S(2)}) copy-start(f32[512,512]{1,0:T(8,128)} %copy-done.2) | copy-start | bytes 3145732
Sparse Core Ops, SparseCore 0:
  22.2 36.7 all-reduce.3
  63.0 77.9 all-reduce.5
where the time goes:
time: 238 us
  waiting for transfers between devices  117 us (49%)
  other arithmetic  87.1 us (37%)
  between operations  16.9 us (7%)
  local copies, waits for them, and re-layouts  6.6 us (3%)
  matrix products  6.44 us (3%)
  starting transfers between devices  3.91 us (2%)
    psum x1, waiting for transfers between devices, shards(): gram_matrix = lax.psum(local_gram, 'spec')  78.9 us
    another operation x14, other arithmetic, shards(): rfactor = jnp.linalg.cholesky(gram_matrix).T  78.6 us
    psum x1, waiting for transfers between devices, shards(): sketch = lax.psum(partial_sketch, 'wave')  36.6 us
  transfers between devices with their start and end apart: 4, of which 3 were waited for; matrix products, arithmetic and copies ran while one was open for 1% of the time, Pallas kernels for 0%

commit v1 on v0

--- a/solution.py
+++ b/solution.py
@@ -1,9 +1,103 @@
 import jax
 import jax.numpy as jnp
 from jax import lax
+from jax.experimental import pallas as pl
+from jax.experimental.pallas import tpu as pltpu
 from jax.sharding import PartitionSpec as P
 
 WING = 32
+T = 128
+S = 8
+HI = lax.Precision.HIGHEST
+
+def rows_of(x, k):
+    return jnp.broadcast_to(x[k:k + 1, :], x.shape)
+
+def lanes_of(x, c):
+    return jnp.broadcast_to(x[:, c:c + 1], x.shape)
+
+def factor_block(d_ref, rk_ref, x_ref):
+    steps = T // S
+    sub = lax.broadcasted_iota(jnp.int32, (S, T), 0)
+    lane = lax.broadcasted_iota(jnp.int32, (S, T), 1)
+    at = [sub == k for k in range(S)]
+    D = [d_ref[S * g:S * g + S, 0:T] for g in range(steps)]
+    E = [jnp.where(lane == sub + S * g, 1.0, 0.0).astype(jnp.float32) for g in range(steps)]
+    C = [lanes_of(D[0], k) for k in range(S)]
+    for s in range(steps):
+        Z = [rows_of(D[s], k) for k in range(S)]
+        Y = [rows_of(E[s], k) for k in range(S)]
+        B = Cn = None
+        if s + 1 < steps:
+            B = [lanes_of(D[s + 1], S * s + k) for k in range(S)]
+            Cn = [lanes_of(D[s + 1], S * (s + 1) + k) for k in range(S)]
+        for k in range(S):
+            d = rows_of(C[k], k)
+            inv = 1.0 / d
+            rs = lax.rsqrt(d)
+            rk_ref[S * s + k:S * s + k + 1, :] = (Z[k] * rs)[0:1]
+            x_ref[S * s + k:S * s + k + 1, :] = (Y[k] * rs)[0:1]
+            Z[k] = Z[k] * inv
+            Y[k] = Y[k] * inv
+            u = {}
+            for c in range(k + 1, S):
+                u[c] = rows_of(C[c], k) * inv
+                C[c] = jnp.where(at[k], u[c], C[c] - C[k] * u[c])
+            for c in range(S):
+                if c != k:
+                    m = rows_of(C[k], c)
+                    Z[c] = Z[c] - m * Z[k]
+                    Y[c] = Y[c] - m * Y[k]
+            if B is not None:
+                bi = B[k] * inv
+                for c in range(k + 1, S):
+                    B[c] = B[c] - B[k] * u[c]
+                for c in range(S):
+                    Cn[c] = Cn[c] - bi * rows_of(B[k], c)
+        for g in range(s + 1, steps):
+            raw = [lanes_of(D[g], S * s + k) for k in range(S)]
+            dd, ee = D[g], E[g]
+            for k in range(S):
+                dd = dd - raw[k] * Z[k]
+                ee = ee - raw[k] * Y[k]
+            D[g], E[g] = dd, ee
+        C = Cn
+
+def chol_body(a_ref, r_ref, w_ref, rk_ref, x_ref):
+    n = a_ref.shape[0]
+    nb = n // T
+    w_ref[...] = a_ref[...]
+    r_ref[...] = jnp.zeros_like(r_ref)
+    row = lax.broadcasted_iota(jnp.int32, (T, T), 0)
+    col = lax.broadcasted_iota(jnp.int32, (T, T), 1)
+    def step(b, _):
+        factor_block(w_ref, rk_ref, x_ref)
+        base = pl.multiple_of(b * T, T)
+        r_ref[pl.ds(base, T), pl.ds(base, T)] = jnp.where(row <= col, rk_ref[...], 0.0)
+        @pl.when(b < nb - 1)
+        def _():
+            x = jnp.where(row >= col, x_ref[...], 0.0)
+            panel = jnp.dot(x, w_ref[0:T, T:n], precision=HI, preferred_element_type=jnp.float32)
+            for t in range(nb - 1):
+                @pl.when(b + 1 + t < nb)
+                def _():
+                    r_ref[pl.ds(base, T), pl.ds(pl.multiple_of(base + (t + 1) * T, T), T)] = panel[:, t * T:(t + 1) * T]
+            for i in range(nb - 1):
+                left = panel[:, i * T:(i + 1) * T]
+                right = panel[:, i * T:]
+                upd = lax.dot_general(left, right, (((0,), (0,)), ((), ())), precision=HI, preferred_element_type=jnp.float32)
+                w_ref[i * T:(i + 1) * T, i * T:n - T] = w_ref[(i + 1) * T:(i + 2) * T, (i + 1) * T:n] - upd
+        return 0
+    lax.fori_loop(0, nb, step, 0)
+
+def chol(a):
+    n = a.shape[0]
+    return pl.pallas_call(
+        chol_body, name="factor",
+        out_shape=jax.ShapeDtypeStruct((n, n), jnp.float32),
+        scratch_shapes=[pltpu.VMEM((n, n), jnp.float32), pltpu.VMEM((T, T), jnp.float32), pltpu.VMEM((T, T), jnp.float32)],
+        compiler_params=pltpu.CompilerParams(vmem_limit_bytes=32 << 20),
+    )(a)
 
 
 voigt_mix = 0.5
@@ -82,7 +176,7 @@
     )
     gram_matrix = lax.psum(local_gram, "spec")
     gram_matrix = gram_matrix / spectra_total
-    rfactor = jnp.linalg.cholesky(gram_matrix).T
+    rfactor = chol(gram_matrix)
     return (residual, rfactor)
 
 

time: 238 us -> 166 us (0.70)
  other arithmetic: 87.1 us -> 7.19 us
  Pallas kernels: 0 us -> 16.3 us
  local copies, waits for them, and re-layouts: 6.6 us -> 2.53 us
  between operations: 16.9 us -> 14.2 us
    another operation x16 -> x2, other arithmetic: 79.9 us -> 1.3 us  [the longest x14 78.6 us: shards(): rfactor = jnp.linalg.cholesky(gram_matrix).T]
    pallas_call x0 -> x1, Pallas kernels: none -> 16.3 us  [chol(): pl.pallas_call(chol_body, name='factor', out_shape=jax.ShapeDtypeStruct((...]
  transfers between devices with their start and end apart: 4 -> 4, of which waited for: 3 -> 3; matrix products, arithmetic and copies ran while one was open for 1% -> 2% of each run, Pallas kernels for 0% -> 0%
where the time goes in v1:
time: 166 us; the launch traced here: 165 us
  waiting for transfers between devices  117 us (70%)
  Pallas kernels  16.3 us (10%)
  between operations  14.2 us (9%)
  other arithmetic  7.19 us (4%)
  matrix products  4.54 us (3%)
  starting transfers between devices  3.73 us (2%)
  local copies, waits for them, and re-layouts  2.53 us (2%)
    psum x1, waiting for transfers between devices, shards(): gram_matrix = lax.psum(local_gram, 'spec')  78.9 us
    psum x1, waiting for transfers between devices, shards(): sketch = lax.psum(partial_sketch, 'wave')  36.8 us
    pallas_call x1, Pallas kernels, chol(): pl.pallas_call(chol_body, name='factor', out_shape=jax.ShapeDtypeStruct((...  16.3 us
  transfers between devices with their start and end apart: 4, of which 3 were waited for; matrix products, arithmetic and copies ran while one was open for 2% of the time, Pallas kernels for 0%

profile of v1, /device:TPU:0, one launch (start us, length us, event | category | flops | bytes accessed | tf_op | source)
XLA Modules:
  0.0 165.5 jit_solution(15269777394834960707)
XLA Ops:
  7.2 0.0 copy-start
  7.2 0.0 all-reduce.3.cloned.1.call-start
  7.2 0.7 convert_element_type.15
  8.0 0.8 select_reduce_fusion.1
  8.8 0.7 mul.59
  9.5 2.2 %fusion.5 = f32[256,576]{0,1:T(8,128)S(1)} fusion(f32[256,4]{0,1:T(4,128)S(1)} %broadcast_divide_fusion, f32[256,4]{0,1:T(4,128)S(1)} %mul.59, f32[256]{0:T(256)S(1)} %convert_element_type.15, s32[256,4]{0,1:T(4,128)} %param.17, s32[576]{0:T(1024)S(1)} %iota_add_fusion), kind=kLoop, calls=%fused_computation.6 | loop fusion | flops 8699904 | bytes 605440 | tf_op jit(solution)/shard_map/reduce_sum | solution.py:136
  11.7 0.1 copy.21
  11.8 2.4 %collective-permute-start = (f32[256,32]{1,0:T(8,128)S(1)}, f32[256,32]{1,0:T(8,128)S(1)}, u32[]{:S(2)}, u32[]{:S(2)}) collective-permute-start(f32[256,32]{1,0:T(8,128)S(1)} %copy.21), channel_id=1, source_target_pairs={{0,1},{1,2},{2,3},{4,5},{5,6},{6,7},{8,9},{9,10},{10,11},{12,13},{... | collective-permute-start | bytes 98312 | tf_op jit(solution)/shard_map/ppermute | solution.py:112
  14.2 0.1 copy.22
  14.3 1.3 collective-permute-start.1
  15.6 0.0 copy-start.2
  15.7 0.0 copy-start.3
  15.7 0.0 copy-start.4
  15.7 0.2 copy.19
  15.9 0.1 copy.20
  16.0 0.6 compare_reduce_fusion
  16.6 0.0 collective-permute-done
  16.6 0.7 add_select_fusion
  17.3 1.1 scatter-add.6
  18.4 1.3 collective-permute-done.1
  19.6 0.1 slice_add_fusion
  19.7 0.9 scatter-add.9
  20.6 0.0 copy-done.2
  20.7 0.0 copy-done.3
  20.7 0.0 copy-done.4
  20.7 0.3 subtract_convert_fusion
  20.9 0.0 copy-done
  20.9 0.0 copy-start.1
  21.0 1.1 fusion.7
  22.0 0.0 all-reduce.3.cloned.1.call-update
  22.1 0.0 all-reduce.5.cloned.1.call-start
  22.1 36.8 %all-reduce.3.cloned.1.call-done = f32[256,512]{1,0:T(8,128)} async-done(((f32[256,512]{1,0:T(8,128)}), f32[256,512]{1,0:T(8,128)}) %all-reduce.3.cloned.1.call-update) | async-done | bytes 524304 | tf_op jit(solution)/shard_map/psum | solution.py:173
  58.9 3.2 %fusion.8 = f32[512,512]{1,0:T(8,128)} fusion(f32[256,512]{1,0:T(8,128)} %all-reduce.3.cloned.1.call-done), kind=kOutput, calls=%fused_computation.20 | convolution fusion | flops 805306368 | bytes 1572864 | tf_op jit(solution)/shard_map/dot_general | solution.py:174
  62.1 0.0 copy-done.1
  62.1 0.0 all-reduce.5.cloned.1.call-update
  62.2 78.9 %all-reduce.5.cloned.1.call-done = f32[512,512]{1,0:T(8,128)} async-done(((f32[512,512]{1,0:T(8,128)}), f32[512,512]{1,0:T(8,128)}) %all-reduce.5.cloned.1.call-update) | async-done | bytes 1048592 | tf_op jit(solution)/shard_map/psum | solution.py:177
  141.1 1.3 broadcast_multiply_fusion.a_ref
  142.4 16.3 %factor.1 = f32[512,512]{1,0:T(8,128)} custom-call(f32[512,512]{1,0:T(8,128)S(1)} %broadcast_multiply_fusion.a_ref), custom_call_target="tpu_custom_call" | custom-call | tf_op jit(solution)/shard_map/factor/pallas_call | solution.py:95
  (4 shorter events, 0.1 us)
Async XLA Ops:
  7.2 13.8 %copy-start = (bf16[512,512]{1,0:T(8,128)(2,1)S(1)}, bf16[512,512]{1,0:T(8,128)(2,1)}, u32[]{:S(2)}) copy-start(bf16[512,512]{1,0:T(8,128)(2,1)} %param.23) | copy-start | bytes 1572868
  7.2 51.8 %all-reduce.3.cloned.1.call-start = ((), (), s32[]{:S(2)}) async-start(), calls=%async_computation | async-start | bytes 1048576 | tf_op jit(solution)/shard_map/psum | solution.py:173
  11.8 4.8 %collective-permute-start = (f32[256,32]{1,0:T(8,128)S(1)}, f32[256,32]{1,0:T(8,128)S(1)}, u32[]{:S(2)}, u32[]{:S(2)}) collective-permute-start(f32[256,32]{1,0:T(8,128)S(1)} %copy.21), channel_id=1, source_target_pairs={{0,1},{1,2},{2,3},{4,5},{5,6},{6,7},{8,9},{9,10},{10,11},{12,13},{... | collective-permute-start | bytes 98312 | tf_op jit(solution)/shard_map/ppermute | solution.py:112
  14.3 5.3 %collective-permute-start.1 = (f32[256,32]{1,0:T(8,128)S(1)}, f32[256,32]{1,0:T(8,128)S(1)}, u32[]{:S(2)}, u32[]{:S(2)}) collective-permute-start(f32[256,32]{1,0:T(8,128)S(1)} %copy.22), channel_id=1, source_target_pairs={{1,0},{2,1},{3,2},{5,4},{6,5},{7,6},{9,8},{10,9},{11,10},{13,12},{... | collective-permute-start | bytes 98312 | tf_op jit(solution)/shard_map/ppermute | solution.py:115
  15.6 5.0 %copy-start.2 = (bf16[256,512]{1,0:T(8,128)(2,1)S(1)}, bf16[256,512]{1,0:T(8,128)(2,1)}, u32[]{:S(2)}) copy-start(bf16[256,512]{1,0:T(8,128)(2,1)} %param.14) | copy-start | bytes 786436
  15.7 5.0 %copy-start.3 = (bf16[16,512]{1,0:T(8,128)(2,1)S(1)}, bf16[16,512]{1,0:T(8,128)(2,1)}, u32[]{:S(2)}) copy-start(bf16[16,512]{1,0:T(8,128)(2,1)} %param.16) | copy-start | bytes 49156
  15.7 5.0 %copy-start.4 = (bf16[256,16]{0,1:T(8,128)(2,1)S(1)}, bf16[256,16]{0,1:T(8,128)(2,1)}, u32[]{:S(2)}) copy-start(bf16[256,16]{0,1:T(8,128)(2,1)} %param.15) | copy-start | bytes 24580
  20.9 41.2 %copy-start.1 = (bf16[256,512]{1,0:T(8,128)(2,1)}, bf16[256,512]{1,0:T(8,128)(2,1)S(1)}, u32[]{:S(2)}) copy-start(bf16[256,512]{1,0:T(8,128)(2,1)S(1)} %subtract_convert_fusion) | copy-start | bytes 786436
  22.1 119.0 %all-reduce.5.cloned.1.call-start = ((), (), s32[]{:S(2)}) async-start(), calls=%async_computation.1 | async-start | bytes 2097152 | tf_op jit(solution)/shard_map/psum | solution.py:177
Sparse Core Ops, SparseCore 0:
  22.2 36.7 all-reduce.2
  63.0 77.9 all-reduce.4

commit v2 on v1

--- a/solution.py
+++ b/solution.py
@@ -63,41 +63,136 @@
             D[g], E[g] = dd, ee
         C = Cn
 
-def chol_body(a_ref, r_ref, w_ref, rk_ref, x_ref):
-    n = a_ref.shape[0]
+def upper_block(b, nb):
+    i = jnp.int32(0)
+    start = jnp.int32(0)
+    for r in range(1, nb):
+        first = r * nb - r * (r - 1) // 2
+        i = i + (b >= first).astype(jnp.int32)
+        start = jnp.where(b >= first, first, start)
+    return i, i + b - start
+
+
+def blocks_of(x, slots, t, nb):
+    b = jnp.minimum(x * slots + t, nb * (nb + 1) // 2 - 1)
+    i, j = upper_block(b, nb)
+    return pl.multiple_of(i * T, T), pl.multiple_of(j * T, T)
+
+
+def gram_blocks(mine, other, slots, scale):
+    rows, k = mine.shape
+
+    def body(mine_ref, other_ref, keep_ref, send_ref, s_ref, g_ref):
+        w = lax.axis_index("wave")
+        core, x = w % 2, w // 2
+        s_ref[...] = mine_ref[...] + other_ref[...]
+        for t in range(slots):
+            i, j = blocks_of(x, slots, t, k // T)
+            g_ref[...] = scale * lax.dot_general(
+                s_ref[:, pl.ds(i, T)], s_ref[:, pl.ds(j, T)], (((0,), (0,)), ((), ())),
+                precision=HI, preferred_element_type=jnp.float32)
+            half = T // 2
+            keep_ref[t] = g_ref[pl.ds(pl.multiple_of(core * half, half), half), :]
+            send_ref[t] = g_ref[pl.ds(pl.multiple_of((1 - core) * half, half), half), :]
+
+    shape = jax.ShapeDtypeStruct((slots, T // 2, T), jnp.float32)
+    return pl.pallas_call(
+        body, name="gram", out_shape=(shape, shape),
+        scratch_shapes=[pltpu.VMEM((rows, k), jnp.float32), pltpu.VMEM((T, T), jnp.float32)],
+        compiler_params=pltpu.CompilerParams(vmem_limit_bytes=32 << 20),
+    )(mine, other)
+
+
+def factor(pieces, offsets, slots, n):
     nb = n // T
-    w_ref[...] = a_ref[...]
-    r_ref[...] = jnp.zeros_like(r_ref)
-    row = lax.broadcasted_iota(jnp.int32, (T, T), 0)
-    col = lax.broadcasted_iota(jnp.int32, (T, T), 1)
-    def step(b, _):
-        factor_block(w_ref, rk_ref, x_ref)
-        base = pl.multiple_of(b * T, T)
-        r_ref[pl.ds(base, T), pl.ds(base, T)] = jnp.where(row <= col, rk_ref[...], 0.0)
-        @pl.when(b < nb - 1)
-        def _():
-            x = jnp.where(row >= col, x_ref[...], 0.0)
-            panel = jnp.dot(x, w_ref[0:T, T:n], precision=HI, preferred_element_type=jnp.float32)
-            for t in range(nb - 1):
-                @pl.when(b + 1 + t < nb)
-                def _():
-                    r_ref[pl.ds(base, T), pl.ds(pl.multiple_of(base + (t + 1) * T, T), T)] = panel[:, t * T:(t + 1) * T]
-            for i in range(nb - 1):
-                left = panel[:, i * T:(i + 1) * T]
-                right = panel[:, i * T:]
-                upd = lax.dot_general(left, right, (((0,), (0,)), ((), ())), precision=HI, preferred_element_type=jnp.float32)
-                w_ref[i * T:(i + 1) * T, i * T:n - T] = w_ref[(i + 1) * T:(i + 2) * T, (i + 1) * T:n] - upd
-        return 0
-    lax.fori_loop(0, nb, step, 0)
-
-def chol(a):
-    n = a.shape[0]
+    part = T // 4
+
+    def body(*refs):
+        piece_refs, (r_ref, w_ref, rk_ref, x_ref) = refs[:len(pieces)], refs[len(pieces):]
+        w = lax.axis_index("wave")
+        y = lax.axis_index("spec") % 2
+        for ref, (dw, dy) in zip(piece_refs, offsets):
+            v = w ^ dw
+            core, x = v % 2, v // 2
+            row = pl.multiple_of(core * (T // 2) + (y ^ dy) * part, part)
+            for t in range(slots):
+                i, j = blocks_of(x, slots, t, nb)
+                w_ref[pl.ds(pl.multiple_of(i + row, part), part), pl.ds(j, T)] = ref[t]
+        r_ref[...] = jnp.zeros_like(r_ref)
+        row = lax.broadcasted_iota(jnp.int32, (T, T), 0)
+        col = lax.broadcasted_iota(jnp.int32, (T, T), 1)
+
+        def step(b, _):
+            factor_block(w_ref, rk_ref, x_ref)
+            base = pl.multiple_of(b * T, T)
+            r_ref[pl.ds(base, T), pl.ds(base, T)] = jnp.where(row <= col, rk_ref[...], 0.0)
+
+            @pl.when(b < nb - 1)
+            def _():
+                x = jnp.where(row >= col, x_ref[...], 0.0)
+                panel = jnp.dot(x, w_ref[0:T, T:n], precision=HI, preferred_element_type=jnp.float32)
+                for t in range(nb - 1):
+                    @pl.when(b + 1 + t < nb)
+                    def _():
+                        at = pl.multiple_of(base + (t + 1) * T, T)
+                        r_ref[pl.ds(base, T), pl.ds(at, T)] = panel[:, t * T:(t + 1) * T]
+                for i in range(nb - 1):
+                    update = lax.dot_general(
+                        panel[:, i * T:(i + 1) * T], panel[:, i * T:], (((0,), (0,)), ((), ())),
+                        precision=HI, preferred_element_type=jnp.float32)
+                    w_ref[i * T:(i + 1) * T, i * T:n - T] = w_ref[(i + 1) * T:(i + 2) * T, (i + 1) * T:n] - update
+            return 0
+
+        lax.fori_loop(0, nb, step, 0)
+
     return pl.pallas_call(
-        chol_body, name="factor",
-        out_shape=jax.ShapeDtypeStruct((n, n), jnp.float32),
-        scratch_shapes=[pltpu.VMEM((n, n), jnp.float32), pltpu.VMEM((T, T), jnp.float32), pltpu.VMEM((T, T), jnp.float32)],
+        body, name="factor", out_shape=jax.ShapeDtypeStruct((n, n), jnp.float32),
+        scratch_shapes=[pltpu.VMEM((n, n), jnp.float32), pltpu.VMEM((T, T), jnp.float32),
+                        pltpu.VMEM((T, T), jnp.float32)],
         compiler_params=pltpu.CompilerParams(vmem_limit_bytes=32 << 20),
-    )(a)
+    )(*pieces)
+
+
+def swap(x, axis, bit):
+    return lax.ppermute(x, axis, [(i, i ^ bit) for i in range(lax.axis_size(axis))])
+
+
+def bits_from(first, count):
+    bits = []
+    while first < count:
+        bits.append(first)
+        first *= 2
+    return bits
+
+
+def half_of(x, which, dim):
+    size = x.shape[dim] // 2
+    return lax.dynamic_slice_in_dim(x, which * size, size, dim)
+
+
+def reduce_and_factor(partial_sketch, spectra_total):
+    waves, specs = lax.axis_size("wave"), lax.axis_size("spec")
+    core, y = lax.axis_index("wave") % 2, lax.axis_index("spec") % 2
+    k = partial_sketch.shape[1]
+    slots = -(-((k // T) * (k // T + 1) // 2) // (waves // 2))
+    mine = half_of(partial_sketch, core, 0)
+    other = swap(half_of(partial_sketch, 1 - core, 0), "wave", 1)
+    for bit in bits_from(2, waves):
+        mine = mine + other
+        other = swap(mine, "wave", bit)
+    keep, send = gram_blocks(mine, other, slots, 1.0 / spectra_total)
+    got = swap(send, "wave", 1)
+    mine = half_of(keep, y, 1) + half_of(got, y, 1)
+    other = half_of(keep, 1 - y, 1) + half_of(got, 1 - y, 1)
+    mine = mine + swap(other, "spec", 1)
+    for bit in bits_from(2, specs):
+        mine = mine + swap(mine, "spec", bit)
+    pieces, offsets = [mine], [(0, 0)]
+    steps = [("spec", 1)] + [("wave", b) for b in bits_from(2, waves)] + [("wave", 1)]
+    for axis, bit in steps:
+        pieces = pieces + [swap(p, axis, bit) for p in pieces]
+        offsets = offsets + [(w ^ (bit if axis == "wave" else 0), y_ ^ (bit if axis == "spec" else 0)) for w, y_ in offsets]
+    return factor(pieces, offsets, slots, k)
 
 
 voigt_mix = 0.5
@@ -170,13 +265,7 @@
     )
     spectra_total = spectra * lax.axis_size("spec")
     partial_sketch = jnp.dot(residual, sketch_matrix, preferred_element_type=jnp.float32)
-    sketch = lax.psum(partial_sketch, "wave")
-    local_gram = jnp.dot(
-        sketch.T, sketch, precision=lax.Precision.HIGHEST, preferred_element_type=jnp.float32
-    )
-    gram_matrix = lax.psum(local_gram, "spec")
-    gram_matrix = gram_matrix / spectra_total
-    rfactor = chol(gram_matrix)
+    rfactor = reduce_and_factor(partial_sketch, spectra_total)
     return (residual, rfactor)
 
 

time: 166 us -> 71.7 us (0.43)
  waiting for transfers between devices: 117 us -> 28 us
  between operations: 14.2 us -> 0.92 us
  starting transfers between devices: 3.73 us -> 16.4 us
  matrix products: 4.54 us -> 0.55 us
    psum x2 -> x0, waiting for transfers between devices: 116 us -> none  [the longest x1 78.9 us: shards(): gram_matrix = lax.psum(local_gram, 'spec')]
    ppermute x0 -> x13, waiting for transfers between devices: none -> 26.8 us  [swap(): lax.ppermute(x, axis, [(i, i ^ bit) for i in range(lax.axis_size(axis))])]
    ppermute x0 -> x13, starting transfers between devices: none -> 12.7 us  [swap(): lax.ppermute(x, axis, [(i, i ^ bit) for i in range(lax.axis_size(axis))])]
    dot_general x1 -> x0, matrix products: 3.2 us -> none  [shards(): jnp.dot(sketch.T, sketch, precision=lax.Precision.HIGHEST, preferred_elem...]
    pallas_call x1 -> x2, Pallas kernels: 16.3 us -> 17 us  [the longest x1 16.4 us: factor(): pl.pallas_call(body, name='factor', out_shape=jax.ShapeDtypeStruct((n, n)...]
  transfers between devices with their start and end apart: 4 -> 15, of which waited for: 3 -> 11; matrix products, arithmetic and copies ran while one was open for 2% -> 4% of each run, Pallas kernels for 0% -> 0%
where the time goes in v2:
time: 71.7 us; the launch traced here: 71.4 us
  waiting for transfers between devices  28 us (39%)
  Pallas kernels  17 us (24%)
  starting transfers between devices  16.4 us (23%)
  other arithmetic  5.97 us (8%)
  local copies, waits for them, and re-layouts  2.56 us (4%)
  between operations  0.92 us (1%)
    ppermute x13, waiting for transfers between devices, swap(): lax.ppermute(x, axis, [(i, i ^ bit) for i in range(lax.axis_size(axis))])  26.8 us
    pallas_call x1, Pallas kernels, factor(): pl.pallas_call(body, name='factor', out_shape=jax.ShapeDtypeStruct((n, n)...  16.4 us
    ppermute x13, starting transfers between devices, swap(): lax.ppermute(x, axis, [(i, i ^ bit) for i in range(lax.axis_size(axis))])  12.7 us
    ppermute x1, starting transfers between devices, extended_2(): lax.ppermute(lax.slice_in_dim(block, block.shape[dim] - width, None, axis...  2.36 us
    reduce_sum x1, other arithmetic, windowed_depth(): return jnp.sum(values, axis=1)  2.24 us
  transfers between devices with their start and end apart: 15, of which 11 were waited for; matrix products, arithmetic and copies ran while one was open for 4% of the time, Pallas kernels for 0%

profile of v2, /device:TPU:0, one launch (start us, length us, event | category | flops | bytes accessed | tf_op | source)
XLA Modules:
  0.0 71.4 jit_solution(12236521812353250195)
XLA Ops:
  0.6 0.0 copy-start
  0.6 0.7 %convert_element_type.15 = f32[256]{0:T(256)S(1)} convert(s32[256]{0:T(256)} %param.20) | non-fusion elementwise | flops 256 | bytes 2048 | tf_op jit(solution)/shard_map/convert_element_type | solution.py:253
  1.4 0.8 %select_reduce_fusion.1 = (f32[256,4]{0,1:T(4,128)S(1)}, f32[256,4]{0,1:T(4,128)S(1)}) fusion(f32[32]{0:T(128)} %param.21, s32[256,4]{0,1:T(4,128)} %param.18, f32[32]{0:T(128)} %param.22), kind=kLoop, calls=%fused_computation.13 | loop fusion | flops 161792 | bytes 12544 | tf_op jit(solution)/shard_map/reduce_sum | solution.py:251
  2.2 0.7 mul.73
  2.9 2.2 %fusion.5 = f32[256,576]{0,1:T(8,128)S(1)} fusion(f32[256,4]{0,1:T(4,128)S(1)} %broadcast_divide_fusion, f32[256,4]{0,1:T(4,128)S(1)} %mul.73, f32[256]{0:T(256)S(1)} %convert_element_type.15, s32[256,4]{0,1:T(4,128)} %param.17, s32[576]{0:T(1024)S(1)} %iota_add_fusion), kind=kLoop, calls=%fused_computation.6 | loop fusion | flops 8699904 | bytes 605440 | tf_op jit(solution)/shard_map/reduce_sum | solution.py:231
  5.2 0.1 copy.21
  5.3 2.4 %collective-permute-start = (f32[256,32]{1,0:T(8,128)S(1)}, f32[256,32]{1,0:T(8,128)S(1)}, u32[]{:S(2)}, u32[]{:S(2)}) collective-permute-start(f32[256,32]{1,0:T(8,128)S(1)} %copy.21), channel_id=1, source_target_pairs={{0,1},{1,2},{2,3},{4,5},{5,6},{6,7},{8,9},{9,10},{10,11},{12,13},{... | collective-permute-start | bytes 98312 | tf_op jit(solution)/shard_map/ppermute | solution.py:207
  7.6 0.1 copy.22
  7.7 1.3 %collective-permute-start.1 = (f32[256,32]{1,0:T(8,128)S(1)}, f32[256,32]{1,0:T(8,128)S(1)}, u32[]{:S(2)}, u32[]{:S(2)}) collective-permute-start(f32[256,32]{1,0:T(8,128)S(1)} %copy.22), channel_id=1, source_target_pairs={{1,0},{2,1},{3,2},{5,4},{6,5},{7,6},{9,8},{10,9},{11,10},{13,12},{... | collective-permute-start | bytes 98312 | tf_op jit(solution)/shard_map/ppermute | solution.py:210
  9.1 0.0 copy-start.2
  9.1 0.0 copy-start.3
  9.1 0.0 copy-start.4
  9.1 0.2 copy.19
  9.3 0.1 copy.20
  9.4 0.6 compare_reduce_fusion
  10.1 0.0 collective-permute-done
  10.1 0.7 add_select_fusion
  10.7 1.1 %scatter-add.6 = f32[256,512]{1,0:T(8,128)S(1)} dynamic-update-slice(f32[256,512]{1,0:T(8,128)S(1)} %copy.19, f32[256,32]{1,0:T(8,128)S(1)} %add_select_fusion, s32[]{:T(128)} %constant.96.clone.1, s32[]{:T(128)} %constant.96.clone.1) | dynamic-update-slice | bytes 65540 | tf_op jit(solution)/shard_map/scatter-add | solution.py:260
  11.8 1.2 %collective-permute-done.1 = f32[256,32]{1,0:T(8,128)S(1)} collective-permute-done((f32[256,32]{1,0:T(8,128)S(1)}, f32[256,32]{1,0:T(8,128)S(1)}, u32[]{:S(2)}, u32[]{:S(2)}) %collective-permute-start.1) | collective-permute-done | bytes 32800 | tf_op jit(solution)/shard_map/ppermute | solution.py:210
  13.1 0.1 slice_add_fusion
  13.2 0.9 %scatter-add.9 = f32[256,512]{1,0:T(8,128)S(1)} dynamic-update-slice(f32[256,512]{1,0:T(8,128)S(1)} %scatter-add.6, f32[256,32]{1,0:T(8,128)S(1)} %slice_add_fusion, s32[]{:T(128)} %constant.96.clone.1, s32[]{:T(128)} %constant.95.clone.1) | dynamic-update-slice | bytes 65540 | tf_op jit(solution)/shard_map/scatter-add | solution.py:261
  14.1 0.3 subtract_convert_fusion
  14.4 0.0 copy-start.1
  14.4 0.3 fusion.7
  14.7 3.6 %collective-permute-start.2 = (f32[128,512]{1,0:T(8,128)S(1)}, f32[128,512]{1,0:T(8,128)S(1)}, u32[]{:S(2)}, u32[]{:S(2)}) collective-permute-start(f32[128,512]{1,0:T(8,128)S(1)} %constant_dynamic-slice_fusion), channel_id=1, source_target_pairs={{0,1},{1,0},{2,3},{3,2},{4,5},{5,4},{6,7},{7,6},{8,9},{9,8},{10,11... | collective-permute-start | bytes 786440 | tf_op jit(solution)/shard_map/ppermute | solution.py:157
  18.3 1.2 %collective-permute-done.2 = f32[128,512]{1,0:T(8,128)S(1)} collective-permute-done((f32[128,512]{1,0:T(8,128)S(1)}, f32[128,512]{1,0:T(8,128)S(1)}, u32[]{:S(2)}, u32[]{:S(2)}) %collective-permute-start.2) | collective-permute-done | bytes 262176 | tf_op jit(solution)/shard_map/ppermute | solution.py:157
  19.5 0.5 collective-permute-start.3
  20.1 8.1 %collective-permute-done.3.other_ref = f32[128,512]{1,0:T(8,128)S(1)} collective-permute-done((f32[128,512]{1,0:T(8,128)S(1)}, f32[128,512]{1,0:T(8,128)S(1)}, u32[]{:S(2)}, u32[]{:S(2)}) %collective-permute-start.3) | collective-permute-done | bytes 262176 | tf_op jit(solution)/shard_map/ppermute | solution.py:157
  28.2 0.5 gram.1
  28.7 0.1 collective-permute-start.4
  28.8 1.4 %collective-permute-done.4 = f32[5,64,128]{2,1,0:T(8,128)S(1)} collective-permute-done((f32[5,64,128]{2,1,0:T(8,128)S(1)}, f32[5,64,128]{2,1,0:T(8,128)S(1)}, u32[]{:S(2)}, u32[]{:S(2)}) %collective-permute-start.4) | collective-permute-done | bytes 163872 | tf_op jit(solution)/shard_map/ppermute | solution.py:157
  30.2 1.6 %collective-permute-start.5 = (f32[5,32,128]{2,1,0:T(8,128)S(1)}, f32[5,32,128]{2,1,0:T(8,128)S(1)}, u32[]{:S(2)}, u32[]{:S(2)}) collective-permute-start(f32[5,32,128]{2,1,0:T(8,128)S(1)} %dynamic-slice_add_fusion.1), channel_id=1, source_target_pairs={{0,4},{4,0},{8,12},{12,8},{16,20},{20,16},{24,28},{28,24},{1,5},{5... | collective-permute-start | bytes 245768 | tf_op jit(solution)/shard_map/ppermute | solution.py:157
  31.8 3.0 %collective-permute-done.5 = f32[5,32,128]{2,1,0:T(8,128)S(1)} collective-permute-done((f32[5,32,128]{2,1,0:T(8,128)S(1)}, f32[5,32,128]{2,1,0:T(8,128)S(1)}, u32[]{:S(2)}, u32[]{:S(2)}) %collective-permute-start.5) | collective-permute-done | bytes 81952 | tf_op jit(solution)/shard_map/ppermute | solution.py:157
  34.8 1.6 %collective-permute-start.6 = (f32[5,32,128]{2,1,0:T(8,128)S(1)}, f32[5,32,128]{2,1,0:T(8,128)S(1)}, u32[]{:S(2)}, u32[]{:S(2)}) collective-permute-start(f32[5,32,128]{2,1,0:T(8,128)S(1)} %add_add_fusion), channel_id=1, source_target_pairs={{0,8},{4,12},{8,0},{12,4},{16,24},{20,28},{24,16},{28,20},{1,9},{5... | collective-permute-start | bytes 245768 | tf_op jit(solution)/shard_map/ppermute | solution.py:157
  36.4 2.9 %collective-permute-done.6 = f32[5,32,128]{2,1,0:T(8,128)S(1)} collective-permute-done((f32[5,32,128]{2,1,0:T(8,128)S(1)}, f32[5,32,128]{2,1,0:T(8,128)S(1)}, u32[]{:S(2)}, u32[]{:S(2)}) %collective-permute-start.6) | collective-permute-done | bytes 81952 | tf_op jit(solution)/shard_map/ppermute | solution.py:157
  39.3 2.7 %collective-permute-start.7 = (f32[5,32,128]{2,1,0:T(8,128)S(1)}, f32[5,32,128]{2,1,0:T(8,128)S(1)}, u32[]{:S(2)}, u32[]{:S(2)}) collective-permute-start(f32[5,32,128]{2,1,0:T(8,128)S(1)} %add.90), channel_id=1, source_target_pairs={{0,16},{4,20},{8,24},{12,28},{16,0},{20,4},{24,8},{28,12},{1,17},{... | collective-permute-start | bytes 245768 | tf_op jit(solution)/shard_map/ppermute | solution.py:157
  42.0 2.8 %collective-permute-done.7 = f32[5,32,128]{2,1,0:T(8,128)S(1)} collective-permute-done((f32[5,32,128]{2,1,0:T(8,128)S(1)}, f32[5,32,128]{2,1,0:T(8,128)S(1)}, u32[]{:S(2)}, u32[]{:S(2)}) %collective-permute-start.7) | collective-permute-done | bytes 81952 | tf_op jit(solution)/shard_map/ppermute | solution.py:157
  44.7 1.6 %collective-permute-start.8 = (f32[5,32,128]{2,1,0:T(8,128)S(1)}, f32[5,32,128]{2,1,0:T(8,128)S(1)}, u32[]{:S(2)}, u32[]{:S(2)}) collective-permute-start(f32[5,32,128]{2,1,0:T(8,128)S(1)} %add.91.refs_0_), channel_id=1, source_target_pairs={{0,4},{4,0},{8,12},{12,8},{16,20},{20,16},{24,28},{28,24},{1,5},{5... | collective-permute-start | bytes 245768 | tf_op jit(solution)/shard_map/ppermute | solution.py:157
  46.3 0.3 collective-permute-start.9
  46.6 2.6 %collective-permute-done.8.refs_1_ = f32[5,32,128]{2,1,0:T(8,128)S(1)} collective-permute-done((f32[5,32,128]{2,1,0:T(8,128)S(1)}, f32[5,32,128]{2,1,0:T(8,128)S(1)}, u32[]{:S(2)}, u32[]{:S(2)}) %collective-permute-start.8) | collective-permute-done | bytes 81952 | tf_op jit(solution)/shard_map/ppermute | solution.py:157
  49.2 0.3 collective-permute-start.10
  49.5 0.5 collective-permute-start.12
  50.0 0.7 %collective-permute-done.9.refs_2_ = f32[5,32,128]{2,1,0:T(8,128)S(1)} collective-permute-done((f32[5,32,128]{2,1,0:T(8,128)S(1)}, f32[5,32,128]{2,1,0:T(8,128)S(1)}, u32[]{:S(2)}, u32[]{:S(2)}) %collective-permute-start.9) | collective-permute-done | bytes 81952 | tf_op jit(solution)/shard_map/ppermute | solution.py:157
  50.8 0.0 collective-permute-start.13
  50.8 2.9 %collective-permute-done.10.refs_3_ = f32[5,32,128]{2,1,0:T(8,128)S(1)} collective-permute-done((f32[5,32,128]{2,1,0:T(8,128)S(1)}, f32[5,32,128]{2,1,0:T(8,128)S(1)}, u32[]{:S(2)}, u32[]{:S(2)}) %collective-permute-start.10) | collective-permute-done | bytes 81952 | tf_op jit(solution)/shard_map/ppermute | solution.py:157
  53.7 0.0 collective-permute-start.14
  53.7 1.3 %collective-permute-done.14.refs_7_ = f32[5,32,128]{2,1,0:T(8,128)S(1)} collective-permute-done((f32[5,32,128]{2,1,0:T(8,128)S(1)}, f32[5,32,128]{2,1,0:T(8,128)S(1)}, u32[]{:S(2)}, u32[]{:S(2)}) %collective-permute-start.14) | collective-permute-done | bytes 81952 | tf_op jit(solution)/shard_map/ppermute | solution.py:157
  55.0 16.4 %factor.1 = f32[512,512]{1,0:T(8,128)} custom-call(f32[5,32,128]{2,1,0:T(8,128)S(1)} %add.91.refs_0_, f32[5,32,128]{2,1,0:T(8,128)S(1)} %collective-permute-done.8.refs_1_, f32[5,32,128]{2,1,0:T(8,128)S(1)} %collective-permute-done.9.refs_2_, f32[5,32,128]{2,1,0:T(8,128)S(1)} %collective-permute-done.10.refs_3_, ...), custom_call_target="tpu_custom_call" | custom-call | tf_op jit(solution)/shard_map/factor/pallas_call | solution.py:148
  (19 shorter events, 0.2 us)
Async XLA Ops:
  0.6 13.7 %copy-start = (bf16[512,512]{1,0:T(8,128)(2,1)S(1)}, bf16[512,512]{1,0:T(8,128)(2,1)}, u32[]{:S(2)}) copy-start(bf16[512,512]{1,0:T(8,128)(2,1)} %param.23) | copy-start | bytes 1572868
  5.3 4.8 %collective-permute-start = (f32[256,32]{1,0:T(8,128)S(1)}, f32[256,32]{1,0:T(8,128)S(1)}, u32[]{:S(2)}, u32[]{:S(2)}) collective-permute-start(f32[256,32]{1,0:T(8,128)S(1)} %copy.21), channel_id=1, source_target_pairs={{0,1},{1,2},{2,3},{4,5},{5,6},{6,7},{8,9},{9,10},{10,11},{12,13},{... | collective-permute-start | bytes 98312 | tf_op jit(solution)/shard_map/ppermute | solution.py:207
  7.7 5.3 %collective-permute-start.1 = (f32[256,32]{1,0:T(8,128)S(1)}, f32[256,32]{1,0:T(8,128)S(1)}, u32[]{:S(2)}, u32[]{:S(2)}) collective-permute-start(f32[256,32]{1,0:T(8,128)S(1)} %copy.22), channel_id=1, source_target_pairs={{1,0},{2,1},{3,2},{5,4},{6,5},{7,6},{9,8},{10,9},{11,10},{13,12},{... | collective-permute-start | bytes 98312 | tf_op jit(solution)/shard_map/ppermute | solution.py:210
  9.1 5.0 %copy-start.2 = (bf16[256,512]{1,0:T(8,128)(2,1)S(1)}, bf16[256,512]{1,0:T(8,128)(2,1)}, u32[]{:S(2)}) copy-start(bf16[256,512]{1,0:T(8,128)(2,1)} %param.14) | copy-start | bytes 786436
  9.1 5.0 %copy-start.3 = (bf16[16,512]{1,0:T(8,128)(2,1)S(1)}, bf16[16,512]{1,0:T(8,128)(2,1)}, u32[]{:S(2)}) copy-start(bf16[16,512]{1,0:T(8,128)(2,1)} %param.16) | copy-start | bytes 49156
  9.1 5.0 %copy-start.4 = (bf16[256,16]{0,1:T(8,128)(2,1)S(1)}, bf16[256,16]{0,1:T(8,128)(2,1)}, u32[]{:S(2)}) copy-start(bf16[256,16]{0,1:T(8,128)(2,1)} %param.15) | copy-start | bytes 24580
  14.4 5.2 %copy-start.1 = (bf16[256,512]{1,0:T(8,128)(2,1)}, bf16[256,512]{1,0:T(8,128)(2,1)S(1)}, u32[]{:S(2)}) copy-start(bf16[256,512]{1,0:T(8,128)(2,1)S(1)} %subtract_convert_fusion) | copy-start | bytes 786436
  14.7 4.8 %collective-permute-start.2 = (f32[128,512]{1,0:T(8,128)S(1)}, f32[128,512]{1,0:T(8,128)S(1)}, u32[]{:S(2)}, u32[]{:S(2)}) collective-permute-start(f32[128,512]{1,0:T(8,128)S(1)} %constant_dynamic-slice_fusion), channel_id=1, source_target_pairs={{0,1},{1,0},{2,3},{3,2},{4,5},{5,4},{6,7},{7,6},{8,9},{9,8},{10,11... | collective-permute-start | bytes 786440 | tf_op jit(solution)/shard_map/ppermute | solution.py:157
  19.5 8.7 %collective-permute-start.3 = (f32[128,512]{1,0:T(8,128)S(1)}, f32[128,512]{1,0:T(8,128)S(1)}, u32[]{:S(2)}, u32[]{:S(2)}) collective-permute-start(f32[128,512]{1,0:T(8,128)S(1)} %dynamic-slice_add_fusion.mine_ref), channel_id=1, source_target_pairs={{0,2},{1,3},{2,0},{3,1},{4,6},{5,7},{6,4},{7,5},{8,10},{9,11},{10,... | collective-permute-start | bytes 786440 | tf_op jit(solution)/shard_map/ppermute | solution.py:157
  28.7 1.5 %collective-permute-start.4 = (f32[5,64,128]{2,1,0:T(8,128)S(1)}, f32[5,64,128]{2,1,0:T(8,128)S(1)}, u32[]{:S(2)}, u32[]{:S(2)}) collective-permute-start(f32[5,64,128]{2,1,0:T(8,128)S(1)} %get-tuple-element.29), channel_id=1, source_target_pairs={{0,1},{1,0},{2,3},{3,2},{4,5},{5,4},{6,7},{7,6},{8,9},{9,8},{10,11... | collective-permute-start | bytes 491528 | tf_op jit(solution)/shard_map/ppermute | solution.py:157
  30.2 4.6 %collective-permute-start.5 = (f32[5,32,128]{2,1,0:T(8,128)S(1)}, f32[5,32,128]{2,1,0:T(8,128)S(1)}, u32[]{:S(2)}, u32[]{:S(2)}) collective-permute-start(f32[5,32,128]{2,1,0:T(8,128)S(1)} %dynamic-slice_add_fusion.1), channel_id=1, source_target_pairs={{0,4},{4,0},{8,12},{12,8},{16,20},{20,16},{24,28},{28,24},{1,5},{5... | collective-permute-start | bytes 245768 | tf_op jit(solution)/shard_map/ppermute | solution.py:157
  34.8 4.5 %collective-permute-start.6 = (f32[5,32,128]{2,1,0:T(8,128)S(1)}, f32[5,32,128]{2,1,0:T(8,128)S(1)}, u32[]{:S(2)}, u32[]{:S(2)}) collective-permute-start(f32[5,32,128]{2,1,0:T(8,128)S(1)} %add_add_fusion), channel_id=1, source_target_pairs={{0,8},{4,12},{8,0},{12,4},{16,24},{20,28},{24,16},{28,20},{1,9},{5... | collective-permute-start | bytes 245768 | tf_op jit(solution)/shard_map/ppermute | solution.py:157
  39.3 5.4 %collective-permute-start.7 = (f32[5,32,128]{2,1,0:T(8,128)S(1)}, f32[5,32,128]{2,1,0:T(8,128)S(1)}, u32[]{:S(2)}, u32[]{:S(2)}) collective-permute-start(f32[5,32,128]{2,1,0:T(8,128)S(1)} %add.90), channel_id=1, source_target_pairs={{0,16},{4,20},{8,24},{12,28},{16,0},{20,4},{24,8},{28,12},{1,17},{... | collective-permute-start | bytes 245768 | tf_op jit(solution)/shard_map/ppermute | solution.py:157
  44.7 4.5 %collective-permute-start.8 = (f32[5,32,128]{2,1,0:T(8,128)S(1)}, f32[5,32,128]{2,1,0:T(8,128)S(1)}, u32[]{:S(2)}, u32[]{:S(2)}) collective-permute-start(f32[5,32,128]{2,1,0:T(8,128)S(1)} %add.91.refs_0_), channel_id=1, source_target_pairs={{0,4},{4,0},{8,12},{12,8},{16,20},{20,16},{24,28},{28,24},{1,5},{5... | collective-permute-start | bytes 245768 | tf_op jit(solution)/shard_map/ppermute | solution.py:157
  46.3 4.4 %collective-permute-start.9 = (f32[5,32,128]{2,1,0:T(8,128)S(1)}, f32[5,32,128]{2,1,0:T(8,128)S(1)}, u32[]{:S(2)}, u32[]{:S(2)}) collective-permute-start(f32[5,32,128]{2,1,0:T(8,128)S(1)} %add.91.refs_0_), channel_id=1, source_target_pairs={{0,2},{1,3},{2,0},{3,1},{4,6},{5,7},{6,4},{7,5},{8,10},{9,11},{10,... | collective-permute-start | bytes 245768 | tf_op jit(solution)/shard_map/ppermute | solution.py:157
  49.2 4.4 %collective-permute-start.10 = (f32[5,32,128]{2,1,0:T(8,128)S(1)}, f32[5,32,128]{2,1,0:T(8,128)S(1)}, u32[]{:S(2)}, u32[]{:S(2)}) collective-permute-start(f32[5,32,128]{2,1,0:T(8,128)S(1)} %collective-permute-done.8.refs_1_), channel_id=1, source_target_pairs={{0,2},{1,3},{2,0},{3,1},{4,6},{5,7},{6,4},{7,5},{8,10},{9,11},{10,... | collective-permute-start | bytes 245768 | tf_op jit(solution)/shard_map/ppermute | solution.py:157
  49.5 4.2 %collective-permute-start.11 = (f32[5,32,128]{2,1,0:T(8,128)S(1)}, f32[5,32,128]{2,1,0:T(8,128)S(1)}, u32[]{:S(2)}, u32[]{:S(2)}) collective-permute-start(f32[5,32,128]{2,1,0:T(8,128)S(1)} %add.91.refs_0_), channel_id=1, source_target_pairs={{0,1},{1,0},{2,3},{3,2},{4,5},{5,4},{6,7},{7,6},{8,9},{9,8},{10,11... | collective-permute-start | bytes 245768 | tf_op jit(solution)/shard_map/ppermute | solution.py:157
  49.5 4.2 %collective-permute-start.12 = (f32[5,32,128]{2,1,0:T(8,128)S(1)}, f32[5,32,128]{2,1,0:T(8,128)S(1)}, u32[]{:S(2)}, u32[]{:S(2)}) collective-permute-start(f32[5,32,128]{2,1,0:T(8,128)S(1)} %collective-permute-done.8.refs_1_), channel_id=1, source_target_pairs={{0,1},{1,0},{2,3},{3,2},{4,5},{5,4},{6,7},{7,6},{8,9},{9,8},{10,11... | collective-permute-start | bytes 245768 | tf_op jit(solution)/shard_map/ppermute | solution.py:157
  50.8 2.9 %collective-permute-start.13 = (f32[5,32,128]{2,1,0:T(8,128)S(1)}, f32[5,32,128]{2,1,0:T(8,128)S(1)}, u32[]{:S(2)}, u32[]{:S(2)}) collective-permute-start(f32[5,32,128]{2,1,0:T(8,128)S(1)} %collective-permute-done.9.refs_2_), channel_id=1, source_target_pairs={{0,1},{1,0},{2,3},{3,2},{4,5},{5,4},{6,7},{7,6},{8,9},{9,8},{10,11... | collective-permute-start | bytes 245768 | tf_op jit(solution)/shard_map/ppermute | solution.py:157
  53.7 1.3 %collective-permute-start.14 = (f32[5,32,128]{2,1,0:T(8,128)S(1)}, f32[5,32,128]{2,1,0:T(8,128)S(1)}, u32[]{:S(2)}, u32[]{:S(2)}) collective-permute-start(f32[5,32,128]{2,1,0:T(8,128)S(1)} %collective-permute-done.10.refs_3_), channel_id=1, source_target_pairs={{0,1},{1,0},{2,3},{3,2},{4,5},{5,4},{6,7},{7,6},{8,9},{9,8},{10,11... | collective-permute-start | bytes 245768 | tf_op jit(solution)/shard_map/ppermute | solution.py:157

commit v3 on v2

--- a/solution.py
+++ b/solution.py
@@ -170,13 +170,12 @@
     return lax.dynamic_slice_in_dim(x, which * size, size, dim)
 
 
-def reduce_and_factor(partial_sketch, spectra_total):
+def reduce_and_factor(mine, send, spectra_total):
     waves, specs = lax.axis_size("wave"), lax.axis_size("spec")
-    core, y = lax.axis_index("wave") % 2, lax.axis_index("spec") % 2
-    k = partial_sketch.shape[1]
+    y = lax.axis_index("spec") % 2
+    k = mine.shape[1]
     slots = -(-((k // T) * (k // T + 1) // 2) // (waves // 2))
-    mine = half_of(partial_sketch, core, 0)
-    other = swap(half_of(partial_sketch, 1 - core, 0), "wave", 1)
+    other = swap(send, "wave", 1)
     for bit in bits_from(2, waves):
         mine = mine + other
         other = swap(mine, "wave", bit)
@@ -195,40 +194,78 @@
     return factor(pieces, offsets, slots, k)
 
 
-voigt_mix = 0.5
-log_two = 0.6931471805599453
-
-
-def extended_2(block, sides, width):
-    for axis, dim in sides:
-        count = lax.axis_size(axis)
-        forward = [(i, i + 1) for i in range(count - 1)]
-        backward = [(target, source) for source, target in forward]
-        low = lax.ppermute(
-            lax.slice_in_dim(block, block.shape[dim] - width, None, axis=dim), axis, forward
-        )
-        high = lax.ppermute(lax.slice_in_dim(block, 0, width, axis=dim), axis, backward)
-        block = jnp.concatenate([low, block, high], axis=dim)
-    return block
-
-
-def profile(offset, amplitude, inverse_width, wing_limit):
-    scaled = offset * inverse_width
-    values = amplitude * (
-        voigt_mix / (1.0 + scaled * scaled)
-        + (1.0 - voigt_mix) * jnp.exp(-log_two * scaled * scaled)
-    )
-    return jnp.where(jnp.abs(offset) <= wing_limit, values, 0.0)
-
-
-def windowed_depth(centre_int, amplitude, inverse_width, wing_limit, anchor, width):
-    pixels = anchor + jnp.arange(width, dtype=jnp.int32)
-    offset_int = pixels[None, None, :] - centre_int[:, :, None]
-    offset_float = offset_int.astype(jnp.float32)
-    values = profile(
-        offset_float, amplitude[:, :, None], inverse_width[:, :, None], wing_limit[:, :, None]
-    )
-    return jnp.sum(values, axis=1)
+CHUNK = 64
+
+
+def bell(offset, half_amplitude, inverse_width, wing):
+    u = offset * inverse_width
+    square = u * u
+    value = half_amplitude * (1.0 / (1.0 + square) + jnp.exp2(-square))
+    return jnp.where(jnp.abs(offset) <= wing, value, 0.0)
+
+
+def front(flux, coeffs_t, basis, own, over_core, over_x, wing, strength, widths, sketch_matrix):
+    spectra, pixels = flux.shape
+    absorbers = own.shape[0] // 3
+    half = spectra // 2
+
+    def body(strength_ref, widths_ref, flux_ref, coeffs_ref, basis_ref, own_ref, core_ref, x_ref,
+             wing_ref, m_ref, res_ref, keep_ref, send_ref, tau_ref, out_ref):
+        w = lax.axis_index("wave")
+        core = w % 2
+        first = (w * pixels).astype(jnp.float32)
+        wing_row = wing_ref[...].astype(jnp.float32)
+
+        def read(ref):
+            centre, line, column = (ref[n * absorbers:(n + 1) * absorbers, :] for n in range(3))
+            power = jnp.zeros_like(column)
+            width = jnp.zeros_like(column)
+            for n in range(strength_ref.shape[0]):
+                hit = line == float(n)
+                power = jnp.where(hit, strength_ref[n], power)
+                width = jnp.where(hit, widths_ref[n], width)
+            return centre, 0.5 * (column * power), 1.0 / width
+
+        def depth(params, start, count):
+            centre, amplitude, inverse = params
+            at = lax.broadcasted_iota(jnp.int32, (count, spectra), 0).astype(jnp.float32) + start
+            total = None
+            for a in range(absorbers):
+                one = slice(a, a + 1)
+                term = bell(at - centre[one], amplitude[one], inverse[one], wing_row)
+                total = term if total is None else total + term
+            return total
+
+        mine = read(own_ref)
+
+        def chunk(n, _):
+            row = pl.multiple_of(n * CHUNK, CHUNK)
+            tau_ref[pl.ds(row, CHUNK), :] = depth(mine, first + row.astype(jnp.float32), CHUNK)
+            return 0
+
+        lax.fori_loop(0, pixels // CHUNK, chunk, 0)
+        for ref, before in ((core_ref, core == 1), (x_ref, core == 0)):
+            row = pl.multiple_of(jnp.where(before, 0, pixels - WING), WING)
+            tau_ref[pl.ds(row, WING), :] += depth(read(ref), first + row.astype(jnp.float32), WING)
+        for n in range(pixels // T):
+            lanes = slice(n * T, (n + 1) * T)
+            seen = jnp.exp(-tau_ref[lanes, :].T)
+            continuum = lax.dot_general(coeffs_ref[...], basis_ref[:, lanes], (((0,), (0,)), ((), ())),
+                                        preferred_element_type=jnp.float32)
+            res_ref[:, lanes] = (flux_ref[:, lanes].astype(jnp.float32) - continuum * seen).astype(jnp.bfloat16)
+        out_ref[...] = jnp.dot(res_ref[...], m_ref[...], preferred_element_type=jnp.float32)
+        keep_ref[...] = out_ref[pl.ds(pl.multiple_of(core * half, half), half), :]
+        send_ref[...] = out_ref[pl.ds(pl.multiple_of((1 - core) * half, half), half), :]
+
+    k = sketch_matrix.shape[1]
+    smem, vmem = pl.BlockSpec(memory_space=pltpu.SMEM), pl.BlockSpec(memory_space=pltpu.VMEM)
+    rows = jax.ShapeDtypeStruct((half, k), jnp.float32)
+    return pl.pallas_call(
+        body, name="front", in_specs=[smem] * 2 + [vmem] * 8, out_specs=[vmem] * 3,
+        out_shape=(jax.ShapeDtypeStruct(flux.shape, jnp.bfloat16), rows, rows),
+        scratch_shapes=[pltpu.VMEM((pixels, spectra), jnp.float32), pltpu.VMEM((spectra, k), jnp.float32)],
+        compiler_params=pltpu.CompilerParams(vmem_limit_bytes=32 << 20),
+    )(strength, widths, flux, coeffs_t, basis, own, over_core, over_x, wing, sketch_matrix)
 
 
 def shards(
@@ -243,30 +280,16 @@
     line_widths,
     sketch_matrix,
 ):
-    spectra, pix_local = observed_flux.shape
-    first_pixel = lax.axis_index("wave") * pix_local
-    onehot = (
-        line_index[:, :, None] == jnp.arange(line_strength.shape[0], dtype=jnp.int32)[None, None, :]
-    ).astype(jnp.float32)
-    amplitude = column_factor * jnp.sum(onehot * line_strength, axis=2)
-    inverse_width = 1.0 / jnp.sum(onehot * line_widths, axis=2)
-    wing_limit = wing_width.astype(jnp.float32)[:, None]
-    extended = windowed_depth(
-        centres, amplitude, inverse_width, wing_limit, first_pixel - WING, pix_local + 2 * WING
-    )
-    outgoing = jnp.concatenate([extended[:, :WING], extended[:, -WING:]], axis=1)
-    padded_rims = extended_2(outgoing, (("wave", 1),), WING)
-    optical_depth = extended[:, WING:-WING]
-    optical_depth = optical_depth.at[:, :WING].add(padded_rims[:, :WING])
-    optical_depth = optical_depth.at[:, -WING:].add(padded_rims[:, 3 * WING :])
-    continuum = jnp.dot(continuum_coeffs, continuum_basis, preferred_element_type=jnp.float32)
-    residual = (observed_flux.astype(jnp.float32) - continuum * jnp.exp(-optical_depth)).astype(
-        jnp.bfloat16
-    )
-    spectra_total = spectra * lax.axis_size("spec")
-    partial_sketch = jnp.dot(residual, sketch_matrix, preferred_element_type=jnp.float32)
-    rfactor = reduce_and_factor(partial_sketch, spectra_total)
-    return (residual, rfactor)
+    waves = lax.axis_size("wave")
+    own = jnp.concatenate(
+        [centres.T.astype(jnp.float32), line_index.T.astype(jnp.float32), column_factor.T], axis=0)
+    across = [(i, (i + 1 if i % 2 else i - 1) % waves) for i in range(waves)]
+    over_x = lax.ppermute(own, "wave", across)
+    over_core = swap(own, "wave", 1)
+    residual, keep, send = front(
+        observed_flux, continuum_coeffs.T, continuum_basis, own, over_core, over_x,
+        wing_width[None, :], line_strength, line_widths, sketch_matrix)
+    return (residual, reduce_and_factor(keep, send, observed_flux.shape[0] * lax.axis_size("spec")))
 
 
 def solution(mesh):

time: 71.7 us -> 65.5 us (0.914)
  waiting for transfers between devices: 28 us -> 22.5 us
  other arithmetic: 5.97 us -> 0.81 us
  Pallas kernels: 17 us -> 19.7 us
  starting transfers between devices: 16.4 us -> 18.1 us
  local copies, waits for them, and re-layouts: 2.56 us -> 3.36 us
    ppermute x13 -> x14, waiting for transfers between devices: 26.8 us -> 21.8 us  [swap(): lax.ppermute(x, axis, [(i, i ^ bit) for i in range(lax.axis_size(axis))])]
    reduce_sum x2 -> x0, other arithmetic: 3.04 us -> none  [the longest x1 2.24 us: windowed_depth(): return jnp.sum(values, axis=1)]
    ppermute x13 -> x14, starting transfers between devices: 12.7 us -> 15.7 us  [swap(): lax.ppermute(x, axis, [(i, i ^ bit) for i in range(lax.axis_size(axis))])]
    unnamed x14 -> x16, local copies, waits for them, and re-layouts: 0.52 us -> 3.36 us
    pallas_call x0 -> x1, Pallas kernels: none -> 2.74 us  [front(): pl.pallas_call(body, name='front', in_specs=[smem] * 2 + [vmem] * 8, out_...]
    scatter-add x2 -> x0, local copies, waits for them, and re-layouts: 1.97 us -> none  [the longest x1 1.08 us: shards(): optical_depth = optical_depth.at[:, :WING].add(padded_rims[:, :WING])]
    another operation x2 -> x0, other arithmetic: 1.3 us -> none
    ppermute x2 -> x1, starting transfers between devices: 3.65 us -> 2.44 us  [shards(): over_x = lax.ppermute(own, 'wave', across)]
  transfers between devices with their start and end apart: 15 -> 15, of which waited for: 11 -> 11; matrix products, arithmetic and copies ran while one was open for 4% -> 0% of each run, Pallas kernels for 0% -> 0%
where the time goes in v3:
time: 65.5 us; the launch traced here: 65.3 us
  waiting for transfers between devices  22.5 us (34%)
  Pallas kernels  19.7 us (30%)
  starting transfers between devices  18.1 us (28%)
  local copies, waits for them, and re-layouts  3.36 us (5%)
  other arithmetic  0.81 us (1%)
  between operations  0.72 us (1%)
    ppermute x14, waiting for transfers between devices, swap(): lax.ppermute(x, axis, [(i, i ^ bit) for i in range(lax.axis_size(axis))])  21.8 us
    pallas_call x1, Pallas kernels, factor(): pl.pallas_call(body, name='factor', out_shape=jax.ShapeDtypeStruct((n, n)...  16.4 us
    ppermute x14, starting transfers between devices, swap(): lax.ppermute(x, axis, [(i, i ^ bit) for i in range(lax.axis_size(axis))])  15.7 us
    unnamed x16, local copies, waits for them, and re-layouts  3.36 us
    pallas_call x1, Pallas kernels, front(): pl.pallas_call(body, name='front', in_specs=[smem] * 2 + [vmem] * 8, out_...  2.74 us
    ppermute x1, starting transfers between devices, shards(): over_x = lax.ppermute(own, 'wave', across)  2.44 us
  transfers between devices with their start and end apart: 15, of which 11 were waited for; matrix products, arithmetic and copies ran while one was open for 0% of the time, Pallas kernels for 0%

profile of v3, /device:TPU:0, one launch (start us, length us, event | category | flops | bytes accessed | tf_op | source)
XLA Modules:
  0.0 65.3 jit_solution(10984062708271850235)
XLA Ops:
  0.6 0.7 %convert_bitcast_fusion = (f32[4,256]{1,0:T(4,128)S(1)}, f32[4,256]{1,0:T(4,128)S(1)}) fusion(s32[256,4]{0,1:T(4,128)} %param.14, s32[256,4]{0,1:T(4,128)} %param.13), kind=kLoop, calls=%fused_computation.3 | loop fusion | flops 2048 | bytes 16384 | tf_op jit(solution)/shard_map/convert_element_type | solution.py:285
  1.3 0.0 copy-start.7
  1.3 0.7 %copy-done.7 = f32[256,4]{0,1:T(4,128)S(1)} copy-done((f32[256,4]{0,1:T(4,128)S(1)}, f32[256,4]{0,1:T(4,128)}, u32[]{:S(2)}) %copy-start.7) | copy-done | bytes 4120
  2.0 0.0 copy-start.2
  2.0 0.0 copy-start.3
  2.0 2.4 %collective-permute-start.1 = (f32[12,256]{1,0:T(8,128)S(1)}, f32[12,256]{1,0:T(8,128)S(1)}, u32[]{:S(2)}, u32[]{:S(2)}) collective-permute-start(f32[12,256]{1,0:T(8,128)S(1)} %pad_maximum_fusion.own_ref), channel_id=1, source_target_pairs={{0,3},{1,2},{2,1},{3,0},{4,7},{5,6},{6,5},{7,4},{8,11},{9,10},{10,... | collective-permute-start | bytes 36872 | tf_op jit(solution)/shard_map/ppermute | solution.py:287
  4.5 0.7 %collective-permute-start = (f32[12,256]{1,0:T(8,128)S(1)}, f32[12,256]{1,0:T(8,128)S(1)}, u32[]{:S(2)}, u32[]{:S(2)}) collective-permute-start(f32[12,256]{1,0:T(8,128)S(1)} %pad_maximum_fusion.own_ref), channel_id=1, source_target_pairs={{0,1},{1,0},{2,3},{3,2},{4,5},{5,4},{6,7},{7,6},{8,9},{9,8},{10,11... | collective-permute-start | bytes 36872 | tf_op jit(solution)/shard_map/ppermute | solution.py:157
  5.2 0.8 %collective-permute-done.1.x_ref = f32[12,256]{1,0:T(8,128)S(1)} collective-permute-done((f32[12,256]{1,0:T(8,128)S(1)}, f32[12,256]{1,0:T(8,128)S(1)}, u32[]{:S(2)}, u32[]{:S(2)}) %collective-permute-start.1) | collective-permute-done | bytes 12320 | tf_op jit(solution)/shard_map/ppermute | solution.py:287
  5.9 0.1 collective-permute-done.core_ref
  6.0 0.0 copy-start.6
  6.0 0.0 copy-start.4
  6.0 0.0 copy-start.5
  6.0 0.0 copy-done.2
  6.0 0.0 copy-done.3
  6.0 0.6 copy-done.6
  6.7 0.0 copy-done.4
  6.7 0.0 copy-done.5
  6.7 1.0 %copy-done = bf16[512,512]{1,0:T(8,128)(2,1)S(1)} copy-done((bf16[512,512]{1,0:T(8,128)(2,1)S(1)}, bf16[512,512]{1,0:T(8,128)(2,1)}, u32[]{:S(2)}) %copy-start) | copy-done | bytes 524312
  7.7 0.9 %copy-done.1 = bf16[256,512]{1,0:T(8,128)(2,1)S(1)} copy-done((bf16[256,512]{1,0:T(8,128)(2,1)S(1)}, bf16[256,512]{1,0:T(8,128)(2,1)}, u32[]{:S(2)}) %copy-start.1) | copy-done | bytes 262168
  8.7 2.7 %front.1 = (bf16[256,512]{1,0:T(8,128)(2,1)}, f32[128,512]{1,0:T(8,128)S(1)}, f32[128,512]{1,0:T(8,128)S(1)}) custom-call(f32[32]{0:T(128)S(1)} %copy-done.5, f32[32]{0:T(128)S(1)} %copy-done.6, bf16[256,512]{1,0:T(8,128)(2,1)S(1)} %copy-done.1, bf16[16,256]{1,0:T(8,128)(2,1)S(1)} %bitcast.7, bf16[16,512]{1,0:T(8,128)(2,1)S(1)} %copy-done.2, ...), custom_call_target="tpu_custom_call" | custom-call | tf_op jit(solution)/shard_map/front/pallas_call | solution.py:263
  11.4 0.6 collective-permute-start.2
  12.0 1.2 %collective-permute-done.2 = f32[128,512]{1,0:T(8,128)S(1)} collective-permute-done((f32[128,512]{1,0:T(8,128)S(1)}, f32[128,512]{1,0:T(8,128)S(1)}, u32[]{:S(2)}, u32[]{:S(2)}) %collective-permute-start.2) | collective-permute-done | bytes 262176 | tf_op jit(solution)/shard_map/ppermute | solution.py:157
  13.2 2.2 %collective-permute-start.3 = (f32[128,512]{1,0:T(8,128)S(1)}, f32[128,512]{1,0:T(8,128)S(1)}, u32[]{:S(2)}, u32[]{:S(2)}) collective-permute-start(f32[128,512]{1,0:T(8,128)S(1)} %add.30.mine_ref), channel_id=1, source_target_pairs={{0,2},{1,3},{2,0},{3,1},{4,6},{5,7},{6,4},{7,5},{8,10},{9,11},{10,... | collective-permute-start | bytes 786440 | tf_op jit(solution)/shard_map/ppermute | solution.py:157
  15.4 6.6 %collective-permute-done.3.other_ref = f32[128,512]{1,0:T(8,128)S(1)} collective-permute-done((f32[128,512]{1,0:T(8,128)S(1)}, f32[128,512]{1,0:T(8,128)S(1)}, u32[]{:S(2)}, u32[]{:S(2)}) %collective-permute-start.3) | collective-permute-done | bytes 262176 | tf_op jit(solution)/shard_map/ppermute | solution.py:157
  22.1 0.5 gram.1
  22.6 0.1 collective-permute-start.4
  22.7 1.4 %collective-permute-done.4 = f32[5,64,128]{2,1,0:T(8,128)S(1)} collective-permute-done((f32[5,64,128]{2,1,0:T(8,128)S(1)}, f32[5,64,128]{2,1,0:T(8,128)S(1)}, u32[]{:S(2)}, u32[]{:S(2)}) %collective-permute-start.4) | collective-permute-done | bytes 163872 | tf_op jit(solution)/shard_map/ppermute | solution.py:157
  24.1 1.8 %collective-permute-start.5 = (f32[5,32,128]{2,1,0:T(8,128)S(1)}, f32[5,32,128]{2,1,0:T(8,128)S(1)}, u32[]{:S(2)}, u32[]{:S(2)}) collective-permute-start(f32[5,32,128]{2,1,0:T(8,128)S(1)} %dynamic-slice_add_fusion), channel_id=1, source_target_pairs={{0,4},{4,0},{8,12},{12,8},{16,20},{20,16},{24,28},{28,24},{1,5},{5... | collective-permute-start | bytes 245768 | tf_op jit(solution)/shard_map/ppermute | solution.py:157
  25.9 2.8 %collective-permute-done.5 = f32[5,32,128]{2,1,0:T(8,128)S(1)} collective-permute-done((f32[5,32,128]{2,1,0:T(8,128)S(1)}, f32[5,32,128]{2,1,0:T(8,128)S(1)}, u32[]{:S(2)}, u32[]{:S(2)}) %collective-permute-start.5) | collective-permute-done | bytes 81952 | tf_op jit(solution)/shard_map/ppermute | solution.py:157
  28.7 1.9 %collective-permute-start.6 = (f32[5,32,128]{2,1,0:T(8,128)S(1)}, f32[5,32,128]{2,1,0:T(8,128)S(1)}, u32[]{:S(2)}, u32[]{:S(2)}) collective-permute-start(f32[5,32,128]{2,1,0:T(8,128)S(1)} %add_add_fusion), channel_id=1, source_target_pairs={{0,8},{4,12},{8,0},{12,4},{16,24},{20,28},{24,16},{28,20},{1,9},{5... | collective-permute-start | bytes 245768 | tf_op jit(solution)/shard_map/ppermute | solution.py:157
  30.5 2.6 %collective-permute-done.6 = f32[5,32,128]{2,1,0:T(8,128)S(1)} collective-permute-done((f32[5,32,128]{2,1,0:T(8,128)S(1)}, f32[5,32,128]{2,1,0:T(8,128)S(1)}, u32[]{:S(2)}, u32[]{:S(2)}) %collective-permute-start.6) | collective-permute-done | bytes 81952 | tf_op jit(solution)/shard_map/ppermute | solution.py:157
  33.2 2.9 %collective-permute-start.7 = (f32[5,32,128]{2,1,0:T(8,128)S(1)}, f32[5,32,128]{2,1,0:T(8,128)S(1)}, u32[]{:S(2)}, u32[]{:S(2)}) collective-permute-start(f32[5,32,128]{2,1,0:T(8,128)S(1)} %add.37), channel_id=1, source_target_pairs={{0,16},{4,20},{8,24},{12,28},{16,0},{20,4},{24,8},{28,12},{1,17},{... | collective-permute-start | bytes 245768 | tf_op jit(solution)/shard_map/ppermute | solution.py:157
  36.1 2.5 %collective-permute-done.7 = f32[5,32,128]{2,1,0:T(8,128)S(1)} collective-permute-done((f32[5,32,128]{2,1,0:T(8,128)S(1)}, f32[5,32,128]{2,1,0:T(8,128)S(1)}, u32[]{:S(2)}, u32[]{:S(2)}) %collective-permute-start.7) | collective-permute-done | bytes 81952 | tf_op jit(solution)/shard_map/ppermute | solution.py:157
  38.6 1.8 %collective-permute-start.8 = (f32[5,32,128]{2,1,0:T(8,128)S(1)}, f32[5,32,128]{2,1,0:T(8,128)S(1)}, u32[]{:S(2)}, u32[]{:S(2)}) collective-permute-start(f32[5,32,128]{2,1,0:T(8,128)S(1)} %add.38.refs_0_), channel_id=1, source_target_pairs={{0,4},{4,0},{8,12},{12,8},{16,20},{20,16},{24,28},{28,24},{1,5},{5... | collective-permute-start | bytes 245768 | tf_op jit(solution)/shard_map/ppermute | solution.py:157
  40.4 1.5 %collective-permute-start.9 = (f32[5,32,128]{2,1,0:T(8,128)S(1)}, f32[5,32,128]{2,1,0:T(8,128)S(1)}, u32[]{:S(2)}, u32[]{:S(2)}) collective-permute-start(f32[5,32,128]{2,1,0:T(8,128)S(1)} %add.38.refs_0_), channel_id=1, source_target_pairs={{0,2},{1,3},{2,0},{3,1},{4,6},{5,7},{6,4},{7,5},{8,10},{9,11},{10,... | collective-permute-start | bytes 245768 | tf_op jit(solution)/shard_map/ppermute | solution.py:157
  41.9 1.2 %collective-permute-done.8.refs_1_ = f32[5,32,128]{2,1,0:T(8,128)S(1)} collective-permute-done((f32[5,32,128]{2,1,0:T(8,128)S(1)}, f32[5,32,128]{2,1,0:T(8,128)S(1)}, u32[]{:S(2)}, u32[]{:S(2)}) %collective-permute-start.8) | collective-permute-done | bytes 81952 | tf_op jit(solution)/shard_map/ppermute | solution.py:157
  43.1 1.7 %collective-permute-start.10 = (f32[5,32,128]{2,1,0:T(8,128)S(1)}, f32[5,32,128]{2,1,0:T(8,128)S(1)}, u32[]{:S(2)}, u32[]{:S(2)}) collective-permute-start(f32[5,32,128]{2,1,0:T(8,128)S(1)} %collective-permute-done.8.refs_1_), channel_id=1, source_target_pairs={{0,2},{1,3},{2,0},{3,1},{4,6},{5,7},{6,4},{7,5},{8,10},{9,11},{10,... | collective-permute-start | bytes 245768 | tf_op jit(solution)/shard_map/ppermute | solution.py:157
  44.9 0.0 collective-permute-start.11
  44.9 0.5 collective-permute-start.12
  45.4 0.0 collective-permute-done.9.refs_2_
  45.4 0.0 collective-permute-start.13
  45.4 2.2 %collective-permute-done.10.refs_3_ = f32[5,32,128]{2,1,0:T(8,128)S(1)} collective-permute-done((f32[5,32,128]{2,1,0:T(8,128)S(1)}, f32[5,32,128]{2,1,0:T(8,128)S(1)}, u32[]{:S(2)}, u32[]{:S(2)}) %collective-permute-start.10) | collective-permute-done | bytes 81952 | tf_op jit(solution)/shard_map/ppermute | solution.py:157
  47.6 0.0 collective-permute-start.14
  47.6 0.0 collective-permute-done.11.refs_4_
  47.6 0.0 collective-permute-done.13.refs_6_
  47.6 0.0 collective-permute-done.12.refs_5_
  47.6 1.3 %collective-permute-done.14.refs_7_ = f32[5,32,128]{2,1,0:T(8,128)S(1)} collective-permute-done((f32[5,32,128]{2,1,0:T(8,128)S(1)}, f32[5,32,128]{2,1,0:T(8,128)S(1)}, u32[]{:S(2)}, u32[]{:S(2)}) %collective-permute-start.14) | collective-permute-done | bytes 81952 | tf_op jit(solution)/shard_map/ppermute | solution.py:157
  48.8 16.4 %factor.1 = f32[512,512]{1,0:T(8,128)} custom-call(f32[5,32,128]{2,1,0:T(8,128)S(1)} %add.38.refs_0_, f32[5,32,128]{2,1,0:T(8,128)S(1)} %collective-permute-done.8.refs_1_, f32[5,32,128]{2,1,0:T(8,128)S(1)} %collective-permute-done.9.refs_2_, f32[5,32,128]{2,1,0:T(8,128)S(1)} %collective-permute-done.10.refs_3_, ...), custom_call_target="tpu_custom_call" | custom-call | tf_op jit(solution)/shard_map/factor/pallas_call | solution.py:148
  (8 shorter events, 0.1 us)
Async XLA Ops:
  1.3 0.7 %copy-start.7 = (f32[256,4]{0,1:T(4,128)S(1)}, f32[256,4]{0,1:T(4,128)}, u32[]{:S(2)}) copy-start(f32[256,4]{0,1:T(4,128)} %param.15) | copy-start | bytes 12292
  2.0 4.0 %copy-start.2 = (bf16[16,512]{1,0:T(8,128)(2,1)S(1)}, bf16[16,512]{1,0:T(8,128)(2,1)}, u32[]{:S(2)}) copy-start(bf16[16,512]{1,0:T(8,128)(2,1)} %basis_ref.1) | copy-start | bytes 49156
  2.0 4.0 %copy-start.3 = (bf16[256,16]{0,1:T(8,128)(2,1)S(1)}, bf16[256,16]{0,1:T(8,128)(2,1)}, u32[]{:S(2)}) copy-start(bf16[256,16]{0,1:T(8,128)(2,1)} %param.11) | copy-start | bytes 24580
  2.0 3.9 %collective-permute-start.1 = (f32[12,256]{1,0:T(8,128)S(1)}, f32[12,256]{1,0:T(8,128)S(1)}, u32[]{:S(2)}, u32[]{:S(2)}) collective-permute-start(f32[12,256]{1,0:T(8,128)S(1)} %pad_maximum_fusion.own_ref), channel_id=1, source_target_pairs={{0,3},{1,2},{2,1},{3,0},{4,7},{5,6},{6,5},{7,4},{8,11},{9,10},{10,... | collective-permute-start | bytes 36872 | tf_op jit(solution)/shard_map/ppermute | solution.py:287
  4.5 1.5 %collective-permute-start = (f32[12,256]{1,0:T(8,128)S(1)}, f32[12,256]{1,0:T(8,128)S(1)}, u32[]{:S(2)}, u32[]{:S(2)}) collective-permute-start(f32[12,256]{1,0:T(8,128)S(1)} %pad_maximum_fusion.own_ref), channel_id=1, source_target_pairs={{0,1},{1,0},{2,3},{3,2},{4,5},{5,4},{6,7},{7,6},{8,9},{9,8},{10,11... | collective-permute-start | bytes 36872 | tf_op jit(solution)/shard_map/ppermute | solution.py:157
  6.0 0.7 %copy-start.6 = (f32[32]{0:T(128)S(1)}, f32[32]{0:T(128)}, u32[]{:S(2)}) copy-start(f32[32]{0:T(128)} %widths_ref.1) | copy-start | bytes 388
  6.0 0.7 %copy-start.4 = (s32[256]{0:T(256)S(1)}, s32[256]{0:T(256)}, u32[]{:S(2)}) copy-start(s32[256]{0:T(256)} %param.16) | copy-start | bytes 3076
  6.0 0.7 %copy-start.5 = (f32[32]{0:T(128)S(1)}, f32[32]{0:T(128)}, u32[]{:S(2)}) copy-start(f32[32]{0:T(128)} %strength_ref.1) | copy-start | bytes 388
  6.7 1.0 %copy-start = (bf16[512,512]{1,0:T(8,128)(2,1)S(1)}, bf16[512,512]{1,0:T(8,128)(2,1)}, u32[]{:S(2)}) copy-start(bf16[512,512]{1,0:T(8,128)(2,1)} %m_ref.1) | copy-start | bytes 1572868
  7.7 0.9 %copy-start.1 = (bf16[256,512]{1,0:T(8,128)(2,1)S(1)}, bf16[256,512]{1,0:T(8,128)(2,1)}, u32[]{:S(2)}) copy-start(bf16[256,512]{1,0:T(8,128)(2,1)} %flux_ref.1) | copy-start | bytes 786436
  11.4 1.7 %collective-permute-start.2 = (f32[128,512]{1,0:T(8,128)S(1)}, f32[128,512]{1,0:T(8,128)S(1)}, u32[]{:S(2)}, u32[]{:S(2)}) collective-permute-start(f32[128,512]{1,0:T(8,128)S(1)} %get-tuple-element.9), channel_id=1, source_target_pairs={{0,1},{1,0},{2,3},{3,2},{4,5},{5,4},{6,7},{7,6},{8,9},{9,8},{10,11... | collective-permute-start | bytes 786440 | tf_op jit(solution)/shard_map/ppermute | solution.py:157
  13.2 8.8 %collective-permute-start.3 = (f32[128,512]{1,0:T(8,128)S(1)}, f32[128,512]{1,0:T(8,128)S(1)}, u32[]{:S(2)}, u32[]{:S(2)}) collective-permute-start(f32[128,512]{1,0:T(8,128)S(1)} %add.30.mine_ref), channel_id=1, source_target_pairs={{0,2},{1,3},{2,0},{3,1},{4,6},{5,7},{6,4},{7,5},{8,10},{9,11},{10,... | collective-permute-start | bytes 786440 | tf_op jit(solution)/shard_map/ppermute | solution.py:157
  22.6 1.5 %collective-permute-start.4 = (f32[5,64,128]{2,1,0:T(8,128)S(1)}, f32[5,64,128]{2,1,0:T(8,128)S(1)}, u32[]{:S(2)}, u32[]{:S(2)}) collective-permute-start(f32[5,64,128]{2,1,0:T(8,128)S(1)} %get-tuple-element.11), channel_id=1, source_target_pairs={{0,1},{1,0},{2,3},{3,2},{4,5},{5,4},{6,7},{7,6},{8,9},{9,8},{10,11... | collective-permute-start | bytes 491528 | tf_op jit(solution)/shard_map/ppermute | solution.py:157
  24.1 4.6 %collective-permute-start.5 = (f32[5,32,128]{2,1,0:T(8,128)S(1)}, f32[5,32,128]{2,1,0:T(8,128)S(1)}, u32[]{:S(2)}, u32[]{:S(2)}) collective-permute-start(f32[5,32,128]{2,1,0:T(8,128)S(1)} %dynamic-slice_add_fusion), channel_id=1, source_target_pairs={{0,4},{4,0},{8,12},{12,8},{16,20},{20,16},{24,28},{28,24},{1,5},{5... | collective-permute-start | bytes 245768 | tf_op jit(solution)/shard_map/ppermute | solution.py:157
  28.7 4.5 %collective-permute-start.6 = (f32[5,32,128]{2,1,0:T(8,128)S(1)}, f32[5,32,128]{2,1,0:T(8,128)S(1)}, u32[]{:S(2)}, u32[]{:S(2)}) collective-permute-start(f32[5,32,128]{2,1,0:T(8,128)S(1)} %add_add_fusion), channel_id=1, source_target_pairs={{0,8},{4,12},{8,0},{12,4},{16,24},{20,28},{24,16},{28,20},{1,9},{5... | collective-permute-start | bytes 245768 | tf_op jit(solution)/shard_map/ppermute | solution.py:157
  33.2 5.4 %collective-permute-start.7 = (f32[5,32,128]{2,1,0:T(8,128)S(1)}, f32[5,32,128]{2,1,0:T(8,128)S(1)}, u32[]{:S(2)}, u32[]{:S(2)}) collective-permute-start(f32[5,32,128]{2,1,0:T(8,128)S(1)} %add.37), channel_id=1, source_target_pairs={{0,16},{4,20},{8,24},{12,28},{16,0},{20,4},{24,8},{28,12},{1,17},{... | collective-permute-start | bytes 245768 | tf_op jit(solution)/shard_map/ppermute | solution.py:157
  38.6 4.5 %collective-permute-start.8 = (f32[5,32,128]{2,1,0:T(8,128)S(1)}, f32[5,32,128]{2,1,0:T(8,128)S(1)}, u32[]{:S(2)}, u32[]{:S(2)}) collective-permute-start(f32[5,32,128]{2,1,0:T(8,128)S(1)} %add.38.refs_0_), channel_id=1, source_target_pairs={{0,4},{4,0},{8,12},{12,8},{16,20},{20,16},{24,28},{28,24},{1,5},{5... | collective-permute-start | bytes 245768 | tf_op jit(solution)/shard_map/ppermute | solution.py:157
  40.4 5.0 %collective-permute-start.9 = (f32[5,32,128]{2,1,0:T(8,128)S(1)}, f32[5,32,128]{2,1,0:T(8,128)S(1)}, u32[]{:S(2)}, u32[]{:S(2)}) collective-permute-start(f32[5,32,128]{2,1,0:T(8,128)S(1)} %add.38.refs_0_), channel_id=1, source_target_pairs={{0,2},{1,3},{2,0},{3,1},{4,6},{5,7},{6,4},{7,5},{8,10},{9,11},{10,... | collective-permute-start | bytes 245768 | tf_op jit(solution)/shard_map/ppermute | solution.py:157
  43.1 4.4 %collective-permute-start.10 = (f32[5,32,128]{2,1,0:T(8,128)S(1)}, f32[5,32,128]{2,1,0:T(8,128)S(1)}, u32[]{:S(2)}, u32[]{:S(2)}) collective-permute-start(f32[5,32,128]{2,1,0:T(8,128)S(1)} %collective-permute-done.8.refs_1_), channel_id=1, source_target_pairs={{0,2},{1,3},{2,0},{3,1},{4,6},{5,7},{6,4},{7,5},{8,10},{9,11},{10,... | collective-permute-start | bytes 245768 | tf_op jit(solution)/shard_map/ppermute | solution.py:157
  44.9 2.7 %collective-permute-start.11 = (f32[5,32,128]{2,1,0:T(8,128)S(1)}, f32[5,32,128]{2,1,0:T(8,128)S(1)}, u32[]{:S(2)}, u32[]{:S(2)}) collective-permute-start(f32[5,32,128]{2,1,0:T(8,128)S(1)} %add.38.refs_0_), channel_id=1, source_target_pairs={{0,1},{1,0},{2,3},{3,2},{4,5},{5,4},{6,7},{7,6},{8,9},{9,8},{10,11... | collective-permute-start | bytes 245768 | tf_op jit(solution)/shard_map/ppermute | solution.py:157
  44.9 2.7 %collective-permute-start.12 = (f32[5,32,128]{2,1,0:T(8,128)S(1)}, f32[5,32,128]{2,1,0:T(8,128)S(1)}, u32[]{:S(2)}, u32[]{:S(2)}) collective-permute-start(f32[5,32,128]{2,1,0:T(8,128)S(1)} %collective-permute-done.8.refs_1_), channel_id=1, source_target_pairs={{0,1},{1,0},{2,3},{3,2},{4,5},{5,4},{6,7},{7,6},{8,9},{9,8},{10,11... | collective-permute-start | bytes 245768 | tf_op jit(solution)/shard_map/ppermute | solution.py:157
  45.4 2.2 %collective-permute-start.13 = (f32[5,32,128]{2,1,0:T(8,128)S(1)}, f32[5,32,128]{2,1,0:T(8,128)S(1)}, u32[]{:S(2)}, u32[]{:S(2)}) collective-permute-start(f32[5,32,128]{2,1,0:T(8,128)S(1)} %collective-permute-done.9.refs_2_), channel_id=1, source_target_pairs={{0,1},{1,0},{2,3},{3,2},{4,5},{5,4},{6,7},{7,6},{8,9},{9,8},{10,11... | collective-permute-start | bytes 245768 | tf_op jit(solution)/shard_map/ppermute | solution.py:157
  47.6 1.3 %collective-permute-start.14 = (f32[5,32,128]{2,1,0:T(8,128)S(1)}, f32[5,32,128]{2,1,0:T(8,128)S(1)}, u32[]{:S(2)}, u32[]{:S(2)}) collective-permute-start(f32[5,32,128]{2,1,0:T(8,128)S(1)} %collective-permute-done.10.refs_3_), channel_id=1, source_target_pairs={{0,1},{1,0},{2,3},{3,2},{4,5},{5,4},{6,7},{7,6},{8,9},{9,8},{10,11... | collective-permute-start | bytes 245768 | tf_op jit(solution)/shard_map/ppermute | solution.py:157

commit v4 on v3

--- a/solution.py
+++ b/solution.py
@@ -80,12 +80,14 @@
 
 
 def gram_blocks(mine, other, slots, scale):
-    rows, k = mine.shape
-
-    def body(mine_ref, other_ref, keep_ref, send_ref, s_ref, g_ref):
+    part, k = mine[0].shape
+
+    def body(*refs):
+        mine_refs, other_refs, (keep_ref, send_ref, s_ref, g_ref) = refs[:PARTS], refs[PARTS:2 * PARTS], refs[2 * PARTS:]
         w = lax.axis_index("wave")
         core, x = w % 2, w // 2
-        s_ref[...] = mine_ref[...] + other_ref[...]
+        for n in range(PARTS):
+            s_ref[n * part:(n + 1) * part, :] = mine_refs[n][...] + other_refs[n][...]
         for t in range(slots):
             i, j = blocks_of(x, slots, t, k // T)
             g_ref[...] = scale * lax.dot_general(
@@ -98,9 +100,9 @@
     shape = jax.ShapeDtypeStruct((slots, T // 2, T), jnp.float32)
     return pl.pallas_call(
         body, name="gram", out_shape=(shape, shape),
-        scratch_shapes=[pltpu.VMEM((rows, k), jnp.float32), pltpu.VMEM((T, T), jnp.float32)],
+        scratch_shapes=[pltpu.VMEM((PARTS * part, k), jnp.float32), pltpu.VMEM((T, T), jnp.float32)],
         compiler_params=pltpu.CompilerParams(vmem_limit_bytes=32 << 20),
-    )(mine, other)
+    )(*mine, *other)
 
 
 def factor(pieces, offsets, slots, n):
@@ -173,12 +175,12 @@
 def reduce_and_factor(mine, send, spectra_total):
     waves, specs = lax.axis_size("wave"), lax.axis_size("spec")
     y = lax.axis_index("spec") % 2
-    k = mine.shape[1]
+    k = mine[0].shape[1]
     slots = -(-((k // T) * (k // T + 1) // 2) // (waves // 2))
-    other = swap(send, "wave", 1)
+    other = [swap(p, "wave", 1) for p in send]
     for bit in bits_from(2, waves):
-        mine = mine + other
-        other = swap(mine, "wave", bit)
+        mine = [p + q for p, q in zip(mine, other)]
+        other = [swap(p, "wave", bit) for p in mine]
     keep, send = gram_blocks(mine, other, slots, 1.0 / spectra_total)
     got = swap(send, "wave", 1)
     mine = half_of(keep, y, 1) + half_of(got, y, 1)
@@ -204,68 +206,108 @@
     return jnp.where(jnp.abs(offset) <= wing, value, 0.0)
 
 
-def front(flux, coeffs_t, basis, own, over_core, over_x, wing, strength, widths, sketch_matrix):
+PARTS = 2
+SMEM = pl.BlockSpec(memory_space=pltpu.SMEM)
+VMEM = pl.BlockSpec(memory_space=pltpu.VMEM)
+HBM = pl.BlockSpec(memory_space=pltpu.HBM)
+
+
+def line_table(centres, line_index, column_factor, wing, strength, widths):
+    absorbers, spectra = centres.shape
+
+    def body(centre_ref, line_ref, column_ref, wing_ref, strength_ref, widths_ref, out_ref,
+             c_ref, l_ref, f_ref, g_ref, power_ref, width_ref, sems):
+        copies = [pltpu.make_async_copy(source, target, sems.at[n]) for n, (source, target) in enumerate(
+            ((strength_ref, power_ref), (widths_ref, width_ref), (line_ref, l_ref), (column_ref, f_ref),
+             (centre_ref, c_ref), (wing_ref, g_ref)))]
+        for copy in copies:
+            copy.start()
+        for copy in copies:
+            copy.wait()
+        line = l_ref[...]
+        power = jnp.zeros(line.shape, jnp.float32)
+        width = jnp.ones(line.shape, jnp.float32)
+        for n in range(strength.shape[0]):
+            hit = line == n
+            power = jnp.where(hit, power_ref[n], power)
+            width = jnp.where(hit, width_ref[n], width)
+        out_ref[0:absorbers, :] = c_ref[...].astype(jnp.float32)
+        out_ref[absorbers:2 * absorbers, :] = 0.5 * (f_ref[...] * power)
+        out_ref[2 * absorbers:3 * absorbers, :] = 1.0 / width
+        out_ref[3 * absorbers:4 * absorbers, :] = jnp.broadcast_to(
+            g_ref[...].astype(jnp.float32), (absorbers, spectra))
+
+    return pl.pallas_call(
+        body, name="lines", in_specs=[HBM] * 6, out_specs=VMEM,
+        out_shape=jax.ShapeDtypeStruct((4 * absorbers, spectra), jnp.float32),
+        scratch_shapes=[pltpu.VMEM(centres.shape, jnp.int32), pltpu.VMEM(centres.shape, jnp.int32),
+                        pltpu.VMEM(centres.shape, jnp.float32), pltpu.VMEM(wing.shape, jnp.int32),
+                        pltpu.SMEM(strength.shape, jnp.float32), pltpu.SMEM(widths.shape, jnp.float32),
+                        pltpu.SemaphoreType.DMA((6,))],
+    )(centres, line_index, column_factor, wing, strength, widths)
+
+
+def front(flux, coeffs_t, basis, own, over_core, over_x, sketch_matrix):
     spectra, pixels = flux.shape
-    absorbers = own.shape[0] // 3
-    half = spectra // 2
-
-    def body(strength_ref, widths_ref, flux_ref, coeffs_ref, basis_ref, own_ref, core_ref, x_ref,
-             wing_ref, m_ref, res_ref, keep_ref, send_ref, tau_ref, out_ref):
+    absorbers = own.shape[0] // 4
+    part = spectra // (2 * PARTS)
+    k = sketch_matrix.shape[1]
+
+    def body(flux_hbm, coeffs_hbm, basis_hbm, m_hbm, own_ref, core_ref, x_ref, res_hbm, *refs):
+        outs, (flux_ref, coeffs_ref, basis_ref, m_ref, res_ref, tau_ref, sems) = refs[:2 * PARTS], refs[2 * PARTS:]
+        loads = [pltpu.make_async_copy(source, target, sems.at[n]) for n, (source, target) in enumerate(
+            ((flux_hbm, flux_ref), (coeffs_hbm, coeffs_ref), (basis_hbm, basis_ref), (m_hbm, m_ref)))]
+        for copy in loads:
+            copy.start()
         w = lax.axis_index("wave")
         core = w % 2
         first = (w * pixels).astype(jnp.float32)
-        wing_row = wing_ref[...].astype(jnp.float32)
-
-        def read(ref):
-            centre, line, column = (ref[n * absorbers:(n + 1) * absorbers, :] for n in range(3))
-            power = jnp.zeros_like(column)
-            width = jnp.zeros_like(column)
-            for n in range(strength_ref.shape[0]):
-                hit = line == float(n)
-                power = jnp.where(hit, strength_ref[n], power)
-                width = jnp.where(hit, widths_ref[n], width)
-            return centre, 0.5 * (column * power), 1.0 / width
-
-        def depth(params, start, count):
-            centre, amplitude, inverse = params
+        wing_row = own_ref[3 * absorbers:3 * absorbers + 1, :]
+
+        def depth(ref, start, count):
             at = lax.broadcasted_iota(jnp.int32, (count, spectra), 0).astype(jnp.float32) + start
             total = None
             for a in range(absorbers):
-                one = slice(a, a + 1)
-                term = bell(at - centre[one], amplitude[one], inverse[one], wing_row)
+                centre, amplitude, inverse = (ref[n * absorbers + a:n * absorbers + a + 1, :] for n in range(3))
+                term = bell(at - centre, amplitude, inverse, wing_row)
                 total = term if total is None else total + term
             return total
 
-        mine = read(own_ref)
-
         def chunk(n, _):
             row = pl.multiple_of(n * CHUNK, CHUNK)
-            tau_ref[pl.ds(row, CHUNK), :] = depth(mine, first + row.astype(jnp.float32), CHUNK)
+            tau_ref[pl.ds(row, CHUNK), :] = depth(own_ref, first + row.astype(jnp.float32), CHUNK)
             return 0
 
         lax.fori_loop(0, pixels // CHUNK, chunk, 0)
         for ref, before in ((core_ref, core == 1), (x_ref, core == 0)):
             row = pl.multiple_of(jnp.where(before, 0, pixels - WING), WING)
-            tau_ref[pl.ds(row, WING), :] += depth(read(ref), first + row.astype(jnp.float32), WING)
+            tau_ref[pl.ds(row, WING), :] += depth(ref, first + row.astype(jnp.float32), WING)
+        for copy in loads[:3]:
+            copy.wait()
         for n in range(pixels // T):
             lanes = slice(n * T, (n + 1) * T)
             seen = jnp.exp(-tau_ref[lanes, :].T)
             continuum = lax.dot_general(coeffs_ref[...], basis_ref[:, lanes], (((0,), (0,)), ((), ())),
                                         preferred_element_type=jnp.float32)
             res_ref[:, lanes] = (flux_ref[:, lanes].astype(jnp.float32) - continuum * seen).astype(jnp.bfloat16)
-        out_ref[...] = jnp.dot(res_ref[...], m_ref[...], preferred_element_type=jnp.float32)
-        keep_ref[...] = out_ref[pl.ds(pl.multiple_of(core * half, half), half), :]
-        send_ref[...] = out_ref[pl.ds(pl.multiple_of((1 - core) * half, half), half), :]
-
-    k = sketch_matrix.shape[1]
-    smem, vmem = pl.BlockSpec(memory_space=pltpu.SMEM), pl.BlockSpec(memory_space=pltpu.VMEM)
-    rows = jax.ShapeDtypeStruct((half, k), jnp.float32)
-    return pl.pallas_call(
-        body, name="front", in_specs=[smem] * 2 + [vmem] * 8, out_specs=[vmem] * 3,
-        out_shape=(jax.ShapeDtypeStruct(flux.shape, jnp.bfloat16), rows, rows),
-        scratch_shapes=[pltpu.VMEM((pixels, spectra), jnp.float32), pltpu.VMEM((spectra, k), jnp.float32)],
-        compiler_params=pltpu.CompilerParams(vmem_limit_bytes=32 << 20),
-    )(strength, widths, flux, coeffs_t, basis, own, over_core, over_x, wing, sketch_matrix)
+        store = pltpu.make_async_copy(res_ref, res_hbm, sems.at[4])
+        store.start()
+        loads[3].wait()
+        for n, out in enumerate(outs):
+            side = core if n < PARTS else 1 - core
+            row = pl.multiple_of(side * (spectra // 2) + (n % PARTS) * part, part)
+            out[...] = jnp.dot(res_ref[pl.ds(row, part), :], m_ref[...], preferred_element_type=jnp.float32)
+        store.wait()
+
+    rows = jax.ShapeDtypeStruct((part, k), jnp.float32)
+    outs = pl.pallas_call(
+        body, name="front", in_specs=[HBM] * 4 + [VMEM] * 3, out_specs=[HBM] + [VMEM] * (2 * PARTS),
+        out_shape=[jax.ShapeDtypeStruct(flux.shape, jnp.bfloat16)] + [rows] * (2 * PARTS),
+        scratch_shapes=[pltpu.VMEM(a.shape, a.dtype) for a in (flux, coeffs_t, basis, sketch_matrix, flux)]
+        + [pltpu.VMEM((pixels, spectra), jnp.float32), pltpu.SemaphoreType.DMA((5,))],
+        compiler_params=pltpu.CompilerParams(vmem_limit_bytes=107 << 19),
+    )(flux, coeffs_t, basis, sketch_matrix, own, over_core, over_x)
+    return outs[0], outs[1:1 + PARTS], outs[1 + PARTS:]
 
 
 def shards(
@@ -281,14 +323,12 @@
     sketch_matrix,
 ):
     waves = lax.axis_size("wave")
-    own = jnp.concatenate(
-        [centres.T.astype(jnp.float32), line_index.T.astype(jnp.float32), column_factor.T], axis=0)
+    own = line_table(centres.T, line_index.T, column_factor.T, wing_width[None, :], line_strength, line_widths)
     across = [(i, (i + 1 if i % 2 else i - 1) % waves) for i in range(waves)]
     over_x = lax.ppermute(own, "wave", across)
     over_core = swap(own, "wave", 1)
     residual, keep, send = front(
-        observed_flux, continuum_coeffs.T, continuum_basis, own, over_core, over_x,
-        wing_width[None, :], line_strength, line_widths, sketch_matrix)
+        observed_flux, continuum_coeffs.T, continuum_basis, own, over_core, over_x, sketch_matrix)
     return (residual, reduce_and_factor(keep, send, observed_flux.shape[0] * lax.axis_size("spec")))
 
 

time: 65.5 us -> 64.1 us (0.979)
  local copies, waits for them, and re-layouts: 3.36 us -> 0.73 us
  Pallas kernels: 19.7 us -> 21.4 us
  other arithmetic: 0.81 us -> 0.1 us
    unnamed x16 -> x6, local copies, waits for them, and re-layouts: 3.36 us -> 0.73 us
    pallas_call x1 -> x2, Pallas kernels: 2.74 us -> 4.38 us  [the longest x1 2.88 us: front(): pl.pallas_call(body, name='front', in_specs=[HBM] * 4 + [VMEM] * 3, out_s...]
    convert_element_type x1 -> x0, other arithmetic: 0.71 us -> none  [shards(): line_index.T.astype(jnp.float32)]
    ppermute x14 -> x16, starting transfers between devices: 15.7 us -> 16 us  [swap(): lax.ppermute(x, axis, [(i, i ^ bit) for i in range(lax.axis_size(axis))])]
    ppermute x14 -> x16, waiting for transfers between devices: 21.8 us -> 21.6 us  [swap(): lax.ppermute(x, axis, [(i, i ^ bit) for i in range(lax.axis_size(axis))])]
  transfers between devices with their start and end apart: 15 -> 17, of which waited for: 11 -> 12; matrix products, arithmetic and copies ran while one was open for 0% -> 0% of each run, Pallas kernels for 0% -> 0%
where the time goes in v4:
time: 64.1 us; the launch traced here: 63.9 us
  waiting for transfers between devices  22.5 us (35%)
  Pallas kernels  21.4 us (33%)
  starting transfers between devices  18.4 us (29%)
  between operations  0.74 us (1%)
  local copies, waits for them, and re-layouts  0.73 us (1%)
    ppermute x16, waiting for transfers between devices, swap(): lax.ppermute(x, axis, [(i, i ^ bit) for i in range(lax.axis_size(axis))])  21.6 us
    pallas_call x1, Pallas kernels, factor(): pl.pallas_call(body, name='factor', out_shape=jax.ShapeDtypeStruct((n, n)...  16.4 us
    ppermute x16, starting transfers between devices, swap(): lax.ppermute(x, axis, [(i, i ^ bit) for i in range(lax.axis_size(axis))])  16 us
    pallas_call x1, Pallas kernels, front(): pl.pallas_call(body, name='front', in_specs=[HBM] * 4 + [VMEM] * 3, out_s...  2.88 us
    ppermute x1, starting transfers between devices, shards(): over_x = lax.ppermute(own, 'wave', across)  2.44 us
    pallas_call x1, Pallas kernels, line_table(): pl.pallas_call(body, name='lines', in_specs=[HBM] * 6, out_specs=VMEM, ou...  1.5 us
  transfers between devices with their start and end apart: 17, of which 12 were waited for; matrix products, arithmetic and copies ran while one was open for 0% of the time, Pallas kernels for 0%

profile of v4, /device:TPU:0, one launch (start us, length us, event | category | flops | bytes accessed | tf_op | source)
XLA Modules:
  0.0 63.9 jit_solution(9087458163025384377)
XLA Ops:
  0.6 0.0 copy-start.1
  0.6 0.0 copy-start.2
  0.7 1.5 %lines.1.own_ref = f32[16,256]{1,0:T(8,128)} custom-call(s32[4,256]{1,0:T(4,128)} %bitcast.6, s32[4,256]{1,0:T(4,128)} %bitcast.7, f32[4,256]{1,0:T(4,128)} %bitcast.8, s32[1,256]{1,0:T(1,128)} %bitcast.9, f32[32]{0:T(128)} %strength_ref.1, f32[32]{0:T(128)} %widths_ref.1), custom_call_target="tpu_custom_call" | custom-call | tf_op jit(solution)/shard_map/lines/pallas_call | solution.py:240
  2.2 2.4 %collective-permute-start.1 = (f32[16,256]{1,0:T(8,128)}, f32[16,256]{1,0:T(8,128)S(1)}, u32[]{:S(2)}, u32[]{:S(2)}) collective-permute-start(f32[16,256]{1,0:T(8,128)} %lines.1.own_ref), channel_id=1, source_target_pairs={{0,3},{1,2},{2,1},{3,0},{4,7},{5,6},{6,5},{7,4},{8,11},{9,10},{10,... | collective-permute-start | bytes 49160 | tf_op jit(solution)/shard_map/ppermute | solution.py:328
  4.6 0.7 %collective-permute-start = (f32[16,256]{1,0:T(8,128)}, f32[16,256]{1,0:T(8,128)S(1)}, u32[]{:S(2)}, u32[]{:S(2)}) collective-permute-start(f32[16,256]{1,0:T(8,128)} %lines.1.own_ref), channel_id=1, source_target_pairs={{0,1},{1,0},{2,3},{3,2},{4,5},{5,4},{6,7},{7,6},{8,9},{9,8},{10,11... | collective-permute-start | bytes 49160 | tf_op jit(solution)/shard_map/ppermute | solution.py:159
  5.3 1.0 %collective-permute-done.1.x_ref = f32[16,256]{1,0:T(8,128)S(1)} collective-permute-done((f32[16,256]{1,0:T(8,128)}, f32[16,256]{1,0:T(8,128)S(1)}, u32[]{:S(2)}, u32[]{:S(2)}) %collective-permute-start.1) | collective-permute-done | bytes 16416 | tf_op jit(solution)/shard_map/ppermute | solution.py:328
  6.3 0.1 collective-permute-done.core_ref
  6.3 0.0 copy-done.1
  6.3 0.0 copy-done.2
  6.3 0.0 copy-start
  6.3 0.7 %copy-done = f32[16,256]{1,0:T(8,128)S(1)} copy-done((f32[16,256]{1,0:T(8,128)S(1)}, f32[16,256]{1,0:T(8,128)}, u32[]{:S(2)}) %copy-start) | copy-done | bytes 16408
  7.1 2.9 %front.1 = (bf16[256,512]{1,0:T(8,128)(2,1)}, f32[64,512]{1,0:T(8,128)S(1)}, f32[64,512]{1,0:T(8,128)S(1)}, f32[64,512]{1,0:T(8,128)}, f32[64,512]{1,0:T(8,128)}) custom-call(bf16[256,512]{1,0:T(8,128)(2,1)} %flux_hbm.1, bf16[16,256]{1,0:T(8,128)(2,1)S(1)} %bitcast.5, bf16[16,512]{1,0:T(8,128)(2,1)S(1)} %copy-done.1, bf16[512,512]{1,0:T(8,128)(2,1)} %m_hbm.1, ...), custom_call_target="tpu_custom_call" | custom-call | tf_op jit(solution)/shard_map/front/pallas_call | solution.py:303
  9.9 0.7 %collective-permute-start.2 = (f32[64,512]{1,0:T(8,128)}, f32[64,512]{1,0:T(8,128)S(1)}, u32[]{:S(2)}, u32[]{:S(2)}) collective-permute-start(f32[64,512]{1,0:T(8,128)} %get-tuple-element.11), channel_id=1, source_target_pairs={{0,1},{1,0},{2,3},{3,2},{4,5},{5,4},{6,7},{7,6},{8,9},{9,8},{10,11... | collective-permute-start | bytes 393224 | tf_op jit(solution)/shard_map/ppermute | solution.py:159
  10.6 0.1 collective-permute-start.3
  10.7 1.1 %collective-permute-done.2 = f32[64,512]{1,0:T(8,128)S(1)} collective-permute-done((f32[64,512]{1,0:T(8,128)}, f32[64,512]{1,0:T(8,128)S(1)}, u32[]{:S(2)}, u32[]{:S(2)}) %collective-permute-start.2) | collective-permute-done | bytes 131104 | tf_op jit(solution)/shard_map/ppermute | solution.py:159
  11.8 2.2 %collective-permute-start.4 = (f32[64,512]{1,0:T(8,128)S(1)}, f32[64,512]{1,0:T(8,128)S(1)}, u32[]{:S(2)}, u32[]{:S(2)}) collective-permute-start(f32[64,512]{1,0:T(8,128)S(1)} %add.33.refs_0_), channel_id=1, source_target_pairs={{0,2},{1,3},{2,0},{3,1},{4,6},{5,7},{6,4},{7,5},{8,10},{9,11},{10,... | collective-permute-start | bytes 393224 | tf_op jit(solution)/shard_map/ppermute | solution.py:159
  14.0 0.0 collective-permute-done.3
  14.1 0.2 collective-permute-start.5
  14.2 4.1 %collective-permute-done.4.refs_2_ = f32[64,512]{1,0:T(8,128)S(1)} collective-permute-done((f32[64,512]{1,0:T(8,128)S(1)}, f32[64,512]{1,0:T(8,128)S(1)}, u32[]{:S(2)}, u32[]{:S(2)}) %collective-permute-start.4) | collective-permute-done | bytes 131104 | tf_op jit(solution)/shard_map/ppermute | solution.py:159
  18.3 2.3 %collective-permute-done.5.refs_3_ = f32[64,512]{1,0:T(8,128)S(1)} collective-permute-done((f32[64,512]{1,0:T(8,128)S(1)}, f32[64,512]{1,0:T(8,128)S(1)}, u32[]{:S(2)}, u32[]{:S(2)}) %collective-permute-start.5) | collective-permute-done | bytes 131104 | tf_op jit(solution)/shard_map/ppermute | solution.py:159
  20.6 0.5 gram.1
  21.2 0.1 collective-permute-start.6
  21.3 1.4 %collective-permute-done.6 = f32[5,64,128]{2,1,0:T(8,128)S(1)} collective-permute-done((f32[5,64,128]{2,1,0:T(8,128)S(1)}, f32[5,64,128]{2,1,0:T(8,128)S(1)}, u32[]{:S(2)}, u32[]{:S(2)}) %collective-permute-start.6) | collective-permute-done | bytes 163872 | tf_op jit(solution)/shard_map/ppermute | solution.py:159
  22.7 1.8 %collective-permute-start.7 = (f32[5,32,128]{2,1,0:T(8,128)S(1)}, f32[5,32,128]{2,1,0:T(8,128)S(1)}, u32[]{:S(2)}, u32[]{:S(2)}) collective-permute-start(f32[5,32,128]{2,1,0:T(8,128)S(1)} %dynamic-slice_add_fusion), channel_id=1, source_target_pairs={{0,4},{4,0},{8,12},{12,8},{16,20},{20,16},{24,28},{28,24},{1,5},{5... | collective-permute-start | bytes 245768 | tf_op jit(solution)/shard_map/ppermute | solution.py:159
  24.5 2.8 %collective-permute-done.7 = f32[5,32,128]{2,1,0:T(8,128)S(1)} collective-permute-done((f32[5,32,128]{2,1,0:T(8,128)S(1)}, f32[5,32,128]{2,1,0:T(8,128)S(1)}, u32[]{:S(2)}, u32[]{:S(2)}) %collective-permute-start.7) | collective-permute-done | bytes 81952 | tf_op jit(solution)/shard_map/ppermute | solution.py:159
  27.2 1.9 %collective-permute-start.8 = (f32[5,32,128]{2,1,0:T(8,128)S(1)}, f32[5,32,128]{2,1,0:T(8,128)S(1)}, u32[]{:S(2)}, u32[]{:S(2)}) collective-permute-start(f32[5,32,128]{2,1,0:T(8,128)S(1)} %add_add_fusion), channel_id=1, source_target_pairs={{0,8},{4,12},{8,0},{12,4},{16,24},{20,28},{24,16},{28,20},{1,9},{5... | collective-permute-start | bytes 245768 | tf_op jit(solution)/shard_map/ppermute | solution.py:159
  29.1 2.6 %collective-permute-done.8 = f32[5,32,128]{2,1,0:T(8,128)S(1)} collective-permute-done((f32[5,32,128]{2,1,0:T(8,128)S(1)}, f32[5,32,128]{2,1,0:T(8,128)S(1)}, u32[]{:S(2)}, u32[]{:S(2)}) %collective-permute-start.8) | collective-permute-done | bytes 81952 | tf_op jit(solution)/shard_map/ppermute | solution.py:159
  31.8 2.9 %collective-permute-start.9 = (f32[5,32,128]{2,1,0:T(8,128)S(1)}, f32[5,32,128]{2,1,0:T(8,128)S(1)}, u32[]{:S(2)}, u32[]{:S(2)}) collective-permute-start(f32[5,32,128]{2,1,0:T(8,128)S(1)} %add.41), channel_id=1, source_target_pairs={{0,16},{4,20},{8,24},{12,28},{16,0},{20,4},{24,8},{28,12},{1,17},{... | collective-permute-start | bytes 245768 | tf_op jit(solution)/shard_map/ppermute | solution.py:159
  34.6 2.5 %collective-permute-done.9 = f32[5,32,128]{2,1,0:T(8,128)S(1)} collective-permute-done((f32[5,32,128]{2,1,0:T(8,128)S(1)}, f32[5,32,128]{2,1,0:T(8,128)S(1)}, u32[]{:S(2)}, u32[]{:S(2)}) %collective-permute-start.9) | collective-permute-done | bytes 81952 | tf_op jit(solution)/shard_map/ppermute | solution.py:159
  37.2 1.8 %collective-permute-start.10 = (f32[5,32,128]{2,1,0:T(8,128)S(1)}, f32[5,32,128]{2,1,0:T(8,128)S(1)}, u32[]{:S(2)}, u32[]{:S(2)}) collective-permute-start(f32[5,32,128]{2,1,0:T(8,128)S(1)} %add.42.refs_0_), channel_id=1, source_target_pairs={{0,4},{4,0},{8,12},{12,8},{16,20},{20,16},{24,28},{28,24},{1,5},{5... | collective-permute-start | bytes 245768 | tf_op jit(solution)/shard_map/ppermute | solution.py:159
  39.0 1.5 %collective-permute-start.11 = (f32[5,32,128]{2,1,0:T(8,128)S(1)}, f32[5,32,128]{2,1,0:T(8,128)S(1)}, u32[]{:S(2)}, u32[]{:S(2)}) collective-permute-start(f32[5,32,128]{2,1,0:T(8,128)S(1)} %add.42.refs_0_), channel_id=1, source_target_pairs={{0,2},{1,3},{2,0},{3,1},{4,6},{5,7},{6,4},{7,5},{8,10},{9,11},{10,... | collective-permute-start | bytes 245768 | tf_op jit(solution)/shard_map/ppermute | solution.py:159
  40.5 1.2 %collective-permute-done.10.refs_1_ = f32[5,32,128]{2,1,0:T(8,128)S(1)} collective-permute-done((f32[5,32,128]{2,1,0:T(8,128)S(1)}, f32[5,32,128]{2,1,0:T(8,128)S(1)}, u32[]{:S(2)}, u32[]{:S(2)}) %collective-permute-start.10) | collective-permute-done | bytes 81952 | tf_op jit(solution)/shard_map/ppermute | solution.py:159
  41.7 1.7 %collective-permute-start.12 = (f32[5,32,128]{2,1,0:T(8,128)S(1)}, f32[5,32,128]{2,1,0:T(8,128)S(1)}, u32[]{:S(2)}, u32[]{:S(2)}) collective-permute-start(f32[5,32,128]{2,1,0:T(8,128)S(1)} %collective-permute-done.10.refs_1_), channel_id=1, source_target_pairs={{0,2},{1,3},{2,0},{3,1},{4,6},{5,7},{6,4},{7,5},{8,10},{9,11},{10,... | collective-permute-start | bytes 245768 | tf_op jit(solution)/shard_map/ppermute | solution.py:159
  43.4 0.0 collective-permute-start.13
  43.4 0.5 collective-permute-start.14
  44.0 0.0 collective-permute-done.11.refs_2_
  44.0 0.0 collective-permute-start.15
  44.0 2.2 %collective-permute-done.12.refs_3_ = f32[5,32,128]{2,1,0:T(8,128)S(1)} collective-permute-done((f32[5,32,128]{2,1,0:T(8,128)S(1)}, f32[5,32,128]{2,1,0:T(8,128)S(1)}, u32[]{:S(2)}, u32[]{:S(2)}) %collective-permute-start.12) | collective-permute-done | bytes 81952 | tf_op jit(solution)/shard_map/ppermute | solution.py:159
  46.1 0.0 collective-permute-start.16
  46.1 0.0 collective-permute-done.13.refs_4_
  46.1 0.0 collective-permute-done.15.refs_6_
  46.2 0.0 collective-permute-done.14.refs_5_
  46.2 1.3 %collective-permute-done.16.refs_7_ = f32[5,32,128]{2,1,0:T(8,128)S(1)} collective-permute-done((f32[5,32,128]{2,1,0:T(8,128)S(1)}, f32[5,32,128]{2,1,0:T(8,128)S(1)}, u32[]{:S(2)}, u32[]{:S(2)}) %collective-permute-start.16) | collective-permute-done | bytes 81952 | tf_op jit(solution)/shard_map/ppermute | solution.py:159
  47.4 16.4 %factor.1 = f32[512,512]{1,0:T(8,128)} custom-call(f32[5,32,128]{2,1,0:T(8,128)S(1)} %add.42.refs_0_, f32[5,32,128]{2,1,0:T(8,128)S(1)} %collective-permute-done.10.refs_1_, f32[5,32,128]{2,1,0:T(8,128)S(1)} %collective-permute-done.11.refs_2_, f32[5,32,128]{2,1,0:T(8,128)S(1)} %collective-permute-done.12.refs_3_, ...), custom_call_target="tpu_custom_call" | custom-call | tf_op jit(solution)/shard_map/factor/pallas_call | solution.py:150
  (6 shorter events, 0.1 us)
Async XLA Ops:
  0.6 5.7 %copy-start.1 = (bf16[16,512]{1,0:T(8,128)(2,1)S(1)}, bf16[16,512]{1,0:T(8,128)(2,1)}, u32[]{:S(2)}) copy-start(bf16[16,512]{1,0:T(8,128)(2,1)} %basis_hbm.1) | copy-start | bytes 49156
  0.6 5.7 %copy-start.2 = (bf16[256,16]{0,1:T(8,128)(2,1)S(1)}, bf16[256,16]{0,1:T(8,128)(2,1)}, u32[]{:S(2)}) copy-start(bf16[256,16]{0,1:T(8,128)(2,1)} %param.11) | copy-start | bytes 24580
  2.2 4.1 %collective-permute-start.1 = (f32[16,256]{1,0:T(8,128)}, f32[16,256]{1,0:T(8,128)S(1)}, u32[]{:S(2)}, u32[]{:S(2)}) collective-permute-start(f32[16,256]{1,0:T(8,128)} %lines.1.own_ref), channel_id=1, source_target_pairs={{0,3},{1,2},{2,1},{3,0},{4,7},{5,6},{6,5},{7,4},{8,11},{9,10},{10,... | collective-permute-start | bytes 49160 | tf_op jit(solution)/shard_map/ppermute | solution.py:328
  4.6 1.7 %collective-permute-start = (f32[16,256]{1,0:T(8,128)}, f32[16,256]{1,0:T(8,128)S(1)}, u32[]{:S(2)}, u32[]{:S(2)}) collective-permute-start(f32[16,256]{1,0:T(8,128)} %lines.1.own_ref), channel_id=1, source_target_pairs={{0,1},{1,0},{2,3},{3,2},{4,5},{5,4},{6,7},{7,6},{8,9},{9,8},{10,11... | collective-permute-start | bytes 49160 | tf_op jit(solution)/shard_map/ppermute | solution.py:159
  6.3 0.7 %copy-start = (f32[16,256]{1,0:T(8,128)S(1)}, f32[16,256]{1,0:T(8,128)}, u32[]{:S(2)}) copy-start(f32[16,256]{1,0:T(8,128)} %lines.1.own_ref) | copy-start | bytes 49156
  9.9 1.9 %collective-permute-start.2 = (f32[64,512]{1,0:T(8,128)}, f32[64,512]{1,0:T(8,128)S(1)}, u32[]{:S(2)}, u32[]{:S(2)}) collective-permute-start(f32[64,512]{1,0:T(8,128)} %get-tuple-element.11), channel_id=1, source_target_pairs={{0,1},{1,0},{2,3},{3,2},{4,5},{5,4},{6,7},{7,6},{8,9},{9,8},{10,11... | collective-permute-start | bytes 393224 | tf_op jit(solution)/shard_map/ppermute | solution.py:159
  10.6 3.4 %collective-permute-start.3 = (f32[64,512]{1,0:T(8,128)}, f32[64,512]{1,0:T(8,128)S(1)}, u32[]{:S(2)}, u32[]{:S(2)}) collective-permute-start(f32[64,512]{1,0:T(8,128)} %get-tuple-element.13), channel_id=1, source_target_pairs={{0,1},{1,0},{2,3},{3,2},{4,5},{5,4},{6,7},{7,6},{8,9},{9,8},{10,11... | collective-permute-start | bytes 393224 | tf_op jit(solution)/shard_map/ppermute | solution.py:159
  11.8 6.5 %collective-permute-start.4 = (f32[64,512]{1,0:T(8,128)S(1)}, f32[64,512]{1,0:T(8,128)S(1)}, u32[]{:S(2)}, u32[]{:S(2)}) collective-permute-start(f32[64,512]{1,0:T(8,128)S(1)} %add.33.refs_0_), channel_id=1, source_target_pairs={{0,2},{1,3},{2,0},{3,1},{4,6},{5,7},{6,4},{7,5},{8,10},{9,11},{10,... | collective-permute-start | bytes 393224 | tf_op jit(solution)/shard_map/ppermute | solution.py:159
  14.1 6.6 %collective-permute-start.5 = (f32[64,512]{1,0:T(8,128)S(1)}, f32[64,512]{1,0:T(8,128)S(1)}, u32[]{:S(2)}, u32[]{:S(2)}) collective-permute-start(f32[64,512]{1,0:T(8,128)S(1)} %add.34.refs_1_), channel_id=1, source_target_pairs={{0,2},{1,3},{2,0},{3,1},{4,6},{5,7},{6,4},{7,5},{8,10},{9,11},{10,... | collective-permute-start | bytes 393224 | tf_op jit(solution)/shard_map/ppermute | solution.py:159
  21.2 1.5 %collective-permute-start.6 = (f32[5,64,128]{2,1,0:T(8,128)S(1)}, f32[5,64,128]{2,1,0:T(8,128)S(1)}, u32[]{:S(2)}, u32[]{:S(2)}) collective-permute-start(f32[5,64,128]{2,1,0:T(8,128)S(1)} %get-tuple-element.15), channel_id=1, source_target_pairs={{0,1},{1,0},{2,3},{3,2},{4,5},{5,4},{6,7},{7,6},{8,9},{9,8},{10,11... | collective-permute-start | bytes 491528 | tf_op jit(solution)/shard_map/ppermute | solution.py:159
  22.7 4.6 %collective-permute-start.7 = (f32[5,32,128]{2,1,0:T(8,128)S(1)}, f32[5,32,128]{2,1,0:T(8,128)S(1)}, u32[]{:S(2)}, u32[]{:S(2)}) collective-permute-start(f32[5,32,128]{2,1,0:T(8,128)S(1)} %dynamic-slice_add_fusion), channel_id=1, source_target_pairs={{0,4},{4,0},{8,12},{12,8},{16,20},{20,16},{24,28},{28,24},{1,5},{5... | collective-permute-start | bytes 245768 | tf_op jit(solution)/shard_map/ppermute | solution.py:159
  27.2 4.5 %collective-permute-start.8 = (f32[5,32,128]{2,1,0:T(8,128)S(1)}, f32[5,32,128]{2,1,0:T(8,128)S(1)}, u32[]{:S(2)}, u32[]{:S(2)}) collective-permute-start(f32[5,32,128]{2,1,0:T(8,128)S(1)} %add_add_fusion), channel_id=1, source_target_pairs={{0,8},{4,12},{8,0},{12,4},{16,24},{20,28},{24,16},{28,20},{1,9},{5... | collective-permute-start | bytes 245768 | tf_op jit(solution)/shard_map/ppermute | solution.py:159
  31.8 5.4 %collective-permute-start.9 = (f32[5,32,128]{2,1,0:T(8,128)S(1)}, f32[5,32,128]{2,1,0:T(8,128)S(1)}, u32[]{:S(2)}, u32[]{:S(2)}) collective-permute-start(f32[5,32,128]{2,1,0:T(8,128)S(1)} %add.41), channel_id=1, source_target_pairs={{0,16},{4,20},{8,24},{12,28},{16,0},{20,4},{24,8},{28,12},{1,17},{... | collective-permute-start | bytes 245768 | tf_op jit(solution)/shard_map/ppermute | solution.py:159
  37.2 4.5 %collective-permute-start.10 = (f32[5,32,128]{2,1,0:T(8,128)S(1)}, f32[5,32,128]{2,1,0:T(8,128)S(1)}, u32[]{:S(2)}, u32[]{:S(2)}) collective-permute-start(f32[5,32,128]{2,1,0:T(8,128)S(1)} %add.42.refs_0_), channel_id=1, source_target_pairs={{0,4},{4,0},{8,12},{12,8},{16,20},{20,16},{24,28},{28,24},{1,5},{5... | collective-permute-start | bytes 245768 | tf_op jit(solution)/shard_map/ppermute | solution.py:159
  39.0 5.0 %collective-permute-start.11 = (f32[5,32,128]{2,1,0:T(8,128)S(1)}, f32[5,32,128]{2,1,0:T(8,128)S(1)}, u32[]{:S(2)}, u32[]{:S(2)}) collective-permute-start(f32[5,32,128]{2,1,0:T(8,128)S(1)} %add.42.refs_0_), channel_id=1, source_target_pairs={{0,2},{1,3},{2,0},{3,1},{4,6},{5,7},{6,4},{7,5},{8,10},{9,11},{10,... | collective-permute-start | bytes 245768 | tf_op jit(solution)/shard_map/ppermute | solution.py:159
  41.7 4.4 %collective-permute-start.12 = (f32[5,32,128]{2,1,0:T(8,128)S(1)}, f32[5,32,128]{2,1,0:T(8,128)S(1)}, u32[]{:S(2)}, u32[]{:S(2)}) collective-permute-start(f32[5,32,128]{2,1,0:T(8,128)S(1)} %collective-permute-done.10.refs_1_), channel_id=1, source_target_pairs={{0,2},{1,3},{2,0},{3,1},{4,6},{5,7},{6,4},{7,5},{8,10},{9,11},{10,... | collective-permute-start | bytes 245768 | tf_op jit(solution)/shard_map/ppermute | solution.py:159
  43.4 2.7 %collective-permute-start.13 = (f32[5,32,128]{2,1,0:T(8,128)S(1)}, f32[5,32,128]{2,1,0:T(8,128)S(1)}, u32[]{:S(2)}, u32[]{:S(2)}) collective-permute-start(f32[5,32,128]{2,1,0:T(8,128)S(1)} %add.42.refs_0_), channel_id=1, source_target_pairs={{0,1},{1,0},{2,3},{3,2},{4,5},{5,4},{6,7},{7,6},{8,9},{9,8},{10,11... | collective-permute-start | bytes 245768 | tf_op jit(solution)/shard_map/ppermute | solution.py:159
  43.4 2.7 %collective-permute-start.14 = (f32[5,32,128]{2,1,0:T(8,128)S(1)}, f32[5,32,128]{2,1,0:T(8,128)S(1)}, u32[]{:S(2)}, u32[]{:S(2)}) collective-permute-start(f32[5,32,128]{2,1,0:T(8,128)S(1)} %collective-permute-done.10.refs_1_), channel_id=1, source_target_pairs={{0,1},{1,0},{2,3},{3,2},{4,5},{5,4},{6,7},{7,6},{8,9},{9,8},{10,11... | collective-permute-start | bytes 245768 | tf_op jit(solution)/shard_map/ppermute | solution.py:159
  44.0 2.2 %collective-permute-start.15 = (f32[5,32,128]{2,1,0:T(8,128)S(1)}, f32[5,32,128]{2,1,0:T(8,128)S(1)}, u32[]{:S(2)}, u32[]{:S(2)}) collective-permute-start(f32[5,32,128]{2,1,0:T(8,128)S(1)} %collective-permute-done.11.refs_2_), channel_id=1, source_target_pairs={{0,1},{1,0},{2,3},{3,2},{4,5},{5,4},{6,7},{7,6},{8,9},{9,8},{10,11... | collective-permute-start | bytes 245768 | tf_op jit(solution)/shard_map/ppermute | solution.py:159
  46.1 1.3 %collective-permute-start.16 = (f32[5,32,128]{2,1,0:T(8,128)S(1)}, f32[5,32,128]{2,1,0:T(8,128)S(1)}, u32[]{:S(2)}, u32[]{:S(2)}) collective-permute-start(f32[5,32,128]{2,1,0:T(8,128)S(1)} %collective-permute-done.12.refs_3_), channel_id=1, source_target_pairs={{0,1},{1,0},{2,3},{3,2},{4,5},{5,4},{6,7},{7,6},{8,9},{9,8},{10,11... | collective-permute-start | bytes 245768 | tf_op jit(solution)/shard_map/ppermute | solution.py:159

commit v5 on v4

--- a/solution.py
+++ b/solution.py
@@ -16,52 +16,79 @@
 def lanes_of(x, c):
     return jnp.broadcast_to(x[:, c:c + 1], x.shape)
 
-def factor_block(d_ref, rk_ref, x_ref):
+NEAR = 2
+
+def split3(x):
+    a = x.astype(jnp.bfloat16)
+    r = x - a.astype(jnp.float32)
+    b = r.astype(jnp.bfloat16)
+    return a, b, (r - b.astype(jnp.float32)).astype(jnp.bfloat16)
+
+def outer(x, y):
+    x1, x2, x3 = split3(x)
+    y1, y2, y3 = split3(y)
+    left = jnp.concatenate([x1, x1, x2, x1, x2, x3], axis=0)
+    right = jnp.concatenate([y1, y2, y1, y3, y2, y1], axis=0)
+    return lax.dot_general(left, right, (((0,), (0,)), ((), ())), preferred_element_type=jnp.float32)
+
+def factor_block(d_ref, x_ref):
     steps = T // S
     sub = lax.broadcasted_iota(jnp.int32, (S, T), 0)
     lane = lax.broadcasted_iota(jnp.int32, (S, T), 1)
     at = [sub == k for k in range(S)]
     D = [d_ref[S * g:S * g + S, 0:T] for g in range(steps)]
-    E = [jnp.where(lane == sub + S * g, 1.0, 0.0).astype(jnp.float32) for g in range(steps)]
     C = [lanes_of(D[0], k) for k in range(S)]
+    later = None
     for s in range(steps):
-        Z = [rows_of(D[s], k) for k in range(S)]
-        Y = [rows_of(E[s], k) for k in range(S)]
+        done = (lane >= S * s) & (lane < S * s + S)
+        rows = D[s]
+        start = jnp.where(done, jnp.where(lane == sub + S * s, 1.0, 0.0), rows)
+        W = [rows_of(start, k) for k in range(S)]
         B = Cn = None
         if s + 1 < steps:
             B = [lanes_of(D[s + 1], S * s + k) for k in range(S)]
+            first = list(B)
+            Ca = [None] * S
             Cn = [lanes_of(D[s + 1], S * (s + 1) + k) for k in range(S)]
         for k in range(S):
             d = rows_of(C[k], k)
             inv = 1.0 / d
-            rs = lax.rsqrt(d)
-            rk_ref[S * s + k:S * s + k + 1, :] = (Z[k] * rs)[0:1]
-            x_ref[S * s + k:S * s + k + 1, :] = (Y[k] * rs)[0:1]
-            Z[k] = Z[k] * inv
-            Y[k] = Y[k] * inv
+            x_ref[S * s + k:S * s + k + 1, :] = (W[k] * lax.rsqrt(d))[0:1]
             u = {}
             for c in range(k + 1, S):
                 u[c] = rows_of(C[c], k) * inv
                 C[c] = jnp.where(at[k], u[c], C[c] - C[k] * u[c])
-            for c in range(S):
-                if c != k:
-                    m = rows_of(C[k], c)
-                    Z[c] = Z[c] - m * Z[k]
-                    Y[c] = Y[c] - m * Y[k]
+                W[c] = W[c] - u[c] * W[k]
+            W[k] = W[k] * inv
+            for c in range(k):
+                W[c] = W[c] - rows_of(C[k], c) * W[k]
             if B is not None:
                 bi = B[k] * inv
                 for c in range(k + 1, S):
                     B[c] = B[c] - B[k] * u[c]
                 for c in range(S):
-                    Cn[c] = Cn[c] - bi * rows_of(B[k], c)
-        for g in range(s + 1, steps):
-            raw = [lanes_of(D[g], S * s + k) for k in range(S)]
-            dd, ee = D[g], E[g]
-            for k in range(S):
-                dd = dd - raw[k] * Z[k]
-                ee = ee - raw[k] * Y[k]
-            D[g], E[g] = dd, ee
-        C = Cn
+                    v = bi * rows_of(B[k], c)
+                    Ca[c] = v if k == 0 else Ca[c] + v
+        if later is not None:
+            for g, part in later:
+                D[g] = D[g] - part
+        for g in range(s + 1, min(s + 1 + NEAR, steps)):
+            raw = first if g == s + 1 else [lanes_of(D[g], S * s + k) for k in range(S)]
+            terms = [raw[k] * W[k] for k in range(S)]
+            while len(terms) > 1:
+                terms = [p + q for p, q in zip(terms[::2], terms[1::2])]
+            D[g] = jnp.where(done, 0.0, D[g]) - terms[0]
+        later = None
+        if s + 1 + NEAR < steps:
+            w = W[S - 1]
+            for k in range(S - 1):
+                w = jnp.where(at[k], W[k], w)
+            full = outer(rows, w)
+            later = []
+            for g in range(s + 1 + NEAR, steps):
+                D[g] = jnp.where(done, 0.0, D[g])
+                later.append((g, full[S * g:S * g + S, :]))
+        C = [p - q for p, q in zip(Cn, Ca)] if Cn is not None else None
 
 def upper_block(b, nb):
     i = jnp.int32(0)
@@ -110,7 +137,7 @@
     part = T // 4
 
     def body(*refs):
-        piece_refs, (r_ref, w_ref, rk_ref, x_ref) = refs[:len(pieces)], refs[len(pieces):]
+        piece_refs, (r_ref, w_ref, x_ref) = refs[:len(pieces)], refs[len(pieces):]
         w = lax.axis_index("wave")
         y = lax.axis_index("spec") % 2
         for ref, (dw, dy) in zip(piece_refs, offsets):
@@ -125,13 +152,14 @@
         col = lax.broadcasted_iota(jnp.int32, (T, T), 1)
 
         def step(b, _):
-            factor_block(w_ref, rk_ref, x_ref)
+            factor_block(w_ref, x_ref)
             base = pl.multiple_of(b * T, T)
-            r_ref[pl.ds(base, T), pl.ds(base, T)] = jnp.where(row <= col, rk_ref[...], 0.0)
+            x = jnp.where(row >= col, x_ref[...], 0.0)
+            diagonal = jnp.dot(x, w_ref[0:T, 0:T], precision=HI, preferred_element_type=jnp.float32)
+            r_ref[pl.ds(base, T), pl.ds(base, T)] = jnp.where(row <= col, diagonal, 0.0)
 
             @pl.when(b < nb - 1)
             def _():
-                x = jnp.where(row >= col, x_ref[...], 0.0)
                 panel = jnp.dot(x, w_ref[0:T, T:n], precision=HI, preferred_element_type=jnp.float32)
                 for t in range(nb - 1):
                     @pl.when(b + 1 + t < nb)
@@ -149,8 +177,7 @@
 
     return pl.pallas_call(
         body, name="factor", out_shape=jax.ShapeDtypeStruct((n, n), jnp.float32),
-        scratch_shapes=[pltpu.VMEM((n, n), jnp.float32), pltpu.VMEM((T, T), jnp.float32),
-                        pltpu.VMEM((T, T), jnp.float32)],
+        scratch_shapes=[pltpu.VMEM((n, n), jnp.float32), pltpu.VMEM((T, T), jnp.float32)],
         compiler_params=pltpu.CompilerParams(vmem_limit_bytes=32 << 20),
     )(*pieces)
 

time: 64.1 us -> 63 us (0.983)
  Pallas kernels: 21.4 us -> 20.2 us
    pallas_call x1, Pallas kernels: 16.4 us -> 15.3 us  [factor(): pl.pallas_call(body, name='factor', out_shape=jax.ShapeDtypeStruct((n, n)...]
where the time goes in v5:
time: 63 us; the launch traced here: 62.7 us
  waiting for transfers between devices  22.5 us (36%)
  Pallas kernels  20.2 us (32%)
  starting transfers between devices  18.4 us (29%)
  between operations  0.74 us (1%)
  local copies, waits for them, and re-layouts  0.73 us (1%)
    ppermute x16, waiting for transfers between devices, swap(): lax.ppermute(x, axis, [(i, i ^ bit) for i in range(lax.axis_size(axis))])  21.6 us
    ppermute x16, starting transfers between devices, swap(): lax.ppermute(x, axis, [(i, i ^ bit) for i in range(lax.axis_size(axis))])  16 us
    pallas_call x1, Pallas kernels, factor(): pl.pallas_call(body, name='factor', out_shape=jax.ShapeDtypeStruct((n, n)...  15.3 us
    pallas_call x1, Pallas kernels, front(): pl.pallas_call(body, name='front', in_specs=[HBM] * 4 + [VMEM] * 3, out_s...  2.88 us
    ppermute x1, starting transfers between devices, shards(): over_x = lax.ppermute(own, 'wave', across)  2.44 us
    pallas_call x1, Pallas kernels, line_table(): pl.pallas_call(body, name='lines', in_specs=[HBM] * 6, out_specs=VMEM, ou...  1.5 us
  transfers between devices with their start and end apart: 17, of which 12 were waited for; matrix products, arithmetic and copies ran while one was open for 0% of the time, Pallas kernels for 0%

profile of v5, /device:TPU:0, one launch (start us, length us, event | category | flops | bytes accessed | tf_op | source)
XLA Modules:
  0.0 62.7 jit_solution(2825723845337729890)
XLA Ops:
  0.6 0.0 copy-start.1
  0.6 0.0 copy-start.2
  0.7 1.5 %lines.1.own_ref = f32[16,256]{1,0:T(8,128)} custom-call(s32[4,256]{1,0:T(4,128)} %bitcast.6, s32[4,256]{1,0:T(4,128)} %bitcast.7, f32[4,256]{1,0:T(4,128)} %bitcast.8, s32[1,256]{1,0:T(1,128)} %bitcast.9, f32[32]{0:T(128)} %strength_ref.1, f32[32]{0:T(128)} %widths_ref.1), custom_call_target="tpu_custom_call" | custom-call | tf_op jit(solution)/shard_map/lines/pallas_call | solution.py:267
  2.2 2.4 %collective-permute-start.1 = (f32[16,256]{1,0:T(8,128)}, f32[16,256]{1,0:T(8,128)S(1)}, u32[]{:S(2)}, u32[]{:S(2)}) collective-permute-start(f32[16,256]{1,0:T(8,128)} %lines.1.own_ref), channel_id=1, source_target_pairs={{0,3},{1,2},{2,1},{3,0},{4,7},{5,6},{6,5},{7,4},{8,11},{9,10},{10,... | collective-permute-start | bytes 49160 | tf_op jit(solution)/shard_map/ppermute | solution.py:355
  4.6 0.7 %collective-permute-start = (f32[16,256]{1,0:T(8,128)}, f32[16,256]{1,0:T(8,128)S(1)}, u32[]{:S(2)}, u32[]{:S(2)}) collective-permute-start(f32[16,256]{1,0:T(8,128)} %lines.1.own_ref), channel_id=1, source_target_pairs={{0,1},{1,0},{2,3},{3,2},{4,5},{5,4},{6,7},{7,6},{8,9},{9,8},{10,11... | collective-permute-start | bytes 49160 | tf_op jit(solution)/shard_map/ppermute | solution.py:186
  5.3 1.0 %collective-permute-done.1.x_ref = f32[16,256]{1,0:T(8,128)S(1)} collective-permute-done((f32[16,256]{1,0:T(8,128)}, f32[16,256]{1,0:T(8,128)S(1)}, u32[]{:S(2)}, u32[]{:S(2)}) %collective-permute-start.1) | collective-permute-done | bytes 16416 | tf_op jit(solution)/shard_map/ppermute | solution.py:355
  6.3 0.1 collective-permute-done.core_ref
  6.3 0.0 copy-done.1
  6.3 0.0 copy-done.2
  6.3 0.0 copy-start
  6.3 0.7 %copy-done = f32[16,256]{1,0:T(8,128)S(1)} copy-done((f32[16,256]{1,0:T(8,128)S(1)}, f32[16,256]{1,0:T(8,128)}, u32[]{:S(2)}) %copy-start) | copy-done | bytes 16408
  7.1 2.9 %front.1 = (bf16[256,512]{1,0:T(8,128)(2,1)}, f32[64,512]{1,0:T(8,128)S(1)}, f32[64,512]{1,0:T(8,128)S(1)}, f32[64,512]{1,0:T(8,128)}, f32[64,512]{1,0:T(8,128)}) custom-call(bf16[256,512]{1,0:T(8,128)(2,1)} %flux_hbm.1, bf16[16,256]{1,0:T(8,128)(2,1)S(1)} %bitcast.5, bf16[16,512]{1,0:T(8,128)(2,1)S(1)} %copy-done.1, bf16[512,512]{1,0:T(8,128)(2,1)} %m_hbm.1, ...), custom_call_target="tpu_custom_call" | custom-call | tf_op jit(solution)/shard_map/front/pallas_call | solution.py:330
  9.9 0.7 %collective-permute-start.2 = (f32[64,512]{1,0:T(8,128)}, f32[64,512]{1,0:T(8,128)S(1)}, u32[]{:S(2)}, u32[]{:S(2)}) collective-permute-start(f32[64,512]{1,0:T(8,128)} %get-tuple-element.11), channel_id=1, source_target_pairs={{0,1},{1,0},{2,3},{3,2},{4,5},{5,4},{6,7},{7,6},{8,9},{9,8},{10,11... | collective-permute-start | bytes 393224 | tf_op jit(solution)/shard_map/ppermute | solution.py:186
  10.6 0.1 collective-permute-start.3
  10.7 1.1 %collective-permute-done.2 = f32[64,512]{1,0:T(8,128)S(1)} collective-permute-done((f32[64,512]{1,0:T(8,128)}, f32[64,512]{1,0:T(8,128)S(1)}, u32[]{:S(2)}, u32[]{:S(2)}) %collective-permute-start.2) | collective-permute-done | bytes 131104 | tf_op jit(solution)/shard_map/ppermute | solution.py:186
  11.8 2.2 %collective-permute-start.4 = (f32[64,512]{1,0:T(8,128)S(1)}, f32[64,512]{1,0:T(8,128)S(1)}, u32[]{:S(2)}, u32[]{:S(2)}) collective-permute-start(f32[64,512]{1,0:T(8,128)S(1)} %add.33.refs_0_), channel_id=1, source_target_pairs={{0,2},{1,3},{2,0},{3,1},{4,6},{5,7},{6,4},{7,5},{8,10},{9,11},{10,... | collective-permute-start | bytes 393224 | tf_op jit(solution)/shard_map/ppermute | solution.py:186
  14.0 0.0 collective-permute-done.3
  14.1 0.2 collective-permute-start.5
  14.2 4.1 %collective-permute-done.4.refs_2_ = f32[64,512]{1,0:T(8,128)S(1)} collective-permute-done((f32[64,512]{1,0:T(8,128)S(1)}, f32[64,512]{1,0:T(8,128)S(1)}, u32[]{:S(2)}, u32[]{:S(2)}) %collective-permute-start.4) | collective-permute-done | bytes 131104 | tf_op jit(solution)/shard_map/ppermute | solution.py:186
  18.3 2.3 %collective-permute-done.5.refs_3_ = f32[64,512]{1,0:T(8,128)S(1)} collective-permute-done((f32[64,512]{1,0:T(8,128)S(1)}, f32[64,512]{1,0:T(8,128)S(1)}, u32[]{:S(2)}, u32[]{:S(2)}) %collective-permute-start.5) | collective-permute-done | bytes 131104 | tf_op jit(solution)/shard_map/ppermute | solution.py:186
  20.6 0.5 gram.1
  21.2 0.1 collective-permute-start.6
  21.3 1.4 %collective-permute-done.6 = f32[5,64,128]{2,1,0:T(8,128)S(1)} collective-permute-done((f32[5,64,128]{2,1,0:T(8,128)S(1)}, f32[5,64,128]{2,1,0:T(8,128)S(1)}, u32[]{:S(2)}, u32[]{:S(2)}) %collective-permute-start.6) | collective-permute-done | bytes 163872 | tf_op jit(solution)/shard_map/ppermute | solution.py:186
  22.7 1.8 %collective-permute-start.7 = (f32[5,32,128]{2,1,0:T(8,128)S(1)}, f32[5,32,128]{2,1,0:T(8,128)S(1)}, u32[]{:S(2)}, u32[]{:S(2)}) collective-permute-start(f32[5,32,128]{2,1,0:T(8,128)S(1)} %dynamic-slice_add_fusion), channel_id=1, source_target_pairs={{0,4},{4,0},{8,12},{12,8},{16,20},{20,16},{24,28},{28,24},{1,5},{5... | collective-permute-start | bytes 245768 | tf_op jit(solution)/shard_map/ppermute | solution.py:186
  24.5 2.8 %collective-permute-done.7 = f32[5,32,128]{2,1,0:T(8,128)S(1)} collective-permute-done((f32[5,32,128]{2,1,0:T(8,128)S(1)}, f32[5,32,128]{2,1,0:T(8,128)S(1)}, u32[]{:S(2)}, u32[]{:S(2)}) %collective-permute-start.7) | collective-permute-done | bytes 81952 | tf_op jit(solution)/shard_map/ppermute | solution.py:186
  27.2 1.9 %collective-permute-start.8 = (f32[5,32,128]{2,1,0:T(8,128)S(1)}, f32[5,32,128]{2,1,0:T(8,128)S(1)}, u32[]{:S(2)}, u32[]{:S(2)}) collective-permute-start(f32[5,32,128]{2,1,0:T(8,128)S(1)} %add_add_fusion), channel_id=1, source_target_pairs={{0,8},{4,12},{8,0},{12,4},{16,24},{20,28},{24,16},{28,20},{1,9},{5... | collective-permute-start | bytes 245768 | tf_op jit(solution)/shard_map/ppermute | solution.py:186
  29.1 2.6 %collective-permute-done.8 = f32[5,32,128]{2,1,0:T(8,128)S(1)} collective-permute-done((f32[5,32,128]{2,1,0:T(8,128)S(1)}, f32[5,32,128]{2,1,0:T(8,128)S(1)}, u32[]{:S(2)}, u32[]{:S(2)}) %collective-permute-start.8) | collective-permute-done | bytes 81952 | tf_op jit(solution)/shard_map/ppermute | solution.py:186
  31.8 2.9 %collective-permute-start.9 = (f32[5,32,128]{2,1,0:T(8,128)S(1)}, f32[5,32,128]{2,1,0:T(8,128)S(1)}, u32[]{:S(2)}, u32[]{:S(2)}) collective-permute-start(f32[5,32,128]{2,1,0:T(8,128)S(1)} %add.41), channel_id=1, source_target_pairs={{0,16},{4,20},{8,24},{12,28},{16,0},{20,4},{24,8},{28,12},{1,17},{... | collective-permute-start | bytes 245768 | tf_op jit(solution)/shard_map/ppermute | solution.py:186
  34.6 2.5 %collective-permute-done.9 = f32[5,32,128]{2,1,0:T(8,128)S(1)} collective-permute-done((f32[5,32,128]{2,1,0:T(8,128)S(1)}, f32[5,32,128]{2,1,0:T(8,128)S(1)}, u32[]{:S(2)}, u32[]{:S(2)}) %collective-permute-start.9) | collective-permute-done | bytes 81952 | tf_op jit(solution)/shard_map/ppermute | solution.py:186
  37.2 1.8 %collective-permute-start.10 = (f32[5,32,128]{2,1,0:T(8,128)S(1)}, f32[5,32,128]{2,1,0:T(8,128)S(1)}, u32[]{:S(2)}, u32[]{:S(2)}) collective-permute-start(f32[5,32,128]{2,1,0:T(8,128)S(1)} %add.42.refs_0_), channel_id=1, source_target_pairs={{0,4},{4,0},{8,12},{12,8},{16,20},{20,16},{24,28},{28,24},{1,5},{5... | collective-permute-start | bytes 245768 | tf_op jit(solution)/shard_map/ppermute | solution.py:186
  39.0 1.5 %collective-permute-start.11 = (f32[5,32,128]{2,1,0:T(8,128)S(1)}, f32[5,32,128]{2,1,0:T(8,128)S(1)}, u32[]{:S(2)}, u32[]{:S(2)}) collective-permute-start(f32[5,32,128]{2,1,0:T(8,128)S(1)} %add.42.refs_0_), channel_id=1, source_target_pairs={{0,2},{1,3},{2,0},{3,1},{4,6},{5,7},{6,4},{7,5},{8,10},{9,11},{10,... | collective-permute-start | bytes 245768 | tf_op jit(solution)/shard_map/ppermute | solution.py:186
  40.5 1.2 %collective-permute-done.10.refs_1_ = f32[5,32,128]{2,1,0:T(8,128)S(1)} collective-permute-done((f32[5,32,128]{2,1,0:T(8,128)S(1)}, f32[5,32,128]{2,1,0:T(8,128)S(1)}, u32[]{:S(2)}, u32[]{:S(2)}) %collective-permute-start.10) | collective-permute-done | bytes 81952 | tf_op jit(solution)/shard_map/ppermute | solution.py:186
  41.7 1.7 %collective-permute-start.12 = (f32[5,32,128]{2,1,0:T(8,128)S(1)}, f32[5,32,128]{2,1,0:T(8,128)S(1)}, u32[]{:S(2)}, u32[]{:S(2)}) collective-permute-start(f32[5,32,128]{2,1,0:T(8,128)S(1)} %collective-permute-done.10.refs_1_), channel_id=1, source_target_pairs={{0,2},{1,3},{2,0},{3,1},{4,6},{5,7},{6,4},{7,5},{8,10},{9,11},{10,... | collective-permute-start | bytes 245768 | tf_op jit(solution)/shard_map/ppermute | solution.py:186
  43.4 0.0 collective-permute-start.13
  43.4 0.5 collective-permute-start.14
  44.0 0.0 collective-permute-done.11.refs_2_
  44.0 0.0 collective-permute-start.15
  44.0 2.2 %collective-permute-done.12.refs_3_ = f32[5,32,128]{2,1,0:T(8,128)S(1)} collective-permute-done((f32[5,32,128]{2,1,0:T(8,128)S(1)}, f32[5,32,128]{2,1,0:T(8,128)S(1)}, u32[]{:S(2)}, u32[]{:S(2)}) %collective-permute-start.12) | collective-permute-done | bytes 81952 | tf_op jit(solution)/shard_map/ppermute | solution.py:186
  46.1 0.0 collective-permute-start.16
  46.1 0.0 collective-permute-done.13.refs_4_
  46.1 0.0 collective-permute-done.15.refs_6_
  46.2 0.0 collective-permute-done.14.refs_5_
  46.2 1.3 %collective-permute-done.16.refs_7_ = f32[5,32,128]{2,1,0:T(8,128)S(1)} collective-permute-done((f32[5,32,128]{2,1,0:T(8,128)S(1)}, f32[5,32,128]{2,1,0:T(8,128)S(1)}, u32[]{:S(2)}, u32[]{:S(2)}) %collective-permute-start.16) | collective-permute-done | bytes 81952 | tf_op jit(solution)/shard_map/ppermute | solution.py:186
  47.4 15.3 %factor.1 = f32[512,512]{1,0:T(8,128)} custom-call(f32[5,32,128]{2,1,0:T(8,128)S(1)} %add.42.refs_0_, f32[5,32,128]{2,1,0:T(8,128)S(1)} %collective-permute-done.10.refs_1_, f32[5,32,128]{2,1,0:T(8,128)S(1)} %collective-permute-done.11.refs_2_, f32[5,32,128]{2,1,0:T(8,128)S(1)} %collective-permute-done.12.refs_3_, ...), custom_call_target="tpu_custom_call" | custom-call | tf_op jit(solution)/shard_map/factor/pallas_call | solution.py:178
  (6 shorter events, 0.1 us)
Async XLA Ops:
  0.6 5.7 %copy-start.1 = (bf16[16,512]{1,0:T(8,128)(2,1)S(1)}, bf16[16,512]{1,0:T(8,128)(2,1)}, u32[]{:S(2)}) copy-start(bf16[16,512]{1,0:T(8,128)(2,1)} %basis_hbm.1) | copy-start | bytes 49156
  0.6 5.7 %copy-start.2 = (bf16[256,16]{0,1:T(8,128)(2,1)S(1)}, bf16[256,16]{0,1:T(8,128)(2,1)}, u32[]{:S(2)}) copy-start(bf16[256,16]{0,1:T(8,128)(2,1)} %param.11) | copy-start | bytes 24580
  2.2 4.1 %collective-permute-start.1 = (f32[16,256]{1,0:T(8,128)}, f32[16,256]{1,0:T(8,128)S(1)}, u32[]{:S(2)}, u32[]{:S(2)}) collective-permute-start(f32[16,256]{1,0:T(8,128)} %lines.1.own_ref), channel_id=1, source_target_pairs={{0,3},{1,2},{2,1},{3,0},{4,7},{5,6},{6,5},{7,4},{8,11},{9,10},{10,... | collective-permute-start | bytes 49160 | tf_op jit(solution)/shard_map/ppermute | solution.py:355
  4.6 1.7 %collective-permute-start = (f32[16,256]{1,0:T(8,128)}, f32[16,256]{1,0:T(8,128)S(1)}, u32[]{:S(2)}, u32[]{:S(2)}) collective-permute-start(f32[16,256]{1,0:T(8,128)} %lines.1.own_ref), channel_id=1, source_target_pairs={{0,1},{1,0},{2,3},{3,2},{4,5},{5,4},{6,7},{7,6},{8,9},{9,8},{10,11... | collective-permute-start | bytes 49160 | tf_op jit(solution)/shard_map/ppermute | solution.py:186
  6.3 0.7 %copy-start = (f32[16,256]{1,0:T(8,128)S(1)}, f32[16,256]{1,0:T(8,128)}, u32[]{:S(2)}) copy-start(f32[16,256]{1,0:T(8,128)} %lines.1.own_ref) | copy-start | bytes 49156
  9.9 1.9 %collective-permute-start.2 = (f32[64,512]{1,0:T(8,128)}, f32[64,512]{1,0:T(8,128)S(1)}, u32[]{:S(2)}, u32[]{:S(2)}) collective-permute-start(f32[64,512]{1,0:T(8,128)} %get-tuple-element.11), channel_id=1, source_target_pairs={{0,1},{1,0},{2,3},{3,2},{4,5},{5,4},{6,7},{7,6},{8,9},{9,8},{10,11... | collective-permute-start | bytes 393224 | tf_op jit(solution)/shard_map/ppermute | solution.py:186
  10.6 3.4 %collective-permute-start.3 = (f32[64,512]{1,0:T(8,128)}, f32[64,512]{1,0:T(8,128)S(1)}, u32[]{:S(2)}, u32[]{:S(2)}) collective-permute-start(f32[64,512]{1,0:T(8,128)} %get-tuple-element.13), channel_id=1, source_target_pairs={{0,1},{1,0},{2,3},{3,2},{4,5},{5,4},{6,7},{7,6},{8,9},{9,8},{10,11... | collective-permute-start | bytes 393224 | tf_op jit(solution)/shard_map/ppermute | solution.py:186
  11.8 6.5 %collective-permute-start.4 = (f32[64,512]{1,0:T(8,128)S(1)}, f32[64,512]{1,0:T(8,128)S(1)}, u32[]{:S(2)}, u32[]{:S(2)}) collective-permute-start(f32[64,512]{1,0:T(8,128)S(1)} %add.33.refs_0_), channel_id=1, source_target_pairs={{0,2},{1,3},{2,0},{3,1},{4,6},{5,7},{6,4},{7,5},{8,10},{9,11},{10,... | collective-permute-start | bytes 393224 | tf_op jit(solution)/shard_map/ppermute | solution.py:186
  14.1 6.6 %collective-permute-start.5 = (f32[64,512]{1,0:T(8,128)S(1)}, f32[64,512]{1,0:T(8,128)S(1)}, u32[]{:S(2)}, u32[]{:S(2)}) collective-permute-start(f32[64,512]{1,0:T(8,128)S(1)} %add.34.refs_1_), channel_id=1, source_target_pairs={{0,2},{1,3},{2,0},{3,1},{4,6},{5,7},{6,4},{7,5},{8,10},{9,11},{10,... | collective-permute-start | bytes 393224 | tf_op jit(solution)/shard_map/ppermute | solution.py:186
  21.2 1.5 %collective-permute-start.6 = (f32[5,64,128]{2,1,0:T(8,128)S(1)}, f32[5,64,128]{2,1,0:T(8,128)S(1)}, u32[]{:S(2)}, u32[]{:S(2)}) collective-permute-start(f32[5,64,128]{2,1,0:T(8,128)S(1)} %get-tuple-element.15), channel_id=1, source_target_pairs={{0,1},{1,0},{2,3},{3,2},{4,5},{5,4},{6,7},{7,6},{8,9},{9,8},{10,11... | collective-permute-start | bytes 491528 | tf_op jit(solution)/shard_map/ppermute | solution.py:186
  22.7 4.6 %collective-permute-start.7 = (f32[5,32,128]{2,1,0:T(8,128)S(1)}, f32[5,32,128]{2,1,0:T(8,128)S(1)}, u32[]{:S(2)}, u32[]{:S(2)}) collective-permute-start(f32[5,32,128]{2,1,0:T(8,128)S(1)} %dynamic-slice_add_fusion), channel_id=1, source_target_pairs={{0,4},{4,0},{8,12},{12,8},{16,20},{20,16},{24,28},{28,24},{1,5},{5... | collective-permute-start | bytes 245768 | tf_op jit(solution)/shard_map/ppermute | solution.py:186
  27.2 4.5 %collective-permute-start.8 = (f32[5,32,128]{2,1,0:T(8,128)S(1)}, f32[5,32,128]{2,1,0:T(8,128)S(1)}, u32[]{:S(2)}, u32[]{:S(2)}) collective-permute-start(f32[5,32,128]{2,1,0:T(8,128)S(1)} %add_add_fusion), channel_id=1, source_target_pairs={{0,8},{4,12},{8,0},{12,4},{16,24},{20,28},{24,16},{28,20},{1,9},{5... | collective-permute-start | bytes 245768 | tf_op jit(solution)/shard_map/ppermute | solution.py:186
  31.8 5.4 %collective-permute-start.9 = (f32[5,32,128]{2,1,0:T(8,128)S(1)}, f32[5,32,128]{2,1,0:T(8,128)S(1)}, u32[]{:S(2)}, u32[]{:S(2)}) collective-permute-start(f32[5,32,128]{2,1,0:T(8,128)S(1)} %add.41), channel_id=1, source_target_pairs={{0,16},{4,20},{8,24},{12,28},{16,0},{20,4},{24,8},{28,12},{1,17},{... | collective-permute-start | bytes 245768 | tf_op jit(solution)/shard_map/ppermute | solution.py:186
  37.2 4.5 %collective-permute-start.10 = (f32[5,32,128]{2,1,0:T(8,128)S(1)}, f32[5,32,128]{2,1,0:T(8,128)S(1)}, u32[]{:S(2)}, u32[]{:S(2)}) collective-permute-start(f32[5,32,128]{2,1,0:T(8,128)S(1)} %add.42.refs_0_), channel_id=1, source_target_pairs={{0,4},{4,0},{8,12},{12,8},{16,20},{20,16},{24,28},{28,24},{1,5},{5... | collective-permute-start | bytes 245768 | tf_op jit(solution)/shard_map/ppermute | solution.py:186
  39.0 5.0 %collective-permute-start.11 = (f32[5,32,128]{2,1,0:T(8,128)S(1)}, f32[5,32,128]{2,1,0:T(8,128)S(1)}, u32[]{:S(2)}, u32[]{:S(2)}) collective-permute-start(f32[5,32,128]{2,1,0:T(8,128)S(1)} %add.42.refs_0_), channel_id=1, source_target_pairs={{0,2},{1,3},{2,0},{3,1},{4,6},{5,7},{6,4},{7,5},{8,10},{9,11},{10,... | collective-permute-start | bytes 245768 | tf_op jit(solution)/shard_map/ppermute | solution.py:186
  41.7 4.4 %collective-permute-start.12 = (f32[5,32,128]{2,1,0:T(8,128)S(1)}, f32[5,32,128]{2,1,0:T(8,128)S(1)}, u32[]{:S(2)}, u32[]{:S(2)}) collective-permute-start(f32[5,32,128]{2,1,0:T(8,128)S(1)} %collective-permute-done.10.refs_1_), channel_id=1, source_target_pairs={{0,2},{1,3},{2,0},{3,1},{4,6},{5,7},{6,4},{7,5},{8,10},{9,11},{10,... | collective-permute-start | bytes 245768 | tf_op jit(solution)/shard_map/ppermute | solution.py:186
  43.4 2.7 %collective-permute-start.13 = (f32[5,32,128]{2,1,0:T(8,128)S(1)}, f32[5,32,128]{2,1,0:T(8,128)S(1)}, u32[]{:S(2)}, u32[]{:S(2)}) collective-permute-start(f32[5,32,128]{2,1,0:T(8,128)S(1)} %add.42.refs_0_), channel_id=1, source_target_pairs={{0,1},{1,0},{2,3},{3,2},{4,5},{5,4},{6,7},{7,6},{8,9},{9,8},{10,11... | collective-permute-start | bytes 245768 | tf_op jit(solution)/shard_map/ppermute | solution.py:186
  43.4 2.7 %collective-permute-start.14 = (f32[5,32,128]{2,1,0:T(8,128)S(1)}, f32[5,32,128]{2,1,0:T(8,128)S(1)}, u32[]{:S(2)}, u32[]{:S(2)}) collective-permute-start(f32[5,32,128]{2,1,0:T(8,128)S(1)} %collective-permute-done.10.refs_1_), channel_id=1, source_target_pairs={{0,1},{1,0},{2,3},{3,2},{4,5},{5,4},{6,7},{7,6},{8,9},{9,8},{10,11... | collective-permute-start | bytes 245768 | tf_op jit(solution)/shard_map/ppermute | solution.py:186
  44.0 2.2 %collective-permute-start.15 = (f32[5,32,128]{2,1,0:T(8,128)S(1)}, f32[5,32,128]{2,1,0:T(8,128)S(1)}, u32[]{:S(2)}, u32[]{:S(2)}) collective-permute-start(f32[5,32,128]{2,1,0:T(8,128)S(1)} %collective-permute-done.11.refs_2_), channel_id=1, source_target_pairs={{0,1},{1,0},{2,3},{3,2},{4,5},{5,4},{6,7},{7,6},{8,9},{9,8},{10,11... | collective-permute-start | bytes 245768 | tf_op jit(solution)/shard_map/ppermute | solution.py:186
  46.1 1.3 %collective-permute-start.16 = (f32[5,32,128]{2,1,0:T(8,128)S(1)}, f32[5,32,128]{2,1,0:T(8,128)S(1)}, u32[]{:S(2)}, u32[]{:S(2)}) collective-permute-start(f32[5,32,128]{2,1,0:T(8,128)S(1)} %collective-permute-done.12.refs_3_), channel_id=1, source_target_pairs={{0,1},{1,0},{2,3},{3,2},{4,5},{5,4},{6,7},{7,6},{8,9},{9,8},{10,11... | collective-permute-start | bytes 245768 | tf_op jit(solution)/shard_map/ppermute | solution.py:186

commit v6 on v5

--- a/solution.py
+++ b/solution.py
@@ -24,12 +24,13 @@
     b = r.astype(jnp.bfloat16)
     return a, b, (r - b.astype(jnp.float32)).astype(jnp.bfloat16)
 
+LEFT, RIGHT = (0, 0, 1, 0, 1, 2), (0, 1, 0, 2, 1, 0)
+
+def stack(parts, order, axis):
+    return jnp.concatenate([parts[n] for n in order], axis=axis)
+
 def outer(x, y):
-    x1, x2, x3 = split3(x)
-    y1, y2, y3 = split3(y)
-    left = jnp.concatenate([x1, x1, x2, x1, x2, x3], axis=0)
-    right = jnp.concatenate([y1, y2, y1, y3, y2, y1], axis=0)
-    return lax.dot_general(left, right, (((0,), (0,)), ((), ())), preferred_element_type=jnp.float32)
+    return lax.dot_general(stack(split3(x), LEFT, 0), stack(split3(y), RIGHT, 0), (((0,), (0,)), ((), ())), preferred_element_type=jnp.float32)
 
 def factor_block(d_ref, x_ref):
     steps = T // S
@@ -147,33 +148,26 @@
             for t in range(slots):
                 i, j = blocks_of(x, slots, t, nb)
                 w_ref[pl.ds(pl.multiple_of(i + row, part), part), pl.ds(j, T)] = ref[t]
-        r_ref[...] = jnp.zeros_like(r_ref)
+        for b in range(1, nb):
+            r_ref[b * T:(b + 1) * T, 0:b * T] = jnp.zeros((T, b * T), jnp.float32)
         row = lax.broadcasted_iota(jnp.int32, (T, T), 0)
         col = lax.broadcasted_iota(jnp.int32, (T, T), 1)
 
-        def step(b, _):
-            factor_block(w_ref, x_ref)
-            base = pl.multiple_of(b * T, T)
-            x = jnp.where(row >= col, x_ref[...], 0.0)
-            diagonal = jnp.dot(x, w_ref[0:T, 0:T], precision=HI, preferred_element_type=jnp.float32)
-            r_ref[pl.ds(base, T), pl.ds(base, T)] = jnp.where(row <= col, diagonal, 0.0)
-
-            @pl.when(b < nb - 1)
-            def _():
-                panel = jnp.dot(x, w_ref[0:T, T:n], precision=HI, preferred_element_type=jnp.float32)
-                for t in range(nb - 1):
-                    @pl.when(b + 1 + t < nb)
-                    def _():
-                        at = pl.multiple_of(base + (t + 1) * T, T)
-                        r_ref[pl.ds(base, T), pl.ds(at, T)] = panel[:, t * T:(t + 1) * T]
-                for i in range(nb - 1):
-                    update = lax.dot_general(
-                        panel[:, i * T:(i + 1) * T], panel[:, i * T:], (((0,), (0,)), ((), ())),
-                        precision=HI, preferred_element_type=jnp.float32)
-                    w_ref[i * T:(i + 1) * T, i * T:n - T] = w_ref[(i + 1) * T:(i + 2) * T, (i + 1) * T:n] - update
-            return 0
-
-        lax.fori_loop(0, nb, step, 0)
+        for b in range(nb):
+            low, high = b * T, (b + 1) * T
+            factor_block(w_ref.at[low:high, low:high], x_ref)
+            inverse = jnp.where(row >= col, x_ref[...], 0.0)
+            rows = jnp.dot(stack(split3(inverse), LEFT, 1), stack(split3(w_ref[low:high, low:n]), RIGHT, 0),
+                           preferred_element_type=jnp.float32)
+            r_ref[low:high, low:high] = jnp.where(row <= col, rows[:, 0:T], 0.0)
+            if b == nb - 1:
+                break
+            r_ref[low:high, high:n] = rows[:, T:]
+            right = stack(split3(rows[:, T:]), RIGHT, 0)
+            for i in range(b + 1, nb):
+                left = stack(split3(rows[:, (i - b) * T:(i - b + 1) * T].T), LEFT, 1)
+                w_ref[i * T:(i + 1) * T, i * T:n] -= jnp.dot(
+                    left, right[:, (i - b - 1) * T:], preferred_element_type=jnp.float32)
 
     return pl.pallas_call(
         body, name="factor", out_shape=jax.ShapeDtypeStruct((n, n), jnp.float32),
@@ -355,7 +349,7 @@
     over_x = lax.ppermute(own, "wave", across)
     over_core = swap(own, "wave", 1)
     residual, keep, send = front(
-        observed_flux, continuum_coeffs.T, continuum_basis, own, over_core, over_x, sketch_matrix)
+        observed_flux, continuum_coeffs.T, continuum_basis, jnp.maximum(own, 0.0), over_core, over_x, sketch_matrix)
     return (residual, reduce_and_factor(keep, send, observed_flux.shape[0] * lax.axis_size("spec")))
 
 

time: 63 us -> 60.4 us (0.959)
  Pallas kernels: 20.2 us -> 18.3 us
  local copies, waits for them, and re-layouts: 0.73 us -> 0.01 us
  other arithmetic: 0.1 us -> 0.81 us
  waiting for transfers between devices: 22.5 us -> 21.8 us
    pallas_call x1, Pallas kernels: 15.3 us -> 13.4 us  [factor(): pl.pallas_call(body, name='factor', out_shape=jax.ShapeDtypeStruct((n, n)...]
    ppermute x1, waiting for transfers between devices: 0.98 us -> 0.26 us  [shards(): over_x = lax.ppermute(own, 'wave', across)]
    max x0 -> x1, other arithmetic: none -> 0.72 us  [shards(): jnp.maximum(own, 0.0)]
    unnamed x6 -> x4, local copies, waits for them, and re-layouts: 0.73 us -> 0.01 us
  transfers between devices with their start and end apart: 17 -> 17, of which waited for: 12 -> 12; matrix products, arithmetic and copies ran while one was open for 0% -> 1% of each run, Pallas kernels for 0% -> 0%
where the time goes in v6:
time: 60.4 us; the launch traced here: 60.1 us
  waiting for transfers between devices  21.8 us (36%)
  starting transfers between devices  18.4 us (30%)
  Pallas kernels  18.3 us (30%)
  other arithmetic  0.81 us (1%)
  between operations  0.74 us (1%)
    ppermute x16, waiting for transfers between devices, swap(): lax.ppermute(x, axis, [(i, i ^ bit) for i in range(lax.axis_size(axis))])  21.6 us
    ppermute x16, starting transfers between devices, swap(): lax.ppermute(x, axis, [(i, i ^ bit) for i in range(lax.axis_size(axis))])  16 us
    pallas_call x1, Pallas kernels, factor(): pl.pallas_call(body, name='factor', out_shape=jax.ShapeDtypeStruct((n, n)...  13.4 us
    pallas_call x1, Pallas kernels, front(): pl.pallas_call(body, name='front', in_specs=[HBM] * 4 + [VMEM] * 3, out_s...  2.9 us
    ppermute x1, starting transfers between devices, shards(): over_x = lax.ppermute(own, 'wave', across)  2.44 us
    pallas_call x1, Pallas kernels, line_table(): pl.pallas_call(body, name='lines', in_specs=[HBM] * 6, out_specs=VMEM, ou...  1.42 us
  transfers between devices with their start and end apart: 17, of which 12 were waited for; matrix products, arithmetic and copies ran while one was open for 1% of the time, Pallas kernels for 0%

profile of v6, /device:TPU:0, one launch (start us, length us, event | category | flops | bytes accessed | tf_op | source)
XLA Modules:
  0.0 60.1 jit_solution(5919610667087021409)
XLA Ops:
  0.6 1.4 %lines.1 = f32[16,256]{1,0:T(8,128)} custom-call(s32[4,256]{1,0:T(4,128)} %bitcast.6, s32[4,256]{1,0:T(4,128)} %bitcast.7, f32[4,256]{1,0:T(4,128)} %bitcast.8, s32[1,256]{1,0:T(1,128)} %bitcast.9, f32[32]{0:T(128)} %strength_ref.1, f32[32]{0:T(128)} %widths_ref.1), custom_call_target="tpu_custom_call" | custom-call | tf_op jit(solution)/shard_map/lines/pallas_call | solution.py:261
  2.1 0.0 copy-start
  2.1 0.0 copy-start.1
  2.1 2.4 %collective-permute-start.1 = (f32[16,256]{1,0:T(8,128)}, f32[16,256]{1,0:T(8,128)S(1)}, u32[]{:S(2)}, u32[]{:S(2)}) collective-permute-start(f32[16,256]{1,0:T(8,128)} %lines.1), channel_id=1, source_target_pairs={{0,3},{1,2},{2,1},{3,0},{4,7},{5,6},{6,5},{7,4},{8,11},{9,10},{10,... | collective-permute-start | bytes 49160 | tf_op jit(solution)/shard_map/ppermute | solution.py:349
  4.5 0.7 %collective-permute-start = (f32[16,256]{1,0:T(8,128)}, f32[16,256]{1,0:T(8,128)S(1)}, u32[]{:S(2)}, u32[]{:S(2)}) collective-permute-start(f32[16,256]{1,0:T(8,128)} %lines.1), channel_id=1, source_target_pairs={{0,1},{1,0},{2,3},{3,2},{4,5},{5,4},{6,7},{7,6},{8,9},{9,8},{10,11... | collective-permute-start | bytes 49160 | tf_op jit(solution)/shard_map/ppermute | solution.py:180
  5.2 0.7 %broadcast_maximum_fusion.own_ref = f32[16,256]{1,0:T(8,128)S(1)} fusion(f32[16,256]{1,0:T(8,128)} %lines.1), kind=kLoop, calls=%fused_computation.2 | loop fusion | flops 4096 | bytes 32768 | tf_op jit(solution)/shard_map/max | solution.py:352
  5.9 0.3 collective-permute-done.1.x_ref
  6.2 0.1 collective-permute-done.core_ref
  6.2 0.0 copy-done
  6.3 0.0 copy-done.1
  6.3 2.9 %front.1 = (bf16[256,512]{1,0:T(8,128)(2,1)}, f32[64,512]{1,0:T(8,128)S(1)}, f32[64,512]{1,0:T(8,128)S(1)}, f32[64,512]{1,0:T(8,128)}, f32[64,512]{1,0:T(8,128)}) custom-call(bf16[256,512]{1,0:T(8,128)(2,1)} %flux_hbm.1, bf16[16,256]{1,0:T(8,128)(2,1)S(1)} %bitcast.5, bf16[16,512]{1,0:T(8,128)(2,1)S(1)} %copy-done, bf16[512,512]{1,0:T(8,128)(2,1)} %m_hbm.1, ...), custom_call_target="tpu_custom_call" | custom-call | tf_op jit(solution)/shard_map/front/pallas_call | solution.py:324
  9.2 0.7 %collective-permute-start.2 = (f32[64,512]{1,0:T(8,128)}, f32[64,512]{1,0:T(8,128)S(1)}, u32[]{:S(2)}, u32[]{:S(2)}) collective-permute-start(f32[64,512]{1,0:T(8,128)} %get-tuple-element.11), channel_id=1, source_target_pairs={{0,1},{1,0},{2,3},{3,2},{4,5},{5,4},{6,7},{7,6},{8,9},{9,8},{10,11... | collective-permute-start | bytes 393224 | tf_op jit(solution)/shard_map/ppermute | solution.py:180
  9.8 0.1 collective-permute-start.3
  9.9 1.1 %collective-permute-done.2 = f32[64,512]{1,0:T(8,128)S(1)} collective-permute-done((f32[64,512]{1,0:T(8,128)}, f32[64,512]{1,0:T(8,128)S(1)}, u32[]{:S(2)}, u32[]{:S(2)}) %collective-permute-start.2) | collective-permute-done | bytes 131104 | tf_op jit(solution)/shard_map/ppermute | solution.py:180
  11.1 2.2 %collective-permute-start.4 = (f32[64,512]{1,0:T(8,128)S(1)}, f32[64,512]{1,0:T(8,128)S(1)}, u32[]{:S(2)}, u32[]{:S(2)}) collective-permute-start(f32[64,512]{1,0:T(8,128)S(1)} %add.33.refs_0_), channel_id=1, source_target_pairs={{0,2},{1,3},{2,0},{3,1},{4,6},{5,7},{6,4},{7,5},{8,10},{9,11},{10,... | collective-permute-start | bytes 393224 | tf_op jit(solution)/shard_map/ppermute | solution.py:180
  13.3 0.0 collective-permute-done.3
  13.3 0.2 collective-permute-start.5
  13.5 4.1 %collective-permute-done.4.refs_2_ = f32[64,512]{1,0:T(8,128)S(1)} collective-permute-done((f32[64,512]{1,0:T(8,128)S(1)}, f32[64,512]{1,0:T(8,128)S(1)}, u32[]{:S(2)}, u32[]{:S(2)}) %collective-permute-start.4) | collective-permute-done | bytes 131104 | tf_op jit(solution)/shard_map/ppermute | solution.py:180
  17.5 2.3 %collective-permute-done.5.refs_3_ = f32[64,512]{1,0:T(8,128)S(1)} collective-permute-done((f32[64,512]{1,0:T(8,128)S(1)}, f32[64,512]{1,0:T(8,128)S(1)}, u32[]{:S(2)}, u32[]{:S(2)}) %collective-permute-start.5) | collective-permute-done | bytes 131104 | tf_op jit(solution)/shard_map/ppermute | solution.py:180
  19.9 0.5 gram.1
  20.4 0.1 collective-permute-start.6
  20.5 1.4 %collective-permute-done.6 = f32[5,64,128]{2,1,0:T(8,128)S(1)} collective-permute-done((f32[5,64,128]{2,1,0:T(8,128)S(1)}, f32[5,64,128]{2,1,0:T(8,128)S(1)}, u32[]{:S(2)}, u32[]{:S(2)}) %collective-permute-start.6) | collective-permute-done | bytes 163872 | tf_op jit(solution)/shard_map/ppermute | solution.py:180
  21.9 1.8 %collective-permute-start.7 = (f32[5,32,128]{2,1,0:T(8,128)S(1)}, f32[5,32,128]{2,1,0:T(8,128)S(1)}, u32[]{:S(2)}, u32[]{:S(2)}) collective-permute-start(f32[5,32,128]{2,1,0:T(8,128)S(1)} %dynamic-slice_add_fusion), channel_id=1, source_target_pairs={{0,4},{4,0},{8,12},{12,8},{16,20},{20,16},{24,28},{28,24},{1,5},{5... | collective-permute-start | bytes 245768 | tf_op jit(solution)/shard_map/ppermute | solution.py:180
  23.7 2.8 %collective-permute-done.7 = f32[5,32,128]{2,1,0:T(8,128)S(1)} collective-permute-done((f32[5,32,128]{2,1,0:T(8,128)S(1)}, f32[5,32,128]{2,1,0:T(8,128)S(1)}, u32[]{:S(2)}, u32[]{:S(2)}) %collective-permute-start.7) | collective-permute-done | bytes 81952 | tf_op jit(solution)/shard_map/ppermute | solution.py:180
  26.5 1.9 %collective-permute-start.8 = (f32[5,32,128]{2,1,0:T(8,128)S(1)}, f32[5,32,128]{2,1,0:T(8,128)S(1)}, u32[]{:S(2)}, u32[]{:S(2)}) collective-permute-start(f32[5,32,128]{2,1,0:T(8,128)S(1)} %add_add_fusion), channel_id=1, source_target_pairs={{0,8},{4,12},{8,0},{12,4},{16,24},{20,28},{24,16},{28,20},{1,9},{5... | collective-permute-start | bytes 245768 | tf_op jit(solution)/shard_map/ppermute | solution.py:180
  28.3 2.6 %collective-permute-done.8 = f32[5,32,128]{2,1,0:T(8,128)S(1)} collective-permute-done((f32[5,32,128]{2,1,0:T(8,128)S(1)}, f32[5,32,128]{2,1,0:T(8,128)S(1)}, u32[]{:S(2)}, u32[]{:S(2)}) %collective-permute-start.8) | collective-permute-done | bytes 81952 | tf_op jit(solution)/shard_map/ppermute | solution.py:180
  31.0 2.9 %collective-permute-start.9 = (f32[5,32,128]{2,1,0:T(8,128)S(1)}, f32[5,32,128]{2,1,0:T(8,128)S(1)}, u32[]{:S(2)}, u32[]{:S(2)}) collective-permute-start(f32[5,32,128]{2,1,0:T(8,128)S(1)} %add.41), channel_id=1, source_target_pairs={{0,16},{4,20},{8,24},{12,28},{16,0},{20,4},{24,8},{28,12},{1,17},{... | collective-permute-start | bytes 245768 | tf_op jit(solution)/shard_map/ppermute | solution.py:180
  33.9 2.5 %collective-permute-done.9 = f32[5,32,128]{2,1,0:T(8,128)S(1)} collective-permute-done((f32[5,32,128]{2,1,0:T(8,128)S(1)}, f32[5,32,128]{2,1,0:T(8,128)S(1)}, u32[]{:S(2)}, u32[]{:S(2)}) %collective-permute-start.9) | collective-permute-done | bytes 81952 | tf_op jit(solution)/shard_map/ppermute | solution.py:180
  36.4 1.8 %collective-permute-start.10 = (f32[5,32,128]{2,1,0:T(8,128)S(1)}, f32[5,32,128]{2,1,0:T(8,128)S(1)}, u32[]{:S(2)}, u32[]{:S(2)}) collective-permute-start(f32[5,32,128]{2,1,0:T(8,128)S(1)} %add.42.refs_0_), channel_id=1, source_target_pairs={{0,4},{4,0},{8,12},{12,8},{16,20},{20,16},{24,28},{28,24},{1,5},{5... | collective-permute-start | bytes 245768 | tf_op jit(solution)/shard_map/ppermute | solution.py:180
  38.2 1.5 %collective-permute-start.11 = (f32[5,32,128]{2,1,0:T(8,128)S(1)}, f32[5,32,128]{2,1,0:T(8,128)S(1)}, u32[]{:S(2)}, u32[]{:S(2)}) collective-permute-start(f32[5,32,128]{2,1,0:T(8,128)S(1)} %add.42.refs_0_), channel_id=1, source_target_pairs={{0,2},{1,3},{2,0},{3,1},{4,6},{5,7},{6,4},{7,5},{8,10},{9,11},{10,... | collective-permute-start | bytes 245768 | tf_op jit(solution)/shard_map/ppermute | solution.py:180
  39.8 1.2 %collective-permute-done.10.refs_1_ = f32[5,32,128]{2,1,0:T(8,128)S(1)} collective-permute-done((f32[5,32,128]{2,1,0:T(8,128)S(1)}, f32[5,32,128]{2,1,0:T(8,128)S(1)}, u32[]{:S(2)}, u32[]{:S(2)}) %collective-permute-start.10) | collective-permute-done | bytes 81952 | tf_op jit(solution)/shard_map/ppermute | solution.py:180
  40.9 1.7 %collective-permute-start.12 = (f32[5,32,128]{2,1,0:T(8,128)S(1)}, f32[5,32,128]{2,1,0:T(8,128)S(1)}, u32[]{:S(2)}, u32[]{:S(2)}) collective-permute-start(f32[5,32,128]{2,1,0:T(8,128)S(1)} %collective-permute-done.10.refs_1_), channel_id=1, source_target_pairs={{0,2},{1,3},{2,0},{3,1},{4,6},{5,7},{6,4},{7,5},{8,10},{9,11},{10,... | collective-permute-start | bytes 245768 | tf_op jit(solution)/shard_map/ppermute | solution.py:180
  42.7 0.0 collective-permute-start.13
  42.7 0.5 collective-permute-start.14
  43.2 0.0 collective-permute-done.11.refs_2_
  43.2 0.0 collective-permute-start.15
  43.2 2.2 %collective-permute-done.12.refs_3_ = f32[5,32,128]{2,1,0:T(8,128)S(1)} collective-permute-done((f32[5,32,128]{2,1,0:T(8,128)S(1)}, f32[5,32,128]{2,1,0:T(8,128)S(1)}, u32[]{:S(2)}, u32[]{:S(2)}) %collective-permute-start.12) | collective-permute-done | bytes 81952 | tf_op jit(solution)/shard_map/ppermute | solution.py:180
  45.4 0.0 collective-permute-start.16
  45.4 0.0 collective-permute-done.13.refs_4_
  45.4 0.0 collective-permute-done.15.refs_6_
  45.4 0.0 collective-permute-done.14.refs_5_
  45.4 1.3 %collective-permute-done.16.refs_7_ = f32[5,32,128]{2,1,0:T(8,128)S(1)} collective-permute-done((f32[5,32,128]{2,1,0:T(8,128)S(1)}, f32[5,32,128]{2,1,0:T(8,128)S(1)}, u32[]{:S(2)}, u32[]{:S(2)}) %collective-permute-start.16) | collective-permute-done | bytes 81952 | tf_op jit(solution)/shard_map/ppermute | solution.py:180
  46.7 13.4 %factor.1 = f32[512,512]{1,0:T(8,128)} custom-call(f32[5,32,128]{2,1,0:T(8,128)S(1)} %add.42.refs_0_, f32[5,32,128]{2,1,0:T(8,128)S(1)} %collective-permute-done.10.refs_1_, f32[5,32,128]{2,1,0:T(8,128)S(1)} %collective-permute-done.11.refs_2_, f32[5,32,128]{2,1,0:T(8,128)S(1)} %collective-permute-done.12.refs_3_, ...), custom_call_target="tpu_custom_call" | custom-call | tf_op jit(solution)/shard_map/factor/pallas_call | solution.py:172
  (6 shorter events, 0.1 us)
Async XLA Ops:
  2.1 4.2 %copy-start = (bf16[16,512]{1,0:T(8,128)(2,1)S(1)}, bf16[16,512]{1,0:T(8,128)(2,1)}, u32[]{:S(2)}) copy-start(bf16[16,512]{1,0:T(8,128)(2,1)} %basis_hbm.1) | copy-start | bytes 49156
  2.1 4.2 %copy-start.1 = (bf16[256,16]{0,1:T(8,128)(2,1)S(1)}, bf16[256,16]{0,1:T(8,128)(2,1)}, u32[]{:S(2)}) copy-start(bf16[256,16]{0,1:T(8,128)(2,1)} %param.11) | copy-start | bytes 24580
  2.1 4.1 %collective-permute-start.1 = (f32[16,256]{1,0:T(8,128)}, f32[16,256]{1,0:T(8,128)S(1)}, u32[]{:S(2)}, u32[]{:S(2)}) collective-permute-start(f32[16,256]{1,0:T(8,128)} %lines.1), channel_id=1, source_target_pairs={{0,3},{1,2},{2,1},{3,0},{4,7},{5,6},{6,5},{7,4},{8,11},{9,10},{10,... | collective-permute-start | bytes 49160 | tf_op jit(solution)/shard_map/ppermute | solution.py:349
  4.5 1.7 %collective-permute-start = (f32[16,256]{1,0:T(8,128)}, f32[16,256]{1,0:T(8,128)S(1)}, u32[]{:S(2)}, u32[]{:S(2)}) collective-permute-start(f32[16,256]{1,0:T(8,128)} %lines.1), channel_id=1, source_target_pairs={{0,1},{1,0},{2,3},{3,2},{4,5},{5,4},{6,7},{7,6},{8,9},{9,8},{10,11... | collective-permute-start | bytes 49160 | tf_op jit(solution)/shard_map/ppermute | solution.py:180
  9.2 1.9 %collective-permute-start.2 = (f32[64,512]{1,0:T(8,128)}, f32[64,512]{1,0:T(8,128)S(1)}, u32[]{:S(2)}, u32[]{:S(2)}) collective-permute-start(f32[64,512]{1,0:T(8,128)} %get-tuple-element.11), channel_id=1, source_target_pairs={{0,1},{1,0},{2,3},{3,2},{4,5},{5,4},{6,7},{7,6},{8,9},{9,8},{10,11... | collective-permute-start | bytes 393224 | tf_op jit(solution)/shard_map/ppermute | solution.py:180
  9.8 3.4 %collective-permute-start.3 = (f32[64,512]{1,0:T(8,128)}, f32[64,512]{1,0:T(8,128)S(1)}, u32[]{:S(2)}, u32[]{:S(2)}) collective-permute-start(f32[64,512]{1,0:T(8,128)} %get-tuple-element.13), channel_id=1, source_target_pairs={{0,1},{1,0},{2,3},{3,2},{4,5},{5,4},{6,7},{7,6},{8,9},{9,8},{10,11... | collective-permute-start | bytes 393224 | tf_op jit(solution)/shard_map/ppermute | solution.py:180
  11.1 6.5 %collective-permute-start.4 = (f32[64,512]{1,0:T(8,128)S(1)}, f32[64,512]{1,0:T(8,128)S(1)}, u32[]{:S(2)}, u32[]{:S(2)}) collective-permute-start(f32[64,512]{1,0:T(8,128)S(1)} %add.33.refs_0_), channel_id=1, source_target_pairs={{0,2},{1,3},{2,0},{3,1},{4,6},{5,7},{6,4},{7,5},{8,10},{9,11},{10,... | collective-permute-start | bytes 393224 | tf_op jit(solution)/shard_map/ppermute | solution.py:180
  13.3 6.6 %collective-permute-start.5 = (f32[64,512]{1,0:T(8,128)S(1)}, f32[64,512]{1,0:T(8,128)S(1)}, u32[]{:S(2)}, u32[]{:S(2)}) collective-permute-start(f32[64,512]{1,0:T(8,128)S(1)} %add.34.refs_1_), channel_id=1, source_target_pairs={{0,2},{1,3},{2,0},{3,1},{4,6},{5,7},{6,4},{7,5},{8,10},{9,11},{10,... | collective-permute-start | bytes 393224 | tf_op jit(solution)/shard_map/ppermute | solution.py:180
  20.4 1.5 %collective-permute-start.6 = (f32[5,64,128]{2,1,0:T(8,128)S(1)}, f32[5,64,128]{2,1,0:T(8,128)S(1)}, u32[]{:S(2)}, u32[]{:S(2)}) collective-permute-start(f32[5,64,128]{2,1,0:T(8,128)S(1)} %get-tuple-element.15), channel_id=1, source_target_pairs={{0,1},{1,0},{2,3},{3,2},{4,5},{5,4},{6,7},{7,6},{8,9},{9,8},{10,11... | collective-permute-start | bytes 491528 | tf_op jit(solution)/shard_map/ppermute | solution.py:180
  21.9 4.6 %collective-permute-start.7 = (f32[5,32,128]{2,1,0:T(8,128)S(1)}, f32[5,32,128]{2,1,0:T(8,128)S(1)}, u32[]{:S(2)}, u32[]{:S(2)}) collective-permute-start(f32[5,32,128]{2,1,0:T(8,128)S(1)} %dynamic-slice_add_fusion), channel_id=1, source_target_pairs={{0,4},{4,0},{8,12},{12,8},{16,20},{20,16},{24,28},{28,24},{1,5},{5... | collective-permute-start | bytes 245768 | tf_op jit(solution)/shard_map/ppermute | solution.py:180
  26.5 4.5 %collective-permute-start.8 = (f32[5,32,128]{2,1,0:T(8,128)S(1)}, f32[5,32,128]{2,1,0:T(8,128)S(1)}, u32[]{:S(2)}, u32[]{:S(2)}) collective-permute-start(f32[5,32,128]{2,1,0:T(8,128)S(1)} %add_add_fusion), channel_id=1, source_target_pairs={{0,8},{4,12},{8,0},{12,4},{16,24},{20,28},{24,16},{28,20},{1,9},{5... | collective-permute-start | bytes 245768 | tf_op jit(solution)/shard_map/ppermute | solution.py:180
  31.0 5.4 %collective-permute-start.9 = (f32[5,32,128]{2,1,0:T(8,128)S(1)}, f32[5,32,128]{2,1,0:T(8,128)S(1)}, u32[]{:S(2)}, u32[]{:S(2)}) collective-permute-start(f32[5,32,128]{2,1,0:T(8,128)S(1)} %add.41), channel_id=1, source_target_pairs={{0,16},{4,20},{8,24},{12,28},{16,0},{20,4},{24,8},{28,12},{1,17},{... | collective-permute-start | bytes 245768 | tf_op jit(solution)/shard_map/ppermute | solution.py:180
  36.4 4.5 %collective-permute-start.10 = (f32[5,32,128]{2,1,0:T(8,128)S(1)}, f32[5,32,128]{2,1,0:T(8,128)S(1)}, u32[]{:S(2)}, u32[]{:S(2)}) collective-permute-start(f32[5,32,128]{2,1,0:T(8,128)S(1)} %add.42.refs_0_), channel_id=1, source_target_pairs={{0,4},{4,0},{8,12},{12,8},{16,20},{20,16},{24,28},{28,24},{1,5},{5... | collective-permute-start | bytes 245768 | tf_op jit(solution)/shard_map/ppermute | solution.py:180
  38.2 5.0 %collective-permute-start.11 = (f32[5,32,128]{2,1,0:T(8,128)S(1)}, f32[5,32,128]{2,1,0:T(8,128)S(1)}, u32[]{:S(2)}, u32[]{:S(2)}) collective-permute-start(f32[5,32,128]{2,1,0:T(8,128)S(1)} %add.42.refs_0_), channel_id=1, source_target_pairs={{0,2},{1,3},{2,0},{3,1},{4,6},{5,7},{6,4},{7,5},{8,10},{9,11},{10,... | collective-permute-start | bytes 245768 | tf_op jit(solution)/shard_map/ppermute | solution.py:180
  40.9 4.4 %collective-permute-start.12 = (f32[5,32,128]{2,1,0:T(8,128)S(1)}, f32[5,32,128]{2,1,0:T(8,128)S(1)}, u32[]{:S(2)}, u32[]{:S(2)}) collective-permute-start(f32[5,32,128]{2,1,0:T(8,128)S(1)} %collective-permute-done.10.refs_1_), channel_id=1, source_target_pairs={{0,2},{1,3},{2,0},{3,1},{4,6},{5,7},{6,4},{7,5},{8,10},{9,11},{10,... | collective-permute-start | bytes 245768 | tf_op jit(solution)/shard_map/ppermute | solution.py:180
  42.7 2.7 %collective-permute-start.13 = (f32[5,32,128]{2,1,0:T(8,128)S(1)}, f32[5,32,128]{2,1,0:T(8,128)S(1)}, u32[]{:S(2)}, u32[]{:S(2)}) collective-permute-start(f32[5,32,128]{2,1,0:T(8,128)S(1)} %add.42.refs_0_), channel_id=1, source_target_pairs={{0,1},{1,0},{2,3},{3,2},{4,5},{5,4},{6,7},{7,6},{8,9},{9,8},{10,11... | collective-permute-start | bytes 245768 | tf_op jit(solution)/shard_map/ppermute | solution.py:180
  42.7 2.7 %collective-permute-start.14 = (f32[5,32,128]{2,1,0:T(8,128)S(1)}, f32[5,32,128]{2,1,0:T(8,128)S(1)}, u32[]{:S(2)}, u32[]{:S(2)}) collective-permute-start(f32[5,32,128]{2,1,0:T(8,128)S(1)} %collective-permute-done.10.refs_1_), channel_id=1, source_target_pairs={{0,1},{1,0},{2,3},{3,2},{4,5},{5,4},{6,7},{7,6},{8,9},{9,8},{10,11... | collective-permute-start | bytes 245768 | tf_op jit(solution)/shard_map/ppermute | solution.py:180
  43.2 2.2 %collective-permute-start.15 = (f32[5,32,128]{2,1,0:T(8,128)S(1)}, f32[5,32,128]{2,1,0:T(8,128)S(1)}, u32[]{:S(2)}, u32[]{:S(2)}) collective-permute-start(f32[5,32,128]{2,1,0:T(8,128)S(1)} %collective-permute-done.11.refs_2_), channel_id=1, source_target_pairs={{0,1},{1,0},{2,3},{3,2},{4,5},{5,4},{6,7},{7,6},{8,9},{9,8},{10,11... | collective-permute-start | bytes 245768 | tf_op jit(solution)/shard_map/ppermute | solution.py:180
  45.4 1.3 %collective-permute-start.16 = (f32[5,32,128]{2,1,0:T(8,128)S(1)}, f32[5,32,128]{2,1,0:T(8,128)S(1)}, u32[]{:S(2)}, u32[]{:S(2)}) collective-permute-start(f32[5,32,128]{2,1,0:T(8,128)S(1)} %collective-permute-done.12.refs_3_), channel_id=1, source_target_pairs={{0,1},{1,0},{2,3},{3,2},{4,5},{5,4},{6,7},{7,6},{8,9},{9,8},{10,11... | collective-permute-start | bytes 245768 | tf_op jit(solution)/shard_map/ppermute | solution.py:180

commit v7 on v6

--- a/solution.py
+++ b/solution.py
@@ -228,6 +228,7 @@
 
 
 PARTS = 2
+FRONT_VMEM = 107 << 19
 SMEM = pl.BlockSpec(memory_space=pltpu.SMEM)
 VMEM = pl.BlockSpec(memory_space=pltpu.VMEM)
 HBM = pl.BlockSpec(memory_space=pltpu.HBM)
@@ -268,34 +269,36 @@
     )(centres, line_index, column_factor, wing, strength, widths)
 
 
-def front(flux, coeffs_t, basis, own, over_core, over_x, sketch_matrix):
+def front(n, flux, coeffs_t, basis, own, over_core, over_x, sketch_matrix, residual):
     spectra, pixels = flux.shape
+    count = spectra // PARTS
     absorbers = own.shape[0] // 4
-    part = spectra // (2 * PARTS)
     k = sketch_matrix.shape[1]
-
-    def body(flux_hbm, coeffs_hbm, basis_hbm, m_hbm, own_ref, core_ref, x_ref, res_hbm, *refs):
-        outs, (flux_ref, coeffs_ref, basis_ref, m_ref, res_ref, tau_ref, sems) = refs[:2 * PARTS], refs[2 * PARTS:]
-        loads = [pltpu.make_async_copy(source, target, sems.at[n]) for n, (source, target) in enumerate(
-            ((flux_hbm, flux_ref), (coeffs_hbm, coeffs_ref), (basis_hbm, basis_ref), (m_hbm, m_ref)))]
+    mine = slice(n * count, (n + 1) * count)
+
+    def body(flux_hbm, coeffs_hbm, basis_hbm, m_hbm, own_ref, core_ref, x_ref, *refs):
+        res_hbm, keep_ref, send_ref, flux_ref, coeffs_ref, basis_ref, m_ref, res_ref, tau_ref, sems = refs[-10:]
+        loads = [pltpu.make_async_copy(source, target, sems.at[i]) for i, (source, target) in enumerate(
+            ((flux_hbm.at[mine, :], flux_ref), (coeffs_hbm, coeffs_ref), (basis_hbm, basis_ref), (m_hbm, m_ref)))]
         for copy in loads:
             copy.start()
         w = lax.axis_index("wave")
         core = w % 2
         first = (w * pixels).astype(jnp.float32)
-        wing_row = own_ref[3 * absorbers:3 * absorbers + 1, :]
-
-        def depth(ref, start, count):
-            at = lax.broadcasted_iota(jnp.int32, (count, spectra), 0).astype(jnp.float32) + start
+        wing_row = own_ref[3 * absorbers:3 * absorbers + 1, mine]
+
+        def depth(ref, start, height):
+            at = lax.broadcasted_iota(jnp.int32, (height, count), 0).astype(jnp.float32) + start
             total = None
             for a in range(absorbers):
-                centre, amplitude, inverse = (ref[n * absorbers + a:n * absorbers + a + 1, :] for n in range(3))
+                centre, amplitude, inverse = (
+                    ref[i * absorbers + a:i * absorbers + a + 1, mine] for i in range(3))
                 term = bell(at - centre, amplitude, inverse, wing_row)
                 total = term if total is None else total + term
             return total
 
-        def chunk(n, _):
-            row = pl.multiple_of(n * CHUNK, CHUNK)
+        def chunk(i, _):
+            row = pl.multiple_of(i * CHUNK, CHUNK)
             tau_ref[pl.ds(row, CHUNK), :] = depth(own_ref, first + row.astype(jnp.float32), CHUNK)
             return 0
 
@@ -305,30 +308,35 @@
             tau_ref[pl.ds(row, WING), :] += depth(ref, first + row.astype(jnp.float32), WING)
         for copy in loads[:3]:
             copy.wait()
-        for n in range(pixels // T):
-            lanes = slice(n * T, (n + 1) * T)
+        for i in range(pixels // T):
+            lanes = slice(i * T, (i + 1) * T)
             seen = jnp.exp(-tau_ref[lanes, :].T)
-            continuum = lax.dot_general(coeffs_ref[...], basis_ref[:, lanes], (((0,), (0,)), ((), ())),
+            continuum = lax.dot_general(coeffs_ref[:, mine], basis_ref[:, lanes], (((0,), (0,)), ((), ())),
                                         preferred_element_type=jnp.float32)
             res_ref[:, lanes] = (flux_ref[:, lanes].astype(jnp.float32) - continuum * seen).astype(jnp.bfloat16)
-        store = pltpu.make_async_copy(res_ref, res_hbm, sems.at[4])
+        store = pltpu.make_async_copy(res_ref, res_hbm.at[mine, :], sems.at[4])
         store.start()
         loads[3].wait()
-        for n, out in enumerate(outs):
-            side = core if n < PARTS else 1 - core
-            row = pl.multiple_of(side * (spectra // 2) + (n % PARTS) * part, part)
-            out[...] = jnp.dot(res_ref[pl.ds(row, part), :], m_ref[...], preferred_element_type=jnp.float32)
+        half = count // 2
+        for out, side in ((send_ref, 1 - core), (keep_ref, core)):
+            row = pl.multiple_of(side * half, half)
+            out[...] = jnp.dot(res_ref[pl.ds(row, half), :], m_ref[...], preferred_element_type=jnp.float32)
         store.wait()
 
-    rows = jax.ShapeDtypeStruct((part, k), jnp.float32)
-    outs = pl.pallas_call(
-        body, name="front", in_specs=[HBM] * 4 + [VMEM] * 3, out_specs=[HBM] + [VMEM] * (2 * PARTS),
-        out_shape=[jax.ShapeDtypeStruct(flux.shape, jnp.bfloat16)] + [rows] * (2 * PARTS),
-        scratch_shapes=[pltpu.VMEM(a.shape, a.dtype) for a in (flux, coeffs_t, basis, sketch_matrix, flux)]
-        + [pltpu.VMEM((pixels, spectra), jnp.float32), pltpu.SemaphoreType.DMA((5,))],
-        compiler_params=pltpu.CompilerParams(vmem_limit_bytes=107 << 19),
-    )(flux, coeffs_t, basis, sketch_matrix, own, over_core, over_x)
-    return outs[0], outs[1:1 + PARTS], outs[1 + PARTS:]
+    rows = jax.ShapeDtypeStruct((count // 2, k), jnp.float32)
+    earlier = [] if residual is None else [residual]
+    return pl.pallas_call(
+        body, name="front", in_specs=[HBM] * 4 + [VMEM] * 3 + [HBM] * len(earlier), out_specs=[HBM, VMEM, VMEM],
+        out_shape=[jax.ShapeDtypeStruct(flux.shape, jnp.bfloat16), rows, rows],
+        input_output_aliases={7: 0} if earlier else {},
+        scratch_shapes=[pltpu.VMEM((count, pixels), flux.dtype)]
+        + [pltpu.VMEM(a.shape, a.dtype) for a in (coeffs_t, basis, sketch_matrix)]
+        + [pltpu.VMEM((count, pixels), jnp.bfloat16), pltpu.VMEM((pixels, count), jnp.float32),
+           pltpu.SemaphoreType.DMA((5,))],
+        cost_estimate=pl.CostEstimate(flops=2 * count * pixels * k, transcendentals=0,
+                                      bytes_accessed=4 * count * pixels + 2 * pixels * k),
+        compiler_params=pltpu.CompilerParams(vmem_limit_bytes=FRONT_VMEM),
+    )(flux, coeffs_t, basis, sketch_matrix, own, over_core, over_x, *earlier)
 
 
 def shards(
@@ -348,8 +356,13 @@
     across = [(i, (i + 1 if i % 2 else i - 1) % waves) for i in range(waves)]
     over_x = lax.ppermute(own, "wave", across)
     over_core = swap(own, "wave", 1)
-    residual, keep, send = front(
-        observed_flux, continuum_coeffs.T, continuum_basis, jnp.maximum(own, 0.0), over_core, over_x, sketch_matrix)
+    here = jnp.maximum(own, 0.0)
+    residual, keep, send = None, [], []
+    for n in range(PARTS):
+        residual, stays, goes = front(n, observed_flux, continuum_coeffs.T, continuum_basis, here,
+                                      over_core, over_x, sketch_matrix, residual)
+        keep.append(stays)
+        send.append(goes)
     return (residual, reduce_and_factor(keep, send, observed_flux.shape[0] * lax.axis_size("spec")))
 
 

time: 60.4 us -> 60.1 us (level)
  waiting for transfers between devices: 21.8 us -> 19.9 us
  starting transfers between devices: 18.4 us -> 19.4 us
  Pallas kernels: 18.3 us -> 19.1 us
    ppermute x16, waiting for transfers between devices: 21.6 us -> 19.6 us  [swap(): lax.ppermute(x, axis, [(i, i ^ bit) for i in range(lax.axis_size(axis))])]
    ppermute x16, starting transfers between devices: 16 us -> 16.9 us  [swap(): lax.ppermute(x, axis, [(i, i ^ bit) for i in range(lax.axis_size(axis))])]
    pallas_call x1 -> x2, Pallas kernels: 2.9 us -> 3.68 us  [front(): pl.pallas_call(body, name='front', in_specs=[HBM] * 4 + [VMEM] * 3 + [HBM...]
  transfers between devices with their start and end apart: 17 -> 17, of which waited for: 12 -> 11; matrix products, arithmetic and copies ran while one was open for 1% -> 1% of each run, Pallas kernels for 0% -> 3%
where the time goes in v7:
time: 60.1 us; the launch traced here: 59.9 us
  waiting for transfers between devices  19.9 us (33%)
  starting transfers between devices  19.4 us (32%)
  Pallas kernels  19.1 us (32%)
  other arithmetic  0.82 us (1%)
  between operations  0.75 us (1%)
    ppermute x16, waiting for transfers between devices, swap(): lax.ppermute(x, axis, [(i, i ^ bit) for i in range(lax.axis_size(axis))])  19.6 us
    ppermute x16, starting transfers between devices, swap(): lax.ppermute(x, axis, [(i, i ^ bit) for i in range(lax.axis_size(axis))])  16.9 us
    pallas_call x1, Pallas kernels, factor(): pl.pallas_call(body, name='factor', out_shape=jax.ShapeDtypeStruct((n, n)...  13.4 us
    pallas_call x2, Pallas kernels, front(): pl.pallas_call(body, name='front', in_specs=[HBM] * 4 + [VMEM] * 3 + [HBM...  3.68 us
    ppermute x1, starting transfers between devices, shards(): over_x = lax.ppermute(own, 'wave', across)  2.44 us
    pallas_call x1, Pallas kernels, line_table(): pl.pallas_call(body, name='lines', in_specs=[HBM] * 6, out_specs=VMEM, ou...  1.42 us
  transfers between devices with their start and end apart: 17, of which 11 were waited for; matrix products, arithmetic and copies ran while one was open for 1% of the time, Pallas kernels for 3%

profile of v7, /device:TPU:0, one launch (start us, length us, event | category | flops | bytes accessed | tf_op | source)
XLA Modules:
  0.0 59.9 jit_solution(871097124994962973)
XLA Ops:
  0.6 1.4 %lines.1 = f32[16,256]{1,0:T(8,128)} custom-call(s32[4,256]{1,0:T(4,128)} %bitcast.7, s32[4,256]{1,0:T(4,128)} %bitcast.8, f32[4,256]{1,0:T(4,128)} %bitcast.9, s32[1,256]{1,0:T(1,128)} %bitcast.10, f32[32]{0:T(128)} %strength_ref.1, f32[32]{0:T(128)} %widths_ref.1), custom_call_target="tpu_custom_call" | custom-call | tf_op jit(solution)/shard_map/lines/pallas_call | solution.py:262
  2.1 0.0 copy-start
  2.1 0.0 copy-start.1
  2.1 2.4 %collective-permute-start.1 = (f32[16,256]{1,0:T(8,128)}, f32[16,256]{1,0:T(8,128)S(1)}, u32[]{:S(2)}, u32[]{:S(2)}) collective-permute-start(f32[16,256]{1,0:T(8,128)} %lines.1), channel_id=1, source_target_pairs={{0,3},{1,2},{2,1},{3,0},{4,7},{5,6},{6,5},{7,4},{8,11},{9,10},{10,... | collective-permute-start | bytes 49160 | tf_op jit(solution)/shard_map/ppermute | solution.py:357
  4.5 0.7 %collective-permute-start = (f32[16,256]{1,0:T(8,128)}, f32[16,256]{1,0:T(8,128)S(1)}, u32[]{:S(2)}, u32[]{:S(2)}) collective-permute-start(f32[16,256]{1,0:T(8,128)} %lines.1), channel_id=1, source_target_pairs={{0,1},{1,0},{2,3},{3,2},{4,5},{5,4},{6,7},{7,6},{8,9},{9,8},{10,11... | collective-permute-start | bytes 49160 | tf_op jit(solution)/shard_map/ppermute | solution.py:180
  5.2 0.7 %broadcast_maximum_fusion.own_ref = f32[16,256]{1,0:T(8,128)S(1)} fusion(f32[16,256]{1,0:T(8,128)} %lines.1), kind=kLoop, calls=%fused_computation.2 | loop fusion | flops 4096 | bytes 32768 | tf_op jit(solution)/shard_map/max | solution.py:359
  5.9 0.3 collective-permute-done.1.x_ref
  6.2 0.1 collective-permute-done.core_ref
  6.2 0.0 copy-done
  6.3 0.0 copy-done.1
  6.3 1.8 %front.2 = (bf16[256,512]{1,0:T(8,128)(2,1)}, f32[64,512]{1,0:T(8,128)S(1)}, f32[64,512]{1,0:T(8,128)S(1)}) custom-call(bf16[256,512]{1,0:T(8,128)(2,1)} %flux_hbm.3, bf16[16,256]{1,0:T(8,128)(2,1)S(1)} %bitcast.5, bf16[16,512]{1,0:T(8,128)(2,1)S(1)} %copy-done, bf16[512,512]{1,0:T(8,128)(2,1)} %m_hbm.3, f32[16,256]{1,0:T(8,128)S(1)} %broadcast_maximum_fusion.own_ref, ...), custom_call_target="tpu_custom_call" | custom-call | flops 67108864 | bytes 786432 | tf_op jit(solution)/shard_map/front/pallas_call | solution.py:328
  8.1 0.7 %collective-permute-start.2 = (f32[64,512]{1,0:T(8,128)S(1)}, f32[64,512]{1,0:T(8,128)S(1)}, u32[]{:S(2)}, u32[]{:S(2)}) collective-permute-start(f32[64,512]{1,0:T(8,128)S(1)} %get-tuple-element.13), channel_id=1, source_target_pairs={{0,1},{1,0},{2,3},{3,2},{4,5},{5,4},{6,7},{7,6},{8,9},{9,8},{10,11... | collective-permute-start | bytes 393224 | tf_op jit(solution)/shard_map/ppermute | solution.py:180
  8.8 1.8 %front.3 = (bf16[256,512]{1,0:T(8,128)(2,1)}, f32[64,512]{1,0:T(8,128)S(1)}, f32[64,512]{1,0:T(8,128)S(1)}) custom-call(bf16[256,512]{1,0:T(8,128)(2,1)} %flux_hbm.3, bf16[16,256]{1,0:T(8,128)(2,1)S(1)} %bitcast.6, bf16[16,512]{1,0:T(8,128)(2,1)S(1)} %copy-done, bf16[512,512]{1,0:T(8,128)(2,1)} %m_hbm.3, ...), custom_call_target="tpu_custom_call", output_to_operand_aliasing={{0}: (7, {})} | custom-call | flops 67108864 | bytes 786432 | tf_op jit(solution)/shard_map/front/pallas_call | solution.py:328
  10.6 0.1 collective-permute-start.3
  10.7 0.0 collective-permute-done.2
  10.7 2.3 %collective-permute-start.4 = (f32[64,512]{1,0:T(8,128)S(1)}, f32[64,512]{1,0:T(8,128)S(1)}, u32[]{:S(2)}, u32[]{:S(2)}) collective-permute-start(f32[64,512]{1,0:T(8,128)S(1)} %add.33.refs_0_), channel_id=1, source_target_pairs={{0,2},{1,3},{2,0},{3,1},{4,6},{5,7},{6,4},{7,5},{8,10},{9,11},{10,... | collective-permute-start | bytes 393224 | tf_op jit(solution)/shard_map/ppermute | solution.py:180
  13.1 0.0 collective-permute-done.3
  13.1 1.0 %collective-permute-start.5 = (f32[64,512]{1,0:T(8,128)S(1)}, f32[64,512]{1,0:T(8,128)S(1)}, u32[]{:S(2)}, u32[]{:S(2)}) collective-permute-start(f32[64,512]{1,0:T(8,128)S(1)} %add.34.refs_1_), channel_id=1, source_target_pairs={{0,2},{1,3},{2,0},{3,1},{4,6},{5,7},{6,4},{7,5},{8,10},{9,11},{10,... | collective-permute-start | bytes 393224 | tf_op jit(solution)/shard_map/ppermute | solution.py:180
  14.1 3.3 %collective-permute-done.4.refs_2_ = f32[64,512]{1,0:T(8,128)S(1)} collective-permute-done((f32[64,512]{1,0:T(8,128)S(1)}, f32[64,512]{1,0:T(8,128)S(1)}, u32[]{:S(2)}, u32[]{:S(2)}) %collective-permute-start.4) | collective-permute-done | bytes 131104 | tf_op jit(solution)/shard_map/ppermute | solution.py:180
  17.3 2.3 %collective-permute-done.5.refs_3_ = f32[64,512]{1,0:T(8,128)S(1)} collective-permute-done((f32[64,512]{1,0:T(8,128)S(1)}, f32[64,512]{1,0:T(8,128)S(1)}, u32[]{:S(2)}, u32[]{:S(2)}) %collective-permute-start.5) | collective-permute-done | bytes 131104 | tf_op jit(solution)/shard_map/ppermute | solution.py:180
  19.6 0.5 gram.1
  20.2 0.1 collective-permute-start.6
  20.3 1.4 %collective-permute-done.6 = f32[5,64,128]{2,1,0:T(8,128)S(1)} collective-permute-done((f32[5,64,128]{2,1,0:T(8,128)S(1)}, f32[5,64,128]{2,1,0:T(8,128)S(1)}, u32[]{:S(2)}, u32[]{:S(2)}) %collective-permute-start.6) | collective-permute-done | bytes 163872 | tf_op jit(solution)/shard_map/ppermute | solution.py:180
  21.7 1.8 %collective-permute-start.7 = (f32[5,32,128]{2,1,0:T(8,128)S(1)}, f32[5,32,128]{2,1,0:T(8,128)S(1)}, u32[]{:S(2)}, u32[]{:S(2)}) collective-permute-start(f32[5,32,128]{2,1,0:T(8,128)S(1)} %dynamic-slice_add_fusion), channel_id=1, source_target_pairs={{0,4},{4,0},{8,12},{12,8},{16,20},{20,16},{24,28},{28,24},{1,5},{5... | collective-permute-start | bytes 245768 | tf_op jit(solution)/shard_map/ppermute | solution.py:180
  23.5 2.8 %collective-permute-done.7 = f32[5,32,128]{2,1,0:T(8,128)S(1)} collective-permute-done((f32[5,32,128]{2,1,0:T(8,128)S(1)}, f32[5,32,128]{2,1,0:T(8,128)S(1)}, u32[]{:S(2)}, u32[]{:S(2)}) %collective-permute-start.7) | collective-permute-done | bytes 81952 | tf_op jit(solution)/shard_map/ppermute | solution.py:180
  26.3 1.9 %collective-permute-start.8 = (f32[5,32,128]{2,1,0:T(8,128)S(1)}, f32[5,32,128]{2,1,0:T(8,128)S(1)}, u32[]{:S(2)}, u32[]{:S(2)}) collective-permute-start(f32[5,32,128]{2,1,0:T(8,128)S(1)} %add_add_fusion), channel_id=1, source_target_pairs={{0,8},{4,12},{8,0},{12,4},{16,24},{20,28},{24,16},{28,20},{1,9},{5... | collective-permute-start | bytes 245768 | tf_op jit(solution)/shard_map/ppermute | solution.py:180
  28.1 2.6 %collective-permute-done.8 = f32[5,32,128]{2,1,0:T(8,128)S(1)} collective-permute-done((f32[5,32,128]{2,1,0:T(8,128)S(1)}, f32[5,32,128]{2,1,0:T(8,128)S(1)}, u32[]{:S(2)}, u32[]{:S(2)}) %collective-permute-start.8) | collective-permute-done | bytes 81952 | tf_op jit(solution)/shard_map/ppermute | solution.py:180
  30.8 2.9 %collective-permute-start.9 = (f32[5,32,128]{2,1,0:T(8,128)S(1)}, f32[5,32,128]{2,1,0:T(8,128)S(1)}, u32[]{:S(2)}, u32[]{:S(2)}) collective-permute-start(f32[5,32,128]{2,1,0:T(8,128)S(1)} %add.41), channel_id=1, source_target_pairs={{0,16},{4,20},{8,24},{12,28},{16,0},{20,4},{24,8},{28,12},{1,17},{... | collective-permute-start | bytes 245768 | tf_op jit(solution)/shard_map/ppermute | solution.py:180
  33.6 2.5 %collective-permute-done.9 = f32[5,32,128]{2,1,0:T(8,128)S(1)} collective-permute-done((f32[5,32,128]{2,1,0:T(8,128)S(1)}, f32[5,32,128]{2,1,0:T(8,128)S(1)}, u32[]{:S(2)}, u32[]{:S(2)}) %collective-permute-start.9) | collective-permute-done | bytes 81952 | tf_op jit(solution)/shard_map/ppermute | solution.py:180
  36.2 1.8 %collective-permute-start.10 = (f32[5,32,128]{2,1,0:T(8,128)S(1)}, f32[5,32,128]{2,1,0:T(8,128)S(1)}, u32[]{:S(2)}, u32[]{:S(2)}) collective-permute-start(f32[5,32,128]{2,1,0:T(8,128)S(1)} %add.42.refs_0_), channel_id=1, source_target_pairs={{0,4},{4,0},{8,12},{12,8},{16,20},{20,16},{24,28},{28,24},{1,5},{5... | collective-permute-start | bytes 245768 | tf_op jit(solution)/shard_map/ppermute | solution.py:180
  38.0 1.5 %collective-permute-start.11 = (f32[5,32,128]{2,1,0:T(8,128)S(1)}, f32[5,32,128]{2,1,0:T(8,128)S(1)}, u32[]{:S(2)}, u32[]{:S(2)}) collective-permute-start(f32[5,32,128]{2,1,0:T(8,128)S(1)} %add.42.refs_0_), channel_id=1, source_target_pairs={{0,2},{1,3},{2,0},{3,1},{4,6},{5,7},{6,4},{7,5},{8,10},{9,11},{10,... | collective-permute-start | bytes 245768 | tf_op jit(solution)/shard_map/ppermute | solution.py:180
  39.5 1.2 %collective-permute-done.10.refs_1_ = f32[5,32,128]{2,1,0:T(8,128)S(1)} collective-permute-done((f32[5,32,128]{2,1,0:T(8,128)S(1)}, f32[5,32,128]{2,1,0:T(8,128)S(1)}, u32[]{:S(2)}, u32[]{:S(2)}) %collective-permute-start.10) | collective-permute-done | bytes 81952 | tf_op jit(solution)/shard_map/ppermute | solution.py:180
  40.7 1.7 %collective-permute-start.12 = (f32[5,32,128]{2,1,0:T(8,128)S(1)}, f32[5,32,128]{2,1,0:T(8,128)S(1)}, u32[]{:S(2)}, u32[]{:S(2)}) collective-permute-start(f32[5,32,128]{2,1,0:T(8,128)S(1)} %collective-permute-done.10.refs_1_), channel_id=1, source_target_pairs={{0,2},{1,3},{2,0},{3,1},{4,6},{5,7},{6,4},{7,5},{8,10},{9,11},{10,... | collective-permute-start | bytes 245768 | tf_op jit(solution)/shard_map/ppermute | solution.py:180
  42.4 0.0 collective-permute-start.13
  42.4 0.5 collective-permute-start.14
  43.0 0.0 collective-permute-done.11.refs_2_
  43.0 0.0 collective-permute-start.15
  43.0 2.2 %collective-permute-done.12.refs_3_ = f32[5,32,128]{2,1,0:T(8,128)S(1)} collective-permute-done((f32[5,32,128]{2,1,0:T(8,128)S(1)}, f32[5,32,128]{2,1,0:T(8,128)S(1)}, u32[]{:S(2)}, u32[]{:S(2)}) %collective-permute-start.12) | collective-permute-done | bytes 81952 | tf_op jit(solution)/shard_map/ppermute | solution.py:180
  45.1 0.0 collective-permute-start.16
  45.1 0.0 collective-permute-done.13.refs_4_
  45.2 0.0 collective-permute-done.15.refs_6_
  45.2 0.0 collective-permute-done.14.refs_5_
  45.2 1.3 %collective-permute-done.16.refs_7_ = f32[5,32,128]{2,1,0:T(8,128)S(1)} collective-permute-done((f32[5,32,128]{2,1,0:T(8,128)S(1)}, f32[5,32,128]{2,1,0:T(8,128)S(1)}, u32[]{:S(2)}, u32[]{:S(2)}) %collective-permute-start.16) | collective-permute-done | bytes 81952 | tf_op jit(solution)/shard_map/ppermute | solution.py:180
  46.4 13.4 %factor.1 = f32[512,512]{1,0:T(8,128)} custom-call(f32[5,32,128]{2,1,0:T(8,128)S(1)} %add.42.refs_0_, f32[5,32,128]{2,1,0:T(8,128)S(1)} %collective-permute-done.10.refs_1_, f32[5,32,128]{2,1,0:T(8,128)S(1)} %collective-permute-done.11.refs_2_, f32[5,32,128]{2,1,0:T(8,128)S(1)} %collective-permute-done.12.refs_3_, ...), custom_call_target="tpu_custom_call" | custom-call | tf_op jit(solution)/shard_map/factor/pallas_call | solution.py:172
  (6 shorter events, 0.1 us)
Async XLA Ops:
  2.1 4.2 %copy-start = (bf16[16,512]{1,0:T(8,128)(2,1)S(1)}, bf16[16,512]{1,0:T(8,128)(2,1)}, u32[]{:S(2)}) copy-start(bf16[16,512]{1,0:T(8,128)(2,1)} %basis_hbm.3) | copy-start | bytes 49156
  2.1 4.2 %copy-start.1 = (bf16[256,16]{0,1:T(8,128)(2,1)S(1)}, bf16[256,16]{0,1:T(8,128)(2,1)}, u32[]{:S(2)}) copy-start(bf16[256,16]{0,1:T(8,128)(2,1)} %param.11) | copy-start | bytes 24580
  2.1 4.1 %collective-permute-start.1 = (f32[16,256]{1,0:T(8,128)}, f32[16,256]{1,0:T(8,128)S(1)}, u32[]{:S(2)}, u32[]{:S(2)}) collective-permute-start(f32[16,256]{1,0:T(8,128)} %lines.1), channel_id=1, source_target_pairs={{0,3},{1,2},{2,1},{3,0},{4,7},{5,6},{6,5},{7,4},{8,11},{9,10},{10,... | collective-permute-start | bytes 49160 | tf_op jit(solution)/shard_map/ppermute | solution.py:357
  4.5 1.7 %collective-permute-start = (f32[16,256]{1,0:T(8,128)}, f32[16,256]{1,0:T(8,128)S(1)}, u32[]{:S(2)}, u32[]{:S(2)}) collective-permute-start(f32[16,256]{1,0:T(8,128)} %lines.1), channel_id=1, source_target_pairs={{0,1},{1,0},{2,3},{3,2},{4,5},{5,4},{6,7},{7,6},{8,9},{9,8},{10,11... | collective-permute-start | bytes 49160 | tf_op jit(solution)/shard_map/ppermute | solution.py:180
  8.1 2.6 %collective-permute-start.2 = (f32[64,512]{1,0:T(8,128)S(1)}, f32[64,512]{1,0:T(8,128)S(1)}, u32[]{:S(2)}, u32[]{:S(2)}) collective-permute-start(f32[64,512]{1,0:T(8,128)S(1)} %get-tuple-element.13), channel_id=1, source_target_pairs={{0,1},{1,0},{2,3},{3,2},{4,5},{5,4},{6,7},{7,6},{8,9},{9,8},{10,11... | collective-permute-start | bytes 393224 | tf_op jit(solution)/shard_map/ppermute | solution.py:180
  10.6 2.5 %collective-permute-start.3 = (f32[64,512]{1,0:T(8,128)S(1)}, f32[64,512]{1,0:T(8,128)S(1)}, u32[]{:S(2)}, u32[]{:S(2)}) collective-permute-start(f32[64,512]{1,0:T(8,128)S(1)} %get-tuple-element.15), channel_id=1, source_target_pairs={{0,1},{1,0},{2,3},{3,2},{4,5},{5,4},{6,7},{7,6},{8,9},{9,8},{10,11... | collective-permute-start | bytes 393224 | tf_op jit(solution)/shard_map/ppermute | solution.py:180
  10.7 6.6 %collective-permute-start.4 = (f32[64,512]{1,0:T(8,128)S(1)}, f32[64,512]{1,0:T(8,128)S(1)}, u32[]{:S(2)}, u32[]{:S(2)}) collective-permute-start(f32[64,512]{1,0:T(8,128)S(1)} %add.33.refs_0_), channel_id=1, source_target_pairs={{0,2},{1,3},{2,0},{3,1},{4,6},{5,7},{6,4},{7,5},{8,10},{9,11},{10,... | collective-permute-start | bytes 393224 | tf_op jit(solution)/shard_map/ppermute | solution.py:180
  13.1 6.6 %collective-permute-start.5 = (f32[64,512]{1,0:T(8,128)S(1)}, f32[64,512]{1,0:T(8,128)S(1)}, u32[]{:S(2)}, u32[]{:S(2)}) collective-permute-start(f32[64,512]{1,0:T(8,128)S(1)} %add.34.refs_1_), channel_id=1, source_target_pairs={{0,2},{1,3},{2,0},{3,1},{4,6},{5,7},{6,4},{7,5},{8,10},{9,11},{10,... | collective-permute-start | bytes 393224 | tf_op jit(solution)/shard_map/ppermute | solution.py:180
  20.2 1.5 %collective-permute-start.6 = (f32[5,64,128]{2,1,0:T(8,128)S(1)}, f32[5,64,128]{2,1,0:T(8,128)S(1)}, u32[]{:S(2)}, u32[]{:S(2)}) collective-permute-start(f32[5,64,128]{2,1,0:T(8,128)S(1)} %get-tuple-element.17), channel_id=1, source_target_pairs={{0,1},{1,0},{2,3},{3,2},{4,5},{5,4},{6,7},{7,6},{8,9},{9,8},{10,11... | collective-permute-start | bytes 491528 | tf_op jit(solution)/shard_map/ppermute | solution.py:180
  21.7 4.6 %collective-permute-start.7 = (f32[5,32,128]{2,1,0:T(8,128)S(1)}, f32[5,32,128]{2,1,0:T(8,128)S(1)}, u32[]{:S(2)}, u32[]{:S(2)}) collective-permute-start(f32[5,32,128]{2,1,0:T(8,128)S(1)} %dynamic-slice_add_fusion), channel_id=1, source_target_pairs={{0,4},{4,0},{8,12},{12,8},{16,20},{20,16},{24,28},{28,24},{1,5},{5... | collective-permute-start | bytes 245768 | tf_op jit(solution)/shard_map/ppermute | solution.py:180
  26.3 4.5 %collective-permute-start.8 = (f32[5,32,128]{2,1,0:T(8,128)S(1)}, f32[5,32,128]{2,1,0:T(8,128)S(1)}, u32[]{:S(2)}, u32[]{:S(2)}) collective-permute-start(f32[5,32,128]{2,1,0:T(8,128)S(1)} %add_add_fusion), channel_id=1, source_target_pairs={{0,8},{4,12},{8,0},{12,4},{16,24},{20,28},{24,16},{28,20},{1,9},{5... | collective-permute-start | bytes 245768 | tf_op jit(solution)/shard_map/ppermute | solution.py:180
  30.8 5.4 %collective-permute-start.9 = (f32[5,32,128]{2,1,0:T(8,128)S(1)}, f32[5,32,128]{2,1,0:T(8,128)S(1)}, u32[]{:S(2)}, u32[]{:S(2)}) collective-permute-start(f32[5,32,128]{2,1,0:T(8,128)S(1)} %add.41), channel_id=1, source_target_pairs={{0,16},{4,20},{8,24},{12,28},{16,0},{20,4},{24,8},{28,12},{1,17},{... | collective-permute-start | bytes 245768 | tf_op jit(solution)/shard_map/ppermute | solution.py:180
  36.2 4.5 %collective-permute-start.10 = (f32[5,32,128]{2,1,0:T(8,128)S(1)}, f32[5,32,128]{2,1,0:T(8,128)S(1)}, u32[]{:S(2)}, u32[]{:S(2)}) collective-permute-start(f32[5,32,128]{2,1,0:T(8,128)S(1)} %add.42.refs_0_), channel_id=1, source_target_pairs={{0,4},{4,0},{8,12},{12,8},{16,20},{20,16},{24,28},{28,24},{1,5},{5... | collective-permute-start | bytes 245768 | tf_op jit(solution)/shard_map/ppermute | solution.py:180
  38.0 5.0 %collective-permute-start.11 = (f32[5,32,128]{2,1,0:T(8,128)S(1)}, f32[5,32,128]{2,1,0:T(8,128)S(1)}, u32[]{:S(2)}, u32[]{:S(2)}) collective-permute-start(f32[5,32,128]{2,1,0:T(8,128)S(1)} %add.42.refs_0_), channel_id=1, source_target_pairs={{0,2},{1,3},{2,0},{3,1},{4,6},{5,7},{6,4},{7,5},{8,10},{9,11},{10,... | collective-permute-start | bytes 245768 | tf_op jit(solution)/shard_map/ppermute | solution.py:180
  40.7 4.4 %collective-permute-start.12 = (f32[5,32,128]{2,1,0:T(8,128)S(1)}, f32[5,32,128]{2,1,0:T(8,128)S(1)}, u32[]{:S(2)}, u32[]{:S(2)}) collective-permute-start(f32[5,32,128]{2,1,0:T(8,128)S(1)} %collective-permute-done.10.refs_1_), channel_id=1, source_target_pairs={{0,2},{1,3},{2,0},{3,1},{4,6},{5,7},{6,4},{7,5},{8,10},{9,11},{10,... | collective-permute-start | bytes 245768 | tf_op jit(solution)/shard_map/ppermute | solution.py:180
  42.4 2.7 %collective-permute-start.13 = (f32[5,32,128]{2,1,0:T(8,128)S(1)}, f32[5,32,128]{2,1,0:T(8,128)S(1)}, u32[]{:S(2)}, u32[]{:S(2)}) collective-permute-start(f32[5,32,128]{2,1,0:T(8,128)S(1)} %add.42.refs_0_), channel_id=1, source_target_pairs={{0,1},{1,0},{2,3},{3,2},{4,5},{5,4},{6,7},{7,6},{8,9},{9,8},{10,11... | collective-permute-start | bytes 245768 | tf_op jit(solution)/shard_map/ppermute | solution.py:180
  42.4 2.7 %collective-permute-start.14 = (f32[5,32,128]{2,1,0:T(8,128)S(1)}, f32[5,32,128]{2,1,0:T(8,128)S(1)}, u32[]{:S(2)}, u32[]{:S(2)}) collective-permute-start(f32[5,32,128]{2,1,0:T(8,128)S(1)} %collective-permute-done.10.refs_1_), channel_id=1, source_target_pairs={{0,1},{1,0},{2,3},{3,2},{4,5},{5,4},{6,7},{7,6},{8,9},{9,8},{10,11... | collective-permute-start | bytes 245768 | tf_op jit(solution)/shard_map/ppermute | solution.py:180
  43.0 2.2 %collective-permute-start.15 = (f32[5,32,128]{2,1,0:T(8,128)S(1)}, f32[5,32,128]{2,1,0:T(8,128)S(1)}, u32[]{:S(2)}, u32[]{:S(2)}) collective-permute-start(f32[5,32,128]{2,1,0:T(8,128)S(1)} %collective-permute-done.11.refs_2_), channel_id=1, source_target_pairs={{0,1},{1,0},{2,3},{3,2},{4,5},{5,4},{6,7},{7,6},{8,9},{9,8},{10,11... | collective-permute-start | bytes 245768 | tf_op jit(solution)/shard_map/ppermute | solution.py:180
  45.1 1.3 %collective-permute-start.16 = (f32[5,32,128]{2,1,0:T(8,128)S(1)}, f32[5,32,128]{2,1,0:T(8,128)S(1)}, u32[]{:S(2)}, u32[]{:S(2)}) collective-permute-start(f32[5,32,128]{2,1,0:T(8,128)S(1)} %collective-permute-done.12.refs_3_), channel_id=1, source_target_pairs={{0,1},{1,0},{2,3},{3,2},{4,5},{5,4},{6,7},{7,6},{8,9},{9,8},{10,11... | collective-permute-start | bytes 245768 | tf_op jit(solution)/shard_map/ppermute | solution.py:180

commit v8 on v7

--- a/solution.py
+++ b/solution.py
@@ -141,12 +141,12 @@
         piece_refs, (r_ref, w_ref, x_ref) = refs[:len(pieces)], refs[len(pieces):]
         w = lax.axis_index("wave")
         y = lax.axis_index("spec") % 2
+        blocks = {}
         for ref, (dw, dy) in zip(piece_refs, offsets):
-            v = w ^ dw
-            core, x = v % 2, v // 2
-            row = pl.multiple_of(core * (T // 2) + (y ^ dy) * part, part)
-            for t in range(slots):
-                i, j = blocks_of(x, slots, t, nb)
+            if dw // 2 not in blocks:
+                blocks[dw // 2] = [blocks_of((w // 2) ^ (dw // 2), slots, t, nb) for t in range(slots)]
+            row = ((w % 2) ^ (dw % 2)) * (T // 2) + (y ^ dy) * part
+            for t, (i, j) in enumerate(blocks[dw // 2]):
                 w_ref[pl.ds(pl.multiple_of(i + row, part), part), pl.ds(j, T)] = ref[t]
         for b in range(1, nb):
             r_ref[b * T:(b + 1) * T, 0:b * T] = jnp.zeros((T, b * T), jnp.float32)
@@ -217,7 +217,7 @@
     return factor(pieces, offsets, slots, k)
 
 
-CHUNK = 64
+CHUNK = 32
 
 
 def bell(offset, half_amplitude, inverse_width, wing):

time: 60.1 us -> 60.1 us (level)
  no operation moved by 1% of the time
where the time goes in v8:
time: 60.1 us; the launch traced here: 59.8 us
  waiting for transfers between devices  19.9 us (33%)
  starting transfers between devices  19.4 us (32%)
  Pallas kernels  19 us (32%)
  other arithmetic  0.82 us (1%)
  between operations  0.75 us (1%)
    ppermute x16, waiting for transfers between devices, swap(): lax.ppermute(x, axis, [(i, i ^ bit) for i in range(lax.axis_size(axis))])  19.6 us
    ppermute x16, starting transfers between devices, swap(): lax.ppermute(x, axis, [(i, i ^ bit) for i in range(lax.axis_size(axis))])  16.9 us
    pallas_call x1, Pallas kernels, factor(): pl.pallas_call(body, name='factor', out_shape=jax.ShapeDtypeStruct((n, n)...  13.4 us
    pallas_call x2, Pallas kernels, front(): pl.pallas_call(body, name='front', in_specs=[HBM] * 4 + [VMEM] * 3 + [HBM...  3.68 us
    ppermute x1, starting transfers between devices, shards(): over_x = lax.ppermute(own, 'wave', across)  2.44 us
    pallas_call x1, Pallas kernels, line_table(): pl.pallas_call(body, name='lines', in_specs=[HBM] * 6, out_specs=VMEM, ou...  1.42 us
  transfers between devices with their start and end apart: 17, of which 11 were waited for; matrix products, arithmetic and copies ran while one was open for 1% of the time, Pallas kernels for 3%

profile of v8, /device:TPU:0, one launch (start us, length us, event | category | flops | bytes accessed | tf_op | source)
XLA Modules:
  0.0 59.8 jit_solution(13399560269052548075)
XLA Ops:
  0.6 1.4 %lines.1 = f32[16,256]{1,0:T(8,128)} custom-call(s32[4,256]{1,0:T(4,128)} %bitcast.7, s32[4,256]{1,0:T(4,128)} %bitcast.8, f32[4,256]{1,0:T(4,128)} %bitcast.9, s32[1,256]{1,0:T(1,128)} %bitcast.10, f32[32]{0:T(128)} %strength_ref.1, f32[32]{0:T(128)} %widths_ref.1), custom_call_target="tpu_custom_call" | custom-call | tf_op jit(solution)/shard_map/lines/pallas_call | solution.py:262
  2.1 0.0 copy-start
  2.1 0.0 copy-start.1
  2.1 2.4 %collective-permute-start.1 = (f32[16,256]{1,0:T(8,128)}, f32[16,256]{1,0:T(8,128)S(1)}, u32[]{:S(2)}, u32[]{:S(2)}) collective-permute-start(f32[16,256]{1,0:T(8,128)} %lines.1), channel_id=1, source_target_pairs={{0,3},{1,2},{2,1},{3,0},{4,7},{5,6},{6,5},{7,4},{8,11},{9,10},{10,... | collective-permute-start | bytes 49160 | tf_op jit(solution)/shard_map/ppermute | solution.py:357
  4.5 0.7 %collective-permute-start = (f32[16,256]{1,0:T(8,128)}, f32[16,256]{1,0:T(8,128)S(1)}, u32[]{:S(2)}, u32[]{:S(2)}) collective-permute-start(f32[16,256]{1,0:T(8,128)} %lines.1), channel_id=1, source_target_pairs={{0,1},{1,0},{2,3},{3,2},{4,5},{5,4},{6,7},{7,6},{8,9},{9,8},{10,11... | collective-permute-start | bytes 49160 | tf_op jit(solution)/shard_map/ppermute | solution.py:180
  5.2 0.7 %broadcast_maximum_fusion.own_ref = f32[16,256]{1,0:T(8,128)S(1)} fusion(f32[16,256]{1,0:T(8,128)} %lines.1), kind=kLoop, calls=%fused_computation.2 | loop fusion | flops 4096 | bytes 32768 | tf_op jit(solution)/shard_map/max | solution.py:359
  5.9 0.3 collective-permute-done.1.x_ref
  6.2 0.1 collective-permute-done.core_ref
  6.2 0.0 copy-done
  6.3 0.0 copy-done.1
  6.3 1.8 %front.2 = (bf16[256,512]{1,0:T(8,128)(2,1)}, f32[64,512]{1,0:T(8,128)S(1)}, f32[64,512]{1,0:T(8,128)S(1)}) custom-call(bf16[256,512]{1,0:T(8,128)(2,1)} %flux_hbm.3, bf16[16,256]{1,0:T(8,128)(2,1)S(1)} %bitcast.5, bf16[16,512]{1,0:T(8,128)(2,1)S(1)} %copy-done, bf16[512,512]{1,0:T(8,128)(2,1)} %m_hbm.3, f32[16,256]{1,0:T(8,128)S(1)} %broadcast_maximum_fusion.own_ref, ...), custom_call_target="tpu_custom_call" | custom-call | flops 67108864 | bytes 786432 | tf_op jit(solution)/shard_map/front/pallas_call | solution.py:328
  8.1 0.7 %collective-permute-start.2 = (f32[64,512]{1,0:T(8,128)S(1)}, f32[64,512]{1,0:T(8,128)S(1)}, u32[]{:S(2)}, u32[]{:S(2)}) collective-permute-start(f32[64,512]{1,0:T(8,128)S(1)} %get-tuple-element.13), channel_id=1, source_target_pairs={{0,1},{1,0},{2,3},{3,2},{4,5},{5,4},{6,7},{7,6},{8,9},{9,8},{10,11... | collective-permute-start | bytes 393224 | tf_op jit(solution)/shard_map/ppermute | solution.py:180
  8.8 1.8 %front.3 = (bf16[256,512]{1,0:T(8,128)(2,1)}, f32[64,512]{1,0:T(8,128)S(1)}, f32[64,512]{1,0:T(8,128)S(1)}) custom-call(bf16[256,512]{1,0:T(8,128)(2,1)} %flux_hbm.3, bf16[16,256]{1,0:T(8,128)(2,1)S(1)} %bitcast.6, bf16[16,512]{1,0:T(8,128)(2,1)S(1)} %copy-done, bf16[512,512]{1,0:T(8,128)(2,1)} %m_hbm.3, ...), custom_call_target="tpu_custom_call", output_to_operand_aliasing={{0}: (7, {})} | custom-call | flops 67108864 | bytes 786432 | tf_op jit(solution)/shard_map/front/pallas_call | solution.py:328
  10.6 0.1 collective-permute-start.3
  10.7 0.0 collective-permute-done.2
  10.7 2.3 %collective-permute-start.4 = (f32[64,512]{1,0:T(8,128)S(1)}, f32[64,512]{1,0:T(8,128)S(1)}, u32[]{:S(2)}, u32[]{:S(2)}) collective-permute-start(f32[64,512]{1,0:T(8,128)S(1)} %add.33.refs_0_), channel_id=1, source_target_pairs={{0,2},{1,3},{2,0},{3,1},{4,6},{5,7},{6,4},{7,5},{8,10},{9,11},{10,... | collective-permute-start | bytes 393224 | tf_op jit(solution)/shard_map/ppermute | solution.py:180
  13.1 0.0 collective-permute-done.3
  13.1 1.0 %collective-permute-start.5 = (f32[64,512]{1,0:T(8,128)S(1)}, f32[64,512]{1,0:T(8,128)S(1)}, u32[]{:S(2)}, u32[]{:S(2)}) collective-permute-start(f32[64,512]{1,0:T(8,128)S(1)} %add.34.refs_1_), channel_id=1, source_target_pairs={{0,2},{1,3},{2,0},{3,1},{4,6},{5,7},{6,4},{7,5},{8,10},{9,11},{10,... | collective-permute-start | bytes 393224 | tf_op jit(solution)/shard_map/ppermute | solution.py:180
  14.1 3.3 %collective-permute-done.4.refs_2_ = f32[64,512]{1,0:T(8,128)S(1)} collective-permute-done((f32[64,512]{1,0:T(8,128)S(1)}, f32[64,512]{1,0:T(8,128)S(1)}, u32[]{:S(2)}, u32[]{:S(2)}) %collective-permute-start.4) | collective-permute-done | bytes 131104 | tf_op jit(solution)/shard_map/ppermute | solution.py:180
  17.3 2.3 %collective-permute-done.5.refs_3_ = f32[64,512]{1,0:T(8,128)S(1)} collective-permute-done((f32[64,512]{1,0:T(8,128)S(1)}, f32[64,512]{1,0:T(8,128)S(1)}, u32[]{:S(2)}, u32[]{:S(2)}) %collective-permute-start.5) | collective-permute-done | bytes 131104 | tf_op jit(solution)/shard_map/ppermute | solution.py:180
  19.6 0.5 gram.1
  20.2 0.1 collective-permute-start.6
  20.3 1.4 %collective-permute-done.6 = f32[5,64,128]{2,1,0:T(8,128)S(1)} collective-permute-done((f32[5,64,128]{2,1,0:T(8,128)S(1)}, f32[5,64,128]{2,1,0:T(8,128)S(1)}, u32[]{:S(2)}, u32[]{:S(2)}) %collective-permute-start.6) | collective-permute-done | bytes 163872 | tf_op jit(solution)/shard_map/ppermute | solution.py:180
  21.7 1.8 %collective-permute-start.7 = (f32[5,32,128]{2,1,0:T(8,128)S(1)}, f32[5,32,128]{2,1,0:T(8,128)S(1)}, u32[]{:S(2)}, u32[]{:S(2)}) collective-permute-start(f32[5,32,128]{2,1,0:T(8,128)S(1)} %dynamic-slice_add_fusion), channel_id=1, source_target_pairs={{0,4},{4,0},{8,12},{12,8},{16,20},{20,16},{24,28},{28,24},{1,5},{5... | collective-permute-start | bytes 245768 | tf_op jit(solution)/shard_map/ppermute | solution.py:180
  23.5 2.8 %collective-permute-done.7 = f32[5,32,128]{2,1,0:T(8,128)S(1)} collective-permute-done((f32[5,32,128]{2,1,0:T(8,128)S(1)}, f32[5,32,128]{2,1,0:T(8,128)S(1)}, u32[]{:S(2)}, u32[]{:S(2)}) %collective-permute-start.7) | collective-permute-done | bytes 81952 | tf_op jit(solution)/shard_map/ppermute | solution.py:180
  26.3 1.9 %collective-permute-start.8 = (f32[5,32,128]{2,1,0:T(8,128)S(1)}, f32[5,32,128]{2,1,0:T(8,128)S(1)}, u32[]{:S(2)}, u32[]{:S(2)}) collective-permute-start(f32[5,32,128]{2,1,0:T(8,128)S(1)} %add_add_fusion), channel_id=1, source_target_pairs={{0,8},{4,12},{8,0},{12,4},{16,24},{20,28},{24,16},{28,20},{1,9},{5... | collective-permute-start | bytes 245768 | tf_op jit(solution)/shard_map/ppermute | solution.py:180
  28.1 2.6 %collective-permute-done.8 = f32[5,32,128]{2,1,0:T(8,128)S(1)} collective-permute-done((f32[5,32,128]{2,1,0:T(8,128)S(1)}, f32[5,32,128]{2,1,0:T(8,128)S(1)}, u32[]{:S(2)}, u32[]{:S(2)}) %collective-permute-start.8) | collective-permute-done | bytes 81952 | tf_op jit(solution)/shard_map/ppermute | solution.py:180
  30.8 2.9 %collective-permute-start.9 = (f32[5,32,128]{2,1,0:T(8,128)S(1)}, f32[5,32,128]{2,1,0:T(8,128)S(1)}, u32[]{:S(2)}, u32[]{:S(2)}) collective-permute-start(f32[5,32,128]{2,1,0:T(8,128)S(1)} %add.41), channel_id=1, source_target_pairs={{0,16},{4,20},{8,24},{12,28},{16,0},{20,4},{24,8},{28,12},{1,17},{... | collective-permute-start | bytes 245768 | tf_op jit(solution)/shard_map/ppermute | solution.py:180
  33.6 2.5 %collective-permute-done.9 = f32[5,32,128]{2,1,0:T(8,128)S(1)} collective-permute-done((f32[5,32,128]{2,1,0:T(8,128)S(1)}, f32[5,32,128]{2,1,0:T(8,128)S(1)}, u32[]{:S(2)}, u32[]{:S(2)}) %collective-permute-start.9) | collective-permute-done | bytes 81952 | tf_op jit(solution)/shard_map/ppermute | solution.py:180
  36.2 1.8 %collective-permute-start.10 = (f32[5,32,128]{2,1,0:T(8,128)S(1)}, f32[5,32,128]{2,1,0:T(8,128)S(1)}, u32[]{:S(2)}, u32[]{:S(2)}) collective-permute-start(f32[5,32,128]{2,1,0:T(8,128)S(1)} %add.42.refs_0_), channel_id=1, source_target_pairs={{0,4},{4,0},{8,12},{12,8},{16,20},{20,16},{24,28},{28,24},{1,5},{5... | collective-permute-start | bytes 245768 | tf_op jit(solution)/shard_map/ppermute | solution.py:180
  38.0 1.5 %collective-permute-start.11 = (f32[5,32,128]{2,1,0:T(8,128)S(1)}, f32[5,32,128]{2,1,0:T(8,128)S(1)}, u32[]{:S(2)}, u32[]{:S(2)}) collective-permute-start(f32[5,32,128]{2,1,0:T(8,128)S(1)} %add.42.refs_0_), channel_id=1, source_target_pairs={{0,2},{1,3},{2,0},{3,1},{4,6},{5,7},{6,4},{7,5},{8,10},{9,11},{10,... | collective-permute-start | bytes 245768 | tf_op jit(solution)/shard_map/ppermute | solution.py:180
  39.5 1.2 %collective-permute-done.10.refs_1_ = f32[5,32,128]{2,1,0:T(8,128)S(1)} collective-permute-done((f32[5,32,128]{2,1,0:T(8,128)S(1)}, f32[5,32,128]{2,1,0:T(8,128)S(1)}, u32[]{:S(2)}, u32[]{:S(2)}) %collective-permute-start.10) | collective-permute-done | bytes 81952 | tf_op jit(solution)/shard_map/ppermute | solution.py:180
  40.7 1.7 %collective-permute-start.12 = (f32[5,32,128]{2,1,0:T(8,128)S(1)}, f32[5,32,128]{2,1,0:T(8,128)S(1)}, u32[]{:S(2)}, u32[]{:S(2)}) collective-permute-start(f32[5,32,128]{2,1,0:T(8,128)S(1)} %collective-permute-done.10.refs_1_), channel_id=1, source_target_pairs={{0,2},{1,3},{2,0},{3,1},{4,6},{5,7},{6,4},{7,5},{8,10},{9,11},{10,... | collective-permute-start | bytes 245768 | tf_op jit(solution)/shard_map/ppermute | solution.py:180
  42.4 0.0 collective-permute-start.13
  42.4 0.5 collective-permute-start.14
  43.0 0.0 collective-permute-done.11.refs_2_
  43.0 0.0 collective-permute-start.15
  43.0 2.2 %collective-permute-done.12.refs_3_ = f32[5,32,128]{2,1,0:T(8,128)S(1)} collective-permute-done((f32[5,32,128]{2,1,0:T(8,128)S(1)}, f32[5,32,128]{2,1,0:T(8,128)S(1)}, u32[]{:S(2)}, u32[]{:S(2)}) %collective-permute-start.12) | collective-permute-done | bytes 81952 | tf_op jit(solution)/shard_map/ppermute | solution.py:180
  45.1 0.0 collective-permute-start.16
  45.1 0.0 collective-permute-done.13.refs_4_
  45.2 0.0 collective-permute-done.15.refs_6_
  45.2 0.0 collective-permute-done.14.refs_5_
  45.2 1.3 %collective-permute-done.16.refs_7_ = f32[5,32,128]{2,1,0:T(8,128)S(1)} collective-permute-done((f32[5,32,128]{2,1,0:T(8,128)S(1)}, f32[5,32,128]{2,1,0:T(8,128)S(1)}, u32[]{:S(2)}, u32[]{:S(2)}) %collective-permute-start.16) | collective-permute-done | bytes 81952 | tf_op jit(solution)/shard_map/ppermute | solution.py:180
  46.4 13.4 %factor.1 = f32[512,512]{1,0:T(8,128)} custom-call(f32[5,32,128]{2,1,0:T(8,128)S(1)} %add.42.refs_0_, f32[5,32,128]{2,1,0:T(8,128)S(1)} %collective-permute-done.10.refs_1_, f32[5,32,128]{2,1,0:T(8,128)S(1)} %collective-permute-done.11.refs_2_, f32[5,32,128]{2,1,0:T(8,128)S(1)} %collective-permute-done.12.refs_3_, ...), custom_call_target="tpu_custom_call" | custom-call | tf_op jit(solution)/shard_map/factor/pallas_call | solution.py:172
  (6 shorter events, 0.1 us)
Async XLA Ops:
  2.1 4.2 %copy-start = (bf16[16,512]{1,0:T(8,128)(2,1)S(1)}, bf16[16,512]{1,0:T(8,128)(2,1)}, u32[]{:S(2)}) copy-start(bf16[16,512]{1,0:T(8,128)(2,1)} %basis_hbm.3) | copy-start | bytes 49156
  2.1 4.2 %copy-start.1 = (bf16[256,16]{0,1:T(8,128)(2,1)S(1)}, bf16[256,16]{0,1:T(8,128)(2,1)}, u32[]{:S(2)}) copy-start(bf16[256,16]{0,1:T(8,128)(2,1)} %param.11) | copy-start | bytes 24580
  2.1 4.1 %collective-permute-start.1 = (f32[16,256]{1,0:T(8,128)}, f32[16,256]{1,0:T(8,128)S(1)}, u32[]{:S(2)}, u32[]{:S(2)}) collective-permute-start(f32[16,256]{1,0:T(8,128)} %lines.1), channel_id=1, source_target_pairs={{0,3},{1,2},{2,1},{3,0},{4,7},{5,6},{6,5},{7,4},{8,11},{9,10},{10,... | collective-permute-start | bytes 49160 | tf_op jit(solution)/shard_map/ppermute | solution.py:357
  4.5 1.7 %collective-permute-start = (f32[16,256]{1,0:T(8,128)}, f32[16,256]{1,0:T(8,128)S(1)}, u32[]{:S(2)}, u32[]{:S(2)}) collective-permute-start(f32[16,256]{1,0:T(8,128)} %lines.1), channel_id=1, source_target_pairs={{0,1},{1,0},{2,3},{3,2},{4,5},{5,4},{6,7},{7,6},{8,9},{9,8},{10,11... | collective-permute-start | bytes 49160 | tf_op jit(solution)/shard_map/ppermute | solution.py:180
  8.1 2.6 %collective-permute-start.2 = (f32[64,512]{1,0:T(8,128)S(1)}, f32[64,512]{1,0:T(8,128)S(1)}, u32[]{:S(2)}, u32[]{:S(2)}) collective-permute-start(f32[64,512]{1,0:T(8,128)S(1)} %get-tuple-element.13), channel_id=1, source_target_pairs={{0,1},{1,0},{2,3},{3,2},{4,5},{5,4},{6,7},{7,6},{8,9},{9,8},{10,11... | collective-permute-start | bytes 393224 | tf_op jit(solution)/shard_map/ppermute | solution.py:180
  10.6 2.5 %collective-permute-start.3 = (f32[64,512]{1,0:T(8,128)S(1)}, f32[64,512]{1,0:T(8,128)S(1)}, u32[]{:S(2)}, u32[]{:S(2)}) collective-permute-start(f32[64,512]{1,0:T(8,128)S(1)} %get-tuple-element.15), channel_id=1, source_target_pairs={{0,1},{1,0},{2,3},{3,2},{4,5},{5,4},{6,7},{7,6},{8,9},{9,8},{10,11... | collective-permute-start | bytes 393224 | tf_op jit(solution)/shard_map/ppermute | solution.py:180
  10.7 6.6 %collective-permute-start.4 = (f32[64,512]{1,0:T(8,128)S(1)}, f32[64,512]{1,0:T(8,128)S(1)}, u32[]{:S(2)}, u32[]{:S(2)}) collective-permute-start(f32[64,512]{1,0:T(8,128)S(1)} %add.33.refs_0_), channel_id=1, source_target_pairs={{0,2},{1,3},{2,0},{3,1},{4,6},{5,7},{6,4},{7,5},{8,10},{9,11},{10,... | collective-permute-start | bytes 393224 | tf_op jit(solution)/shard_map/ppermute | solution.py:180
  13.1 6.6 %collective-permute-start.5 = (f32[64,512]{1,0:T(8,128)S(1)}, f32[64,512]{1,0:T(8,128)S(1)}, u32[]{:S(2)}, u32[]{:S(2)}) collective-permute-start(f32[64,512]{1,0:T(8,128)S(1)} %add.34.refs_1_), channel_id=1, source_target_pairs={{0,2},{1,3},{2,0},{3,1},{4,6},{5,7},{6,4},{7,5},{8,10},{9,11},{10,... | collective-permute-start | bytes 393224 | tf_op jit(solution)/shard_map/ppermute | solution.py:180
  20.2 1.5 %collective-permute-start.6 = (f32[5,64,128]{2,1,0:T(8,128)S(1)}, f32[5,64,128]{2,1,0:T(8,128)S(1)}, u32[]{:S(2)}, u32[]{:S(2)}) collective-permute-start(f32[5,64,128]{2,1,0:T(8,128)S(1)} %get-tuple-element.17), channel_id=1, source_target_pairs={{0,1},{1,0},{2,3},{3,2},{4,5},{5,4},{6,7},{7,6},{8,9},{9,8},{10,11... | collective-permute-start | bytes 491528 | tf_op jit(solution)/shard_map/ppermute | solution.py:180
  21.7 4.6 %collective-permute-start.7 = (f32[5,32,128]{2,1,0:T(8,128)S(1)}, f32[5,32,128]{2,1,0:T(8,128)S(1)}, u32[]{:S(2)}, u32[]{:S(2)}) collective-permute-start(f32[5,32,128]{2,1,0:T(8,128)S(1)} %dynamic-slice_add_fusion), channel_id=1, source_target_pairs={{0,4},{4,0},{8,12},{12,8},{16,20},{20,16},{24,28},{28,24},{1,5},{5... | collective-permute-start | bytes 245768 | tf_op jit(solution)/shard_map/ppermute | solution.py:180
  26.3 4.5 %collective-permute-start.8 = (f32[5,32,128]{2,1,0:T(8,128)S(1)}, f32[5,32,128]{2,1,0:T(8,128)S(1)}, u32[]{:S(2)}, u32[]{:S(2)}) collective-permute-start(f32[5,32,128]{2,1,0:T(8,128)S(1)} %add_add_fusion), channel_id=1, source_target_pairs={{0,8},{4,12},{8,0},{12,4},{16,24},{20,28},{24,16},{28,20},{1,9},{5... | collective-permute-start | bytes 245768 | tf_op jit(solution)/shard_map/ppermute | solution.py:180
  30.8 5.4 %collective-permute-start.9 = (f32[5,32,128]{2,1,0:T(8,128)S(1)}, f32[5,32,128]{2,1,0:T(8,128)S(1)}, u32[]{:S(2)}, u32[]{:S(2)}) collective-permute-start(f32[5,32,128]{2,1,0:T(8,128)S(1)} %add.41), channel_id=1, source_target_pairs={{0,16},{4,20},{8,24},{12,28},{16,0},{20,4},{24,8},{28,12},{1,17},{... | collective-permute-start | bytes 245768 | tf_op jit(solution)/shard_map/ppermute | solution.py:180
  36.2 4.5 %collective-permute-start.10 = (f32[5,32,128]{2,1,0:T(8,128)S(1)}, f32[5,32,128]{2,1,0:T(8,128)S(1)}, u32[]{:S(2)}, u32[]{:S(2)}) collective-permute-start(f32[5,32,128]{2,1,0:T(8,128)S(1)} %add.42.refs_0_), channel_id=1, source_target_pairs={{0,4},{4,0},{8,12},{12,8},{16,20},{20,16},{24,28},{28,24},{1,5},{5... | collective-permute-start | bytes 245768 | tf_op jit(solution)/shard_map/ppermute | solution.py:180
  38.0 5.0 %collective-permute-start.11 = (f32[5,32,128]{2,1,0:T(8,128)S(1)}, f32[5,32,128]{2,1,0:T(8,128)S(1)}, u32[]{:S(2)}, u32[]{:S(2)}) collective-permute-start(f32[5,32,128]{2,1,0:T(8,128)S(1)} %add.42.refs_0_), channel_id=1, source_target_pairs={{0,2},{1,3},{2,0},{3,1},{4,6},{5,7},{6,4},{7,5},{8,10},{9,11},{10,... | collective-permute-start | bytes 245768 | tf_op jit(solution)/shard_map/ppermute | solution.py:180
  40.7 4.4 %collective-permute-start.12 = (f32[5,32,128]{2,1,0:T(8,128)S(1)}, f32[5,32,128]{2,1,0:T(8,128)S(1)}, u32[]{:S(2)}, u32[]{:S(2)}) collective-permute-start(f32[5,32,128]{2,1,0:T(8,128)S(1)} %collective-permute-done.10.refs_1_), channel_id=1, source_target_pairs={{0,2},{1,3},{2,0},{3,1},{4,6},{5,7},{6,4},{7,5},{8,10},{9,11},{10,... | collective-permute-start | bytes 245768 | tf_op jit(solution)/shard_map/ppermute | solution.py:180
  42.4 2.7 %collective-permute-start.13 = (f32[5,32,128]{2,1,0:T(8,128)S(1)}, f32[5,32,128]{2,1,0:T(8,128)S(1)}, u32[]{:S(2)}, u32[]{:S(2)}) collective-permute-start(f32[5,32,128]{2,1,0:T(8,128)S(1)} %add.42.refs_0_), channel_id=1, source_target_pairs={{0,1},{1,0},{2,3},{3,2},{4,5},{5,4},{6,7},{7,6},{8,9},{9,8},{10,11... | collective-permute-start | bytes 245768 | tf_op jit(solution)/shard_map/ppermute | solution.py:180
  42.4 2.7 %collective-permute-start.14 = (f32[5,32,128]{2,1,0:T(8,128)S(1)}, f32[5,32,128]{2,1,0:T(8,128)S(1)}, u32[]{:S(2)}, u32[]{:S(2)}) collective-permute-start(f32[5,32,128]{2,1,0:T(8,128)S(1)} %collective-permute-done.10.refs_1_), channel_id=1, source_target_pairs={{0,1},{1,0},{2,3},{3,2},{4,5},{5,4},{6,7},{7,6},{8,9},{9,8},{10,11... | collective-permute-start | bytes 245768 | tf_op jit(solution)/shard_map/ppermute | solution.py:180
  43.0 2.2 %collective-permute-start.15 = (f32[5,32,128]{2,1,0:T(8,128)S(1)}, f32[5,32,128]{2,1,0:T(8,128)S(1)}, u32[]{:S(2)}, u32[]{:S(2)}) collective-permute-start(f32[5,32,128]{2,1,0:T(8,128)S(1)} %collective-permute-done.11.refs_2_), channel_id=1, source_target_pairs={{0,1},{1,0},{2,3},{3,2},{4,5},{5,4},{6,7},{7,6},{8,9},{9,8},{10,11... | collective-permute-start | bytes 245768 | tf_op jit(solution)/shard_map/ppermute | solution.py:180
  45.1 1.3 %collective-permute-start.16 = (f32[5,32,128]{2,1,0:T(8,128)S(1)}, f32[5,32,128]{2,1,0:T(8,128)S(1)}, u32[]{:S(2)}, u32[]{:S(2)}) collective-permute-start(f32[5,32,128]{2,1,0:T(8,128)S(1)} %collective-permute-done.12.refs_3_), channel_id=1, source_target_pairs={{0,1},{1,0},{2,3},{3,2},{4,5},{5,4},{6,7},{7,6},{8,9},{9,8},{10,11... | collective-permute-start | bytes 245768 | tf_op jit(solution)/shard_map/ppermute | solution.py:180

commit v9 on v8

--- a/solution.py
+++ b/solution.py
@@ -223,8 +223,17 @@
 def bell(offset, half_amplitude, inverse_width, wing):
     u = offset * inverse_width
     square = u * u
-    value = half_amplitude * (1.0 / (1.0 + square) + jnp.exp2(-square))
-    return jnp.where(jnp.abs(offset) <= wing, value, 0.0)
+    height = jnp.where(jnp.abs(offset) <= wing, half_amplitude, 0.0)
+    return height, 1.0 + square, height * jnp.exp2(-square)
+
+
+def summed(bells):
+    total = sum(b[2] for b in bells[1:]) + bells[0][2]
+    for (p, q, _), (r, s, _) in zip(bells[::2], bells[1::2]):
+        total = total + (p * s + r * q) / (q * s)
+    if len(bells) % 2:
+        total = total + bells[-1][0] / bells[-1][1]
+    return total
 
 
 PARTS = 2
@@ -289,13 +298,12 @@
 
         def depth(ref, start, height):
             at = lax.broadcasted_iota(jnp.int32, (height, count), 0).astype(jnp.float32) + start
-            total = None
+            bells = []
             for a in range(absorbers):
                 centre, amplitude, inverse = (
                     ref[i * absorbers + a:i * absorbers + a + 1, mine] for i in range(3))
-                term = bell(at - centre, amplitude, inverse, wing_row)
-                total = term if total is None else total + term
-            return total
+                bells.append(bell(at - centre, amplitude, inverse, wing_row))
+            return summed(bells)
 
         def chunk(i, _):
             row = pl.multiple_of(i * CHUNK, CHUNK)

time: 60.1 us -> 60.1 us (level)
  no operation moved by 1% of the time
where the time goes in v9:
time: 60.1 us; the launch traced here: 59.8 us
  waiting for transfers between devices  19.9 us (33%)
  starting transfers between devices  19.4 us (32%)
  Pallas kernels  19 us (32%)
  other arithmetic  0.82 us (1%)
  between operations  0.75 us (1%)
    ppermute x16, waiting for transfers between devices, swap(): lax.ppermute(x, axis, [(i, i ^ bit) for i in range(lax.axis_size(axis))])  19.6 us
    ppermute x16, starting transfers between devices, swap(): lax.ppermute(x, axis, [(i, i ^ bit) for i in range(lax.axis_size(axis))])  16.9 us
    pallas_call x1, Pallas kernels, factor(): pl.pallas_call(body, name='factor', out_shape=jax.ShapeDtypeStruct((n, n)...  13.4 us
    pallas_call x2, Pallas kernels, front(): pl.pallas_call(body, name='front', in_specs=[HBM] * 4 + [VMEM] * 3 + [HBM...  3.68 us
    ppermute x1, starting transfers between devices, shards(): over_x = lax.ppermute(own, 'wave', across)  2.44 us
    pallas_call x1, Pallas kernels, line_table(): pl.pallas_call(body, name='lines', in_specs=[HBM] * 6, out_specs=VMEM, ou...  1.42 us
  transfers between devices with their start and end apart: 17, of which 11 were waited for; matrix products, arithmetic and copies ran while one was open for 1% of the time, Pallas kernels for 3%

profile of v9, /device:TPU:0, one launch (start us, length us, event | category | flops | bytes accessed | tf_op | source)
XLA Modules:
  0.0 59.8 jit_solution(6058994633547410357)
XLA Ops:
  0.6 1.4 %lines.1 = f32[16,256]{1,0:T(8,128)} custom-call(s32[4,256]{1,0:T(4,128)} %bitcast.7, s32[4,256]{1,0:T(4,128)} %bitcast.8, f32[4,256]{1,0:T(4,128)} %bitcast.9, s32[1,256]{1,0:T(1,128)} %bitcast.10, f32[32]{0:T(128)} %strength_ref.1, f32[32]{0:T(128)} %widths_ref.1), custom_call_target="tpu_custom_call" | custom-call | tf_op jit(solution)/shard_map/lines/pallas_call | solution.py:271
  2.1 0.0 copy-start
  2.1 0.0 copy-start.1
  2.1 2.4 %collective-permute-start.1 = (f32[16,256]{1,0:T(8,128)}, f32[16,256]{1,0:T(8,128)S(1)}, u32[]{:S(2)}, u32[]{:S(2)}) collective-permute-start(f32[16,256]{1,0:T(8,128)} %lines.1), channel_id=1, source_target_pairs={{0,3},{1,2},{2,1},{3,0},{4,7},{5,6},{6,5},{7,4},{8,11},{9,10},{10,... | collective-permute-start | bytes 49160 | tf_op jit(solution)/shard_map/ppermute | solution.py:365
  4.5 0.7 %collective-permute-start = (f32[16,256]{1,0:T(8,128)}, f32[16,256]{1,0:T(8,128)S(1)}, u32[]{:S(2)}, u32[]{:S(2)}) collective-permute-start(f32[16,256]{1,0:T(8,128)} %lines.1), channel_id=1, source_target_pairs={{0,1},{1,0},{2,3},{3,2},{4,5},{5,4},{6,7},{7,6},{8,9},{9,8},{10,11... | collective-permute-start | bytes 49160 | tf_op jit(solution)/shard_map/ppermute | solution.py:180
  5.2 0.7 %broadcast_maximum_fusion.own_ref = f32[16,256]{1,0:T(8,128)S(1)} fusion(f32[16,256]{1,0:T(8,128)} %lines.1), kind=kLoop, calls=%fused_computation.2 | loop fusion | flops 4096 | bytes 32768 | tf_op jit(solution)/shard_map/max | solution.py:367
  5.9 0.3 collective-permute-done.1.x_ref
  6.2 0.1 collective-permute-done.core_ref
  6.2 0.0 copy-done
  6.3 0.0 copy-done.1
  6.3 1.8 %front.2 = (bf16[256,512]{1,0:T(8,128)(2,1)}, f32[64,512]{1,0:T(8,128)S(1)}, f32[64,512]{1,0:T(8,128)S(1)}) custom-call(bf16[256,512]{1,0:T(8,128)(2,1)} %flux_hbm.3, bf16[16,256]{1,0:T(8,128)(2,1)S(1)} %bitcast.5, bf16[16,512]{1,0:T(8,128)(2,1)S(1)} %copy-done, bf16[512,512]{1,0:T(8,128)(2,1)} %m_hbm.3, f32[16,256]{1,0:T(8,128)S(1)} %broadcast_maximum_fusion.own_ref, ...), custom_call_target="tpu_custom_call" | custom-call | flops 67108864 | bytes 786432 | tf_op jit(solution)/shard_map/front/pallas_call | solution.py:336
  8.1 0.7 %collective-permute-start.2 = (f32[64,512]{1,0:T(8,128)S(1)}, f32[64,512]{1,0:T(8,128)S(1)}, u32[]{:S(2)}, u32[]{:S(2)}) collective-permute-start(f32[64,512]{1,0:T(8,128)S(1)} %get-tuple-element.13), channel_id=1, source_target_pairs={{0,1},{1,0},{2,3},{3,2},{4,5},{5,4},{6,7},{7,6},{8,9},{9,8},{10,11... | collective-permute-start | bytes 393224 | tf_op jit(solution)/shard_map/ppermute | solution.py:180
  8.8 1.8 %front.3 = (bf16[256,512]{1,0:T(8,128)(2,1)}, f32[64,512]{1,0:T(8,128)S(1)}, f32[64,512]{1,0:T(8,128)S(1)}) custom-call(bf16[256,512]{1,0:T(8,128)(2,1)} %flux_hbm.3, bf16[16,256]{1,0:T(8,128)(2,1)S(1)} %bitcast.6, bf16[16,512]{1,0:T(8,128)(2,1)S(1)} %copy-done, bf16[512,512]{1,0:T(8,128)(2,1)} %m_hbm.3, ...), custom_call_target="tpu_custom_call", output_to_operand_aliasing={{0}: (7, {})} | custom-call | flops 67108864 | bytes 786432 | tf_op jit(solution)/shard_map/front/pallas_call | solution.py:336
  10.6 0.1 collective-permute-start.3
  10.7 0.0 collective-permute-done.2
  10.7 2.3 %collective-permute-start.4 = (f32[64,512]{1,0:T(8,128)S(1)}, f32[64,512]{1,0:T(8,128)S(1)}, u32[]{:S(2)}, u32[]{:S(2)}) collective-permute-start(f32[64,512]{1,0:T(8,128)S(1)} %add.33.refs_0_), channel_id=1, source_target_pairs={{0,2},{1,3},{2,0},{3,1},{4,6},{5,7},{6,4},{7,5},{8,10},{9,11},{10,... | collective-permute-start | bytes 393224 | tf_op jit(solution)/shard_map/ppermute | solution.py:180
  13.1 0.0 collective-permute-done.3
  13.1 1.0 %collective-permute-start.5 = (f32[64,512]{1,0:T(8,128)S(1)}, f32[64,512]{1,0:T(8,128)S(1)}, u32[]{:S(2)}, u32[]{:S(2)}) collective-permute-start(f32[64,512]{1,0:T(8,128)S(1)} %add.34.refs_1_), channel_id=1, source_target_pairs={{0,2},{1,3},{2,0},{3,1},{4,6},{5,7},{6,4},{7,5},{8,10},{9,11},{10,... | collective-permute-start | bytes 393224 | tf_op jit(solution)/shard_map/ppermute | solution.py:180
  14.1 3.3 %collective-permute-done.4.refs_2_ = f32[64,512]{1,0:T(8,128)S(1)} collective-permute-done((f32[64,512]{1,0:T(8,128)S(1)}, f32[64,512]{1,0:T(8,128)S(1)}, u32[]{:S(2)}, u32[]{:S(2)}) %collective-permute-start.4) | collective-permute-done | bytes 131104 | tf_op jit(solution)/shard_map/ppermute | solution.py:180
  17.3 2.3 %collective-permute-done.5.refs_3_ = f32[64,512]{1,0:T(8,128)S(1)} collective-permute-done((f32[64,512]{1,0:T(8,128)S(1)}, f32[64,512]{1,0:T(8,128)S(1)}, u32[]{:S(2)}, u32[]{:S(2)}) %collective-permute-start.5) | collective-permute-done | bytes 131104 | tf_op jit(solution)/shard_map/ppermute | solution.py:180
  19.6 0.5 gram.1
  20.2 0.1 collective-permute-start.6
  20.3 1.4 %collective-permute-done.6 = f32[5,64,128]{2,1,0:T(8,128)S(1)} collective-permute-done((f32[5,64,128]{2,1,0:T(8,128)S(1)}, f32[5,64,128]{2,1,0:T(8,128)S(1)}, u32[]{:S(2)}, u32[]{:S(2)}) %collective-permute-start.6) | collective-permute-done | bytes 163872 | tf_op jit(solution)/shard_map/ppermute | solution.py:180
  21.7 1.8 %collective-permute-start.7 = (f32[5,32,128]{2,1,0:T(8,128)S(1)}, f32[5,32,128]{2,1,0:T(8,128)S(1)}, u32[]{:S(2)}, u32[]{:S(2)}) collective-permute-start(f32[5,32,128]{2,1,0:T(8,128)S(1)} %dynamic-slice_add_fusion), channel_id=1, source_target_pairs={{0,4},{4,0},{8,12},{12,8},{16,20},{20,16},{24,28},{28,24},{1,5},{5... | collective-permute-start | bytes 245768 | tf_op jit(solution)/shard_map/ppermute | solution.py:180
  23.5 2.8 %collective-permute-done.7 = f32[5,32,128]{2,1,0:T(8,128)S(1)} collective-permute-done((f32[5,32,128]{2,1,0:T(8,128)S(1)}, f32[5,32,128]{2,1,0:T(8,128)S(1)}, u32[]{:S(2)}, u32[]{:S(2)}) %collective-permute-start.7) | collective-permute-done | bytes 81952 | tf_op jit(solution)/shard_map/ppermute | solution.py:180
  26.3 1.9 %collective-permute-start.8 = (f32[5,32,128]{2,1,0:T(8,128)S(1)}, f32[5,32,128]{2,1,0:T(8,128)S(1)}, u32[]{:S(2)}, u32[]{:S(2)}) collective-permute-start(f32[5,32,128]{2,1,0:T(8,128)S(1)} %add_add_fusion), channel_id=1, source_target_pairs={{0,8},{4,12},{8,0},{12,4},{16,24},{20,28},{24,16},{28,20},{1,9},{5... | collective-permute-start | bytes 245768 | tf_op jit(solution)/shard_map/ppermute | solution.py:180
  28.1 2.6 %collective-permute-done.8 = f32[5,32,128]{2,1,0:T(8,128)S(1)} collective-permute-done((f32[5,32,128]{2,1,0:T(8,128)S(1)}, f32[5,32,128]{2,1,0:T(8,128)S(1)}, u32[]{:S(2)}, u32[]{:S(2)}) %collective-permute-start.8) | collective-permute-done | bytes 81952 | tf_op jit(solution)/shard_map/ppermute | solution.py:180
  30.8 2.9 %collective-permute-start.9 = (f32[5,32,128]{2,1,0:T(8,128)S(1)}, f32[5,32,128]{2,1,0:T(8,128)S(1)}, u32[]{:S(2)}, u32[]{:S(2)}) collective-permute-start(f32[5,32,128]{2,1,0:T(8,128)S(1)} %add.41), channel_id=1, source_target_pairs={{0,16},{4,20},{8,24},{12,28},{16,0},{20,4},{24,8},{28,12},{1,17},{... | collective-permute-start | bytes 245768 | tf_op jit(solution)/shard_map/ppermute | solution.py:180
  33.6 2.5 %collective-permute-done.9 = f32[5,32,128]{2,1,0:T(8,128)S(1)} collective-permute-done((f32[5,32,128]{2,1,0:T(8,128)S(1)}, f32[5,32,128]{2,1,0:T(8,128)S(1)}, u32[]{:S(2)}, u32[]{:S(2)}) %collective-permute-start.9) | collective-permute-done | bytes 81952 | tf_op jit(solution)/shard_map/ppermute | solution.py:180
  36.2 1.8 %collective-permute-start.10 = (f32[5,32,128]{2,1,0:T(8,128)S(1)}, f32[5,32,128]{2,1,0:T(8,128)S(1)}, u32[]{:S(2)}, u32[]{:S(2)}) collective-permute-start(f32[5,32,128]{2,1,0:T(8,128)S(1)} %add.42.refs_0_), channel_id=1, source_target_pairs={{0,4},{4,0},{8,12},{12,8},{16,20},{20,16},{24,28},{28,24},{1,5},{5... | collective-permute-start | bytes 245768 | tf_op jit(solution)/shard_map/ppermute | solution.py:180
  38.0 1.5 %collective-permute-start.11 = (f32[5,32,128]{2,1,0:T(8,128)S(1)}, f32[5,32,128]{2,1,0:T(8,128)S(1)}, u32[]{:S(2)}, u32[]{:S(2)}) collective-permute-start(f32[5,32,128]{2,1,0:T(8,128)S(1)} %add.42.refs_0_), channel_id=1, source_target_pairs={{0,2},{1,3},{2,0},{3,1},{4,6},{5,7},{6,4},{7,5},{8,10},{9,11},{10,... | collective-permute-start | bytes 245768 | tf_op jit(solution)/shard_map/ppermute | solution.py:180
  39.5 1.2 %collective-permute-done.10.refs_1_ = f32[5,32,128]{2,1,0:T(8,128)S(1)} collective-permute-done((f32[5,32,128]{2,1,0:T(8,128)S(1)}, f32[5,32,128]{2,1,0:T(8,128)S(1)}, u32[]{:S(2)}, u32[]{:S(2)}) %collective-permute-start.10) | collective-permute-done | bytes 81952 | tf_op jit(solution)/shard_map/ppermute | solution.py:180
  40.7 1.7 %collective-permute-start.12 = (f32[5,32,128]{2,1,0:T(8,128)S(1)}, f32[5,32,128]{2,1,0:T(8,128)S(1)}, u32[]{:S(2)}, u32[]{:S(2)}) collective-permute-start(f32[5,32,128]{2,1,0:T(8,128)S(1)} %collective-permute-done.10.refs_1_), channel_id=1, source_target_pairs={{0,2},{1,3},{2,0},{3,1},{4,6},{5,7},{6,4},{7,5},{8,10},{9,11},{10,... | collective-permute-start | bytes 245768 | tf_op jit(solution)/shard_map/ppermute | solution.py:180
  42.4 0.0 collective-permute-start.13
  42.4 0.5 collective-permute-start.14
  43.0 0.0 collective-permute-done.11.refs_2_
  43.0 0.0 collective-permute-start.15
  43.0 2.2 %collective-permute-done.12.refs_3_ = f32[5,32,128]{2,1,0:T(8,128)S(1)} collective-permute-done((f32[5,32,128]{2,1,0:T(8,128)S(1)}, f32[5,32,128]{2,1,0:T(8,128)S(1)}, u32[]{:S(2)}, u32[]{:S(2)}) %collective-permute-start.12) | collective-permute-done | bytes 81952 | tf_op jit(solution)/shard_map/ppermute | solution.py:180
  45.1 0.0 collective-permute-start.16
  45.1 0.0 collective-permute-done.13.refs_4_
  45.2 0.0 collective-permute-done.15.refs_6_
  45.2 0.0 collective-permute-done.14.refs_5_
  45.2 1.3 %collective-permute-done.16.refs_7_ = f32[5,32,128]{2,1,0:T(8,128)S(1)} collective-permute-done((f32[5,32,128]{2,1,0:T(8,128)S(1)}, f32[5,32,128]{2,1,0:T(8,128)S(1)}, u32[]{:S(2)}, u32[]{:S(2)}) %collective-permute-start.16) | collective-permute-done | bytes 81952 | tf_op jit(solution)/shard_map/ppermute | solution.py:180
  46.4 13.4 %factor.1 = f32[512,512]{1,0:T(8,128)} custom-call(f32[5,32,128]{2,1,0:T(8,128)S(1)} %add.42.refs_0_, f32[5,32,128]{2,1,0:T(8,128)S(1)} %collective-permute-done.10.refs_1_, f32[5,32,128]{2,1,0:T(8,128)S(1)} %collective-permute-done.11.refs_2_, f32[5,32,128]{2,1,0:T(8,128)S(1)} %collective-permute-done.12.refs_3_, ...), custom_call_target="tpu_custom_call" | custom-call | tf_op jit(solution)/shard_map/factor/pallas_call | solution.py:172
  (6 shorter events, 0.1 us)
Async XLA Ops:
  2.1 4.2 %copy-start = (bf16[16,512]{1,0:T(8,128)(2,1)S(1)}, bf16[16,512]{1,0:T(8,128)(2,1)}, u32[]{:S(2)}) copy-start(bf16[16,512]{1,0:T(8,128)(2,1)} %basis_hbm.3) | copy-start | bytes 49156
  2.1 4.2 %copy-start.1 = (bf16[256,16]{0,1:T(8,128)(2,1)S(1)}, bf16[256,16]{0,1:T(8,128)(2,1)}, u32[]{:S(2)}) copy-start(bf16[256,16]{0,1:T(8,128)(2,1)} %param.11) | copy-start | bytes 24580
  2.1 4.1 %collective-permute-start.1 = (f32[16,256]{1,0:T(8,128)}, f32[16,256]{1,0:T(8,128)S(1)}, u32[]{:S(2)}, u32[]{:S(2)}) collective-permute-start(f32[16,256]{1,0:T(8,128)} %lines.1), channel_id=1, source_target_pairs={{0,3},{1,2},{2,1},{3,0},{4,7},{5,6},{6,5},{7,4},{8,11},{9,10},{10,... | collective-permute-start | bytes 49160 | tf_op jit(solution)/shard_map/ppermute | solution.py:365
  4.5 1.7 %collective-permute-start = (f32[16,256]{1,0:T(8,128)}, f32[16,256]{1,0:T(8,128)S(1)}, u32[]{:S(2)}, u32[]{:S(2)}) collective-permute-start(f32[16,256]{1,0:T(8,128)} %lines.1), channel_id=1, source_target_pairs={{0,1},{1,0},{2,3},{3,2},{4,5},{5,4},{6,7},{7,6},{8,9},{9,8},{10,11... | collective-permute-start | bytes 49160 | tf_op jit(solution)/shard_map/ppermute | solution.py:180
  8.1 2.6 %collective-permute-start.2 = (f32[64,512]{1,0:T(8,128)S(1)}, f32[64,512]{1,0:T(8,128)S(1)}, u32[]{:S(2)}, u32[]{:S(2)}) collective-permute-start(f32[64,512]{1,0:T(8,128)S(1)} %get-tuple-element.13), channel_id=1, source_target_pairs={{0,1},{1,0},{2,3},{3,2},{4,5},{5,4},{6,7},{7,6},{8,9},{9,8},{10,11... | collective-permute-start | bytes 393224 | tf_op jit(solution)/shard_map/ppermute | solution.py:180
  10.6 2.5 %collective-permute-start.3 = (f32[64,512]{1,0:T(8,128)S(1)}, f32[64,512]{1,0:T(8,128)S(1)}, u32[]{:S(2)}, u32[]{:S(2)}) collective-permute-start(f32[64,512]{1,0:T(8,128)S(1)} %get-tuple-element.15), channel_id=1, source_target_pairs={{0,1},{1,0},{2,3},{3,2},{4,5},{5,4},{6,7},{7,6},{8,9},{9,8},{10,11... | collective-permute-start | bytes 393224 | tf_op jit(solution)/shard_map/ppermute | solution.py:180
  10.7 6.6 %collective-permute-start.4 = (f32[64,512]{1,0:T(8,128)S(1)}, f32[64,512]{1,0:T(8,128)S(1)}, u32[]{:S(2)}, u32[]{:S(2)}) collective-permute-start(f32[64,512]{1,0:T(8,128)S(1)} %add.33.refs_0_), channel_id=1, source_target_pairs={{0,2},{1,3},{2,0},{3,1},{4,6},{5,7},{6,4},{7,5},{8,10},{9,11},{10,... | collective-permute-start | bytes 393224 | tf_op jit(solution)/shard_map/ppermute | solution.py:180
  13.1 6.6 %collective-permute-start.5 = (f32[64,512]{1,0:T(8,128)S(1)}, f32[64,512]{1,0:T(8,128)S(1)}, u32[]{:S(2)}, u32[]{:S(2)}) collective-permute-start(f32[64,512]{1,0:T(8,128)S(1)} %add.34.refs_1_), channel_id=1, source_target_pairs={{0,2},{1,3},{2,0},{3,1},{4,6},{5,7},{6,4},{7,5},{8,10},{9,11},{10,... | collective-permute-start | bytes 393224 | tf_op jit(solution)/shard_map/ppermute | solution.py:180
  20.2 1.5 %collective-permute-start.6 = (f32[5,64,128]{2,1,0:T(8,128)S(1)}, f32[5,64,128]{2,1,0:T(8,128)S(1)}, u32[]{:S(2)}, u32[]{:S(2)}) collective-permute-start(f32[5,64,128]{2,1,0:T(8,128)S(1)} %get-tuple-element.17), channel_id=1, source_target_pairs={{0,1},{1,0},{2,3},{3,2},{4,5},{5,4},{6,7},{7,6},{8,9},{9,8},{10,11... | collective-permute-start | bytes 491528 | tf_op jit(solution)/shard_map/ppermute | solution.py:180
  21.7 4.6 %collective-permute-start.7 = (f32[5,32,128]{2,1,0:T(8,128)S(1)}, f32[5,32,128]{2,1,0:T(8,128)S(1)}, u32[]{:S(2)}, u32[]{:S(2)}) collective-permute-start(f32[5,32,128]{2,1,0:T(8,128)S(1)} %dynamic-slice_add_fusion), channel_id=1, source_target_pairs={{0,4},{4,0},{8,12},{12,8},{16,20},{20,16},{24,28},{28,24},{1,5},{5... | collective-permute-start | bytes 245768 | tf_op jit(solution)/shard_map/ppermute | solution.py:180
  26.3 4.5 %collective-permute-start.8 = (f32[5,32,128]{2,1,0:T(8,128)S(1)}, f32[5,32,128]{2,1,0:T(8,128)S(1)}, u32[]{:S(2)}, u32[]{:S(2)}) collective-permute-start(f32[5,32,128]{2,1,0:T(8,128)S(1)} %add_add_fusion), channel_id=1, source_target_pairs={{0,8},{4,12},{8,0},{12,4},{16,24},{20,28},{24,16},{28,20},{1,9},{5... | collective-permute-start | bytes 245768 | tf_op jit(solution)/shard_map/ppermute | solution.py:180
  30.8 5.4 %collective-permute-start.9 = (f32[5,32,128]{2,1,0:T(8,128)S(1)}, f32[5,32,128]{2,1,0:T(8,128)S(1)}, u32[]{:S(2)}, u32[]{:S(2)}) collective-permute-start(f32[5,32,128]{2,1,0:T(8,128)S(1)} %add.41), channel_id=1, source_target_pairs={{0,16},{4,20},{8,24},{12,28},{16,0},{20,4},{24,8},{28,12},{1,17},{... | collective-permute-start | bytes 245768 | tf_op jit(solution)/shard_map/ppermute | solution.py:180
  36.2 4.5 %collective-permute-start.10 = (f32[5,32,128]{2,1,0:T(8,128)S(1)}, f32[5,32,128]{2,1,0:T(8,128)S(1)}, u32[]{:S(2)}, u32[]{:S(2)}) collective-permute-start(f32[5,32,128]{2,1,0:T(8,128)S(1)} %add.42.refs_0_), channel_id=1, source_target_pairs={{0,4},{4,0},{8,12},{12,8},{16,20},{20,16},{24,28},{28,24},{1,5},{5... | collective-permute-start | bytes 245768 | tf_op jit(solution)/shard_map/ppermute | solution.py:180
  38.0 5.0 %collective-permute-start.11 = (f32[5,32,128]{2,1,0:T(8,128)S(1)}, f32[5,32,128]{2,1,0:T(8,128)S(1)}, u32[]{:S(2)}, u32[]{:S(2)}) collective-permute-start(f32[5,32,128]{2,1,0:T(8,128)S(1)} %add.42.refs_0_), channel_id=1, source_target_pairs={{0,2},{1,3},{2,0},{3,1},{4,6},{5,7},{6,4},{7,5},{8,10},{9,11},{10,... | collective-permute-start | bytes 245768 | tf_op jit(solution)/shard_map/ppermute | solution.py:180
  40.7 4.4 %collective-permute-start.12 = (f32[5,32,128]{2,1,0:T(8,128)S(1)}, f32[5,32,128]{2,1,0:T(8,128)S(1)}, u32[]{:S(2)}, u32[]{:S(2)}) collective-permute-start(f32[5,32,128]{2,1,0:T(8,128)S(1)} %collective-permute-done.10.refs_1_), channel_id=1, source_target_pairs={{0,2},{1,3},{2,0},{3,1},{4,6},{5,7},{6,4},{7,5},{8,10},{9,11},{10,... | collective-permute-start | bytes 245768 | tf_op jit(solution)/shard_map/ppermute | solution.py:180
  42.4 2.7 %collective-permute-start.13 = (f32[5,32,128]{2,1,0:T(8,128)S(1)}, f32[5,32,128]{2,1,0:T(8,128)S(1)}, u32[]{:S(2)}, u32[]{:S(2)}) collective-permute-start(f32[5,32,128]{2,1,0:T(8,128)S(1)} %add.42.refs_0_), channel_id=1, source_target_pairs={{0,1},{1,0},{2,3},{3,2},{4,5},{5,4},{6,7},{7,6},{8,9},{9,8},{10,11... | collective-permute-start | bytes 245768 | tf_op jit(solution)/shard_map/ppermute | solution.py:180
  42.4 2.7 %collective-permute-start.14 = (f32[5,32,128]{2,1,0:T(8,128)S(1)}, f32[5,32,128]{2,1,0:T(8,128)S(1)}, u32[]{:S(2)}, u32[]{:S(2)}) collective-permute-start(f32[5,32,128]{2,1,0:T(8,128)S(1)} %collective-permute-done.10.refs_1_), channel_id=1, source_target_pairs={{0,1},{1,0},{2,3},{3,2},{4,5},{5,4},{6,7},{7,6},{8,9},{9,8},{10,11... | collective-permute-start | bytes 245768 | tf_op jit(solution)/shard_map/ppermute | solution.py:180
  43.0 2.2 %collective-permute-start.15 = (f32[5,32,128]{2,1,0:T(8,128)S(1)}, f32[5,32,128]{2,1,0:T(8,128)S(1)}, u32[]{:S(2)}, u32[]{:S(2)}) collective-permute-start(f32[5,32,128]{2,1,0:T(8,128)S(1)} %collective-permute-done.11.refs_2_), channel_id=1, source_target_pairs={{0,1},{1,0},{2,3},{3,2},{4,5},{5,4},{6,7},{7,6},{8,9},{9,8},{10,11... | collective-permute-start | bytes 245768 | tf_op jit(solution)/shard_map/ppermute | solution.py:180
  45.1 1.3 %collective-permute-start.16 = (f32[5,32,128]{2,1,0:T(8,128)S(1)}, f32[5,32,128]{2,1,0:T(8,128)S(1)}, u32[]{:S(2)}, u32[]{:S(2)}) collective-permute-start(f32[5,32,128]{2,1,0:T(8,128)S(1)} %collective-permute-done.12.refs_3_), channel_id=1, source_target_pairs={{0,1},{1,0},{2,3},{3,2},{4,5},{5,4},{6,7},{7,6},{8,9},{9,8},{10,11... | collective-permute-start | bytes 245768 | tf_op jit(solution)/shard_map/ppermute | solution.py:180
